TPU v7x, 512 devices: a whole 4x8x8 slice. The times are simulated.
512 devices in a mesh: gx: 4 (over y_hi), gy: 8 (over z), gz: 16 (over y_lo, x, core).
Axes of the slice: x: 4, y: 8 (y_hi: 4, y_lo: 2; y = y_hi * 2 + y_lo), z: 8, core: 2. Of those that a mesh axis runs over, the one named last changes fastest.
Arguments:
- dual_blocks: bfloat16 [4, 8, 16, 1024, 1024], P('gx', 'gy', 'gz'), may hold values from -1 to 3, as said below
- load_terms: bfloat16 [4, 8, 16, 1024, 128], P('gx', 'gy', 'gz'), may hold values from -6 to 6
- row_order: int32 [4, 8, 16, 1024], P('gx', 'gy', 'gz'), may hold values from 0 to 1023, each once within a row
- mode_rows: bfloat16 [4, 8, 16, 1024, 6], P('gx', 'gy', 'gz'), may hold values from -0.1875 to 0.1875
- mode_count: int32 [4, 8, 16], P('gx', 'gy', 'gz'), may hold values from 0 to 6, as said below
- coarse_inverse: float32 [4, 8, 96, 96], P('gx', 'gy'), may hold values from -1 to 3, as said below
Outputs:
- multipliers: float32 [4, 8, 16, 1024, 128], P('gx', 'gy', 'gz')
- residual: float32 [4, 8, 16, 1024, 128], P('gx', 'gy', 'gz')
Inputs may be any that keep to these rules, and one draw needn't show every extreme that they name: `mode_count`: subdomains away from the outer boundary have 6 rigid-body modes; subdomains on the outer boundary have 0 to 6; some subdomain has exactly 6 and some boundary subdomain has none. Each subdomain's row of row_order is a permutation of its 1024 rows. `dual_blocks`: each subdomain's block is symmetric positive definite. `coarse_inverse`: each line's matrix is symmetric positive definite.
All inputs are finite; a program needn't handle non-finite values.
Results may differ from a plain program's by a relative error of at most 0.0082.
Values sent between devices are 32-bit elements; how exact they have to be, the bound alone decides.
No kernel may reach another device: no remote copies, remote signals or barrier semaphores. Data moves between devices by JAX's collectives and lax.ppermute only.
A program may use at most 64 MiB of HBM per device.

v0:
```python
import jax
import jax.numpy as jnp
from jax import lax
from jax.sharding import PartitionSpec as P

FACE = 128
EDGE = 16
CORNER = 8
NMODE = 6
ITERS = 3


EIG_LOW = 0.5
EIG_HIGH = 6.0


def from_behind(block, axis, distance):
    devices = range(lax.axis_size(axis))
    route = [(i - distance, i) for i in devices if i - distance in devices]
    return lax.ppermute(block, axis, route)


def slot_table():
    slot_list = []
    begin_row = 0
    for weight_class, width_rows in ((1, FACE), (2, EDGE), (3, CORNER)):
        for sign_one in (-1, 0, 1):
            for sign_two in (-1, 0, 1):
                for sign_three in (-1, 0, 1):
                    if abs(sign_one) + abs(sign_two) + abs(sign_three) == weight_class:
                        slot_list.append(((sign_one, sign_two, sign_three), begin_row, width_rows))
                        begin_row += width_rows
    return slot_list


def partner(packed):
    slot_list = slot_table()
    travelling = []
    for offset, begin_row, width_rows in slot_list:
        travelling.append([offset, list(offset), packed[begin_row : begin_row + width_rows]])
    for axis_pos in range(3):
        for heading in (1, -1):
            chosen = [record for record in travelling if record[1][axis_pos] == heading]
            bundle = jnp.concatenate([record[2] for record in chosen], axis=0)
            if axis_pos == 0:
                arrived = from_behind(bundle, "gx", heading)
            elif axis_pos == 1:
                arrived = from_behind(bundle, "gy", heading)
            else:
                arrived = from_behind(bundle, "gz", heading)
            cursor = 0
            for record in chosen:
                row_count = record[2].shape[0]
                record[2] = arrived[cursor : cursor + row_count]
                record[1][axis_pos] = 0
                cursor += row_count
    by_anchor = {}
    for record in travelling:
        by_anchor[record[0]] = record[2]
    return jnp.concatenate(
        [
            by_anchor[-offset[0], -offset[1], -offset[2]]
            for offset, begin_row, width_rows in slot_list
        ],
        axis=0,
    )


def coarse_amplitude(residual, mode_cols, count_value, inverse):
    highest = lax.Precision.HIGHEST
    project = jnp.dot(mode_cols.T, residual, precision=highest, preferred_element_type=jnp.float32)
    everyone, counts = (
        lax.all_gather(project, "gz", axis=0, tiled=True),
        lax.all_gather(count_value, "gz", axis=0, tiled=True),
    )
    coarse_size = inverse.shape[0]
    line_length = lax.axis_size("gz")
    offsets = jnp.cumsum(counts) - counts
    owner_offset = jnp.repeat(offsets, NMODE)
    owner_count = jnp.repeat(counts, NMODE)
    within = jnp.tile(jnp.arange(NMODE, dtype=jnp.float32), line_length)
    compact_pos = jnp.arange(coarse_size, dtype=jnp.float32)[:, None]
    hits = compact_pos == (owner_offset + within)[None, :]
    valid = (within < owner_count)[None, :]
    select = jnp.where(hits & valid, 1.0, 0.0).astype(jnp.float32)
    compact = jnp.dot(select, everyone, precision=highest, preferred_element_type=jnp.float32)
    select_mine = lax.dynamic_slice_in_dim(select, lax.axis_index("gz") * NMODE, NMODE, 1)
    rows_mine = jnp.dot(
        select_mine.T, inverse, precision=highest, preferred_element_type=jnp.float32
    )
    return jnp.dot(rows_mine, compact, precision=highest, preferred_element_type=jnp.float32)


def precondition(residual, mode_cols, count_value, inverse):
    highest = lax.Precision.HIGHEST
    amplitude = coarse_amplitude(residual, mode_cols, count_value, inverse)
    spread = jnp.dot(mode_cols, amplitude, precision=highest, preferred_element_type=jnp.float32)
    remote_part = partner(spread)
    return residual - spread - remote_part


def apply_operator(dual_packed, direction):
    rounded = direction.astype(jnp.bfloat16)
    local_image = jnp.dot(dual_packed, rounded, preferred_element_type=jnp.float32)
    return local_image + partner(local_image)


def chebyshev(load_rows, dual_packed, mode_cols, count_value, inverse):
    center_value = 0.5 * (EIG_HIGH + EIG_LOW)
    half_width = 0.5 * (EIG_HIGH - EIG_LOW)
    residual = load_rows + partner(load_rows)
    direction = precondition(residual, mode_cols, count_value, inverse) / center_value
    multipliers = direction
    rho_prev = half_width / center_value
    residual = residual - apply_operator(dual_packed, direction)
    for iteration in range(1, ITERS):
        corrected = precondition(residual, mode_cols, count_value, inverse)
        rho_now = 1.0 / (2.0 * center_value / half_width - rho_prev)
        direction = rho_now * rho_prev * direction + 2.0 * rho_now / half_width * corrected
        multipliers = multipliers + direction
        residual = residual - apply_operator(dual_packed, direction)
        rho_prev = rho_now
    return (multipliers, residual)


def local(dual_blocks, load_terms, row_order, mode_rows, mode_count, coarse_inverse):
    packing = row_order[0, 0, 0]
    dual_packed = jnp.take(jnp.take(dual_blocks[0, 0, 0], packing, axis=0), packing, axis=1)
    load_rows = jnp.take(load_terms[0, 0, 0], packing, axis=0).astype(jnp.float32)
    mode_cols = jnp.take(mode_rows[0, 0, 0], packing, axis=0).astype(jnp.float32)
    count_value = mode_count.reshape(1).astype(jnp.float32)
    inverse = coarse_inverse[0, 0]
    multipliers, residual = chebyshev(load_rows, dual_packed, mode_cols, count_value, inverse)
    unpacking = jnp.argsort(packing)
    return (
        jnp.take(multipliers, unpacking, axis=0)[None, None, None],
        jnp.take(residual, unpacking, axis=0)[None, None, None],
    )


def solution(mesh):
    in_specs = (
        P("gx", "gy", "gz", None, None),
        P("gx", "gy", "gz", None, None),
        P("gx", "gy", "gz", None),
        P("gx", "gy", "gz", None, None),
        P("gx", "gy", "gz"),
        P("gx", "gy", None, None),
    )
    out_specs = (P("gx", "gy", "gz", None, None), P("gx", "gy", "gz", None, None))
    return jax.shard_map(local, mesh=mesh, in_specs=in_specs, out_specs=out_specs, check_vma=False)
```

profile of v0, /device:TPU:296, one launch (start us, length us, event | category | flops | bytes accessed | tf_op | source)
XLA Modules:
  0.0 412.8 jit_solution(14644395754896379977)
XLA Ops:
  2.2 5.1 %sort.17 = (s32[1024]{0:T(1024)}, s32[1024]{0:T(1024)S(1)}) sort(s32[1024]{0:T(1024)} %bitcast.42, s32[1024]{0:T(1024)S(1)} %iota.16), dimensions={0}, to_apply=%region_1.2 | sort | flops 10240 | bytes 16384 | tf_op jit(solution)/shard_map/jit(argsort)/sort | solution.py:134
  18.7 28.9 %all-reduce = f32[16]{0:T(128)S(1)} all-reduce(f32[16]{0:T(128)S(1)} %bitcast_dynamic-update-slice_fusion), channel_id=2, replica_groups=mesh['gx'=4,'gy'=8,'gz'=16] {'gz'}, use_global_device_ids=true, to_apply=%add | all-reduce | flops 16 | bytes 128 | tf_op jit(solution)/shard_map/all_gather | solution.py:74
  54.3 4.5 %collective-permute-start = (f32[224,128]{1,0:T(8,128)S(1)}, f32[224,128]{1,0:T(8,128)S(1)}, u32[]{:S(2)}, u32[]{:S(2)}) collective-permute-start(f32[224,128]{1,0:T(8,128)S(1)} %pad_maximum_fusion), channel_id=1, source_target_pairs={{0,128},{128,256},{256,384},{1,129},{129,257},{257,385},{2,130},{1... | collective-permute-start | bytes 344072 | tf_op jit(solution)/shard_map/ppermute | solution.py:20
  83.4 6.5 %collective-permute-done.4 = f32[224,128]{1,0:T(8,128)S(1)} collective-permute-done((f32[224,128]{1,0:T(8,128)}, f32[224,128]{1,0:T(8,128)S(1)}, u32[]{:S(2)}, u32[]{:S(2)}) %collective-permute-start.4) | collective-permute-done | bytes 114720 | tf_op jit(solution)/shard_map/ppermute | solution.py:20
  91.6 16.1 %all-gather.1 = f32[16,6,128]{2,1,0:T(8,128)S(1)} all-gather(f32[1,6,128]{2,1,0:T(8,128)S(1)} %convolution_bitcast_fusion.2), channel_id=1, replica_groups=mesh['gx'=4,'gy'=8,'gz'=16] {'gz'}, dimensions={0}, use_global_device_ids=true | all-gather | bytes 52224 | tf_op jit(solution)/shard_map/all_gather | solution.py:73
  114.5 5.4 %gather_fusion.2 = bf16[1024,1024]{1,0:T(8,128)(2,1)} fusion(bf16[1024,1024]{1,0:T(8,128)(2,1)S(1)} %bitcast.38, s32[1024]{0:T(1024)S(1)} %get-tuple-element.255), kind=kCustom, calls=%fused_computation.4 | custom fusion | bytes 4198400 | tf_op jit(solution)/shard_map/jit(_take)/gather | solution.py:128
  133.9 7.9 %gather_fusion.3 = bf16[1024,1024]{1,0:T(8,128)(2,1)} fusion(bf16[1024,1024]{0,1:T(8,128)(2,1)} %copy.16, s32[1024]{0:T(1024)S(1)} %get-tuple-element.255), kind=kCustom, calls=%fused_computation.5 | custom fusion | bytes 4198400 | tf_op jit(solution)/shard_map/jit(_take)/gather | solution.py:128
  162.6 6.5 %collective-permute-done.10 = f32[224,128]{1,0:T(8,128)S(1)} collective-permute-done((f32[224,128]{1,0:T(8,128)}, f32[224,128]{1,0:T(8,128)S(1)}, u32[]{:S(2)}, u32[]{:S(2)}) %collective-permute-start.10) | collective-permute-done | bytes 114720 | tf_op jit(solution)/shard_map/ppermute | solution.py:20
  173.3 5.8 %collective-permute-start.13 = (f32[224,128]{1,0:T(8,128)S(1)}, f32[224,128]{1,0:T(8,128)S(1)}, u32[]{:S(2)}, u32[]{:S(2)}) collective-permute-start(f32[224,128]{1,0:T(8,128)S(1)} %pad_maximum_fusion.5), channel_id=1, source_target_pairs={{128,0},{256,128},{384,256},{129,1},{257,129},{385,257},{130,2},{2... | collective-permute-start | bytes 344072 | tf_op jit(solution)/shard_map/ppermute | solution.py:20
  183.4 7.3 %collective-permute-done.12 = f32[224,128]{1,0:T(8,128)S(1)} collective-permute-done((f32[224,128]{1,0:T(8,128)S(1)}, f32[224,128]{1,0:T(8,128)S(1)}, u32[]{:S(2)}, u32[]{:S(2)}) %collective-permute-start.12) | collective-permute-done | bytes 114720 | tf_op jit(solution)/shard_map/ppermute | solution.py:20
  204.9 5.8 %collective-permute-done.16 = f32[224,128]{1,0:T(8,128)S(1)} collective-permute-done((f32[224,128]{1,0:T(8,128)S(1)}, f32[224,128]{1,0:T(8,128)S(1)}, u32[]{:S(2)}, u32[]{:S(2)}) %collective-permute-start.16) | collective-permute-done | bytes 114720 | tf_op jit(solution)/shard_map/ppermute | solution.py:20
  211.7 16.3 %all-gather.2 = f32[16,6,128]{2,1,0:T(8,128)S(1)} all-gather(f32[1,6,128]{2,1,0:T(8,128)S(1)} %convolution_bitcast_fusion.1), channel_id=1, replica_groups=mesh['gx'=4,'gy'=8,'gz'=16] {'gz'}, dimensions={0}, use_global_device_ids=true | all-gather | bytes 52224 | tf_op jit(solution)/shard_map/all_gather | solution.py:73
  228.9 4.8 %collective-permute-start.19 = (f32[224,128]{1,0:T(8,128)S(1)}, f32[224,128]{1,0:T(8,128)S(1)}, u32[]{:S(2)}, u32[]{:S(2)}) collective-permute-start(f32[224,128]{1,0:T(8,128)S(1)} %pad_maximum_fusion.7), channel_id=1, source_target_pairs={{128,0},{256,128},{384,256},{129,1},{257,129},{385,257},{130,2},{2... | collective-permute-start | bytes 344072 | tf_op jit(solution)/shard_map/ppermute | solution.py:20
  239.2 7.5 %collective-permute-done.18 = f32[224,128]{1,0:T(8,128)S(1)} collective-permute-done((f32[224,128]{1,0:T(8,128)S(1)}, f32[224,128]{1,0:T(8,128)S(1)}, u32[]{:S(2)}, u32[]{:S(2)}) %collective-permute-start.18) | collective-permute-done | bytes 114720 | tf_op jit(solution)/shard_map/ppermute | solution.py:20
  261.6 6.3 %collective-permute-done.22 = f32[224,128]{1,0:T(8,128)S(1)} collective-permute-done((f32[224,128]{1,0:T(8,128)S(1)}, f32[224,128]{1,0:T(8,128)S(1)}, u32[]{:S(2)}, u32[]{:S(2)}) %collective-permute-start.22) | collective-permute-done | bytes 114720 | tf_op jit(solution)/shard_map/ppermute | solution.py:20
  279.1 6.7 %collective-permute-done.24 = f32[224,128]{1,0:T(8,128)S(1)} collective-permute-done((f32[224,128]{1,0:T(8,128)S(1)}, f32[224,128]{1,0:T(8,128)S(1)}, u32[]{:S(2)}, u32[]{:S(2)}) %collective-permute-start.24) | collective-permute-done | bytes 114720 | tf_op jit(solution)/shard_map/ppermute | solution.py:20
  300.0 5.8 %collective-permute-done.28 = f32[224,128]{1,0:T(8,128)S(1)} collective-permute-done((f32[224,128]{1,0:T(8,128)S(1)}, f32[224,128]{1,0:T(8,128)S(1)}, u32[]{:S(2)}, u32[]{:S(2)}) %collective-permute-start.28) | collective-permute-done | bytes 114720 | tf_op jit(solution)/shard_map/ppermute | solution.py:20
  306.7 17.8 %all-gather.3 = f32[16,6,128]{2,1,0:T(8,128)S(1)} all-gather(f32[1,6,128]{2,1,0:T(8,128)S(1)} %convolution_bitcast_fusion), channel_id=1, replica_groups=mesh['gx'=4,'gy'=8,'gz'=16] {'gz'}, dimensions={0}, use_global_device_ids=true | all-gather | bytes 52224 | tf_op jit(solution)/shard_map/all_gather | solution.py:73
  328.5 5.2 %collective-permute-done.31 = f32[224,128]{1,0:T(8,128)S(1)} collective-permute-done((f32[224,128]{1,0:T(8,128)S(1)}, f32[224,128]{1,0:T(8,128)S(1)}, u32[]{:S(2)}, u32[]{:S(2)}) %collective-permute-start.31) | collective-permute-done | bytes 114720 | tf_op jit(solution)/shard_map/ppermute | solution.py:20
  335.6 6.9 %collective-permute-done.30 = f32[224,128]{1,0:T(8,128)S(1)} collective-permute-done((f32[224,128]{1,0:T(8,128)S(1)}, f32[224,128]{1,0:T(8,128)S(1)}, u32[]{:S(2)}, u32[]{:S(2)}) %collective-permute-start.30) | collective-permute-done | bytes 114720 | tf_op jit(solution)/shard_map/ppermute | solution.py:20
  357.6 6.3 %collective-permute-done.34 = f32[224,128]{1,0:T(8,128)S(1)} collective-permute-done((f32[224,128]{1,0:T(8,128)S(1)}, f32[224,128]{1,0:T(8,128)S(1)}, u32[]{:S(2)}, u32[]{:S(2)}) %collective-permute-start.34) | collective-permute-done | bytes 114720 | tf_op jit(solution)/shard_map/ppermute | solution.py:20
  368.6 4.5 %collective-permute-done.37 = f32[224,128]{1,0:T(8,128)S(1)} collective-permute-done((f32[224,128]{1,0:T(8,128)S(1)}, f32[224,128]{1,0:T(8,128)S(1)}, u32[]{:S(2)}, u32[]{:S(2)}) %collective-permute-start.37) | collective-permute-done | bytes 114720 | tf_op jit(solution)/shard_map/ppermute | solution.py:20
  375.1 6.9 %collective-permute-done.36 = f32[224,128]{1,0:T(8,128)S(1)} collective-permute-done((f32[224,128]{1,0:T(8,128)S(1)}, f32[224,128]{1,0:T(8,128)S(1)}, u32[]{:S(2)}, u32[]{:S(2)}) %collective-permute-start.36) | collective-permute-done | bytes 114720 | tf_op jit(solution)/shard_map/ppermute | solution.py:20
  396.2 5.8 %collective-permute-done.40 = f32[224,128]{1,0:T(8,128)S(1)} collective-permute-done((f32[224,128]{1,0:T(8,128)S(1)}, f32[224,128]{1,0:T(8,128)S(1)}, u32[]{:S(2)}, u32[]{:S(2)}) %collective-permute-start.40) | collective-permute-done | bytes 114720 | tf_op jit(solution)/shard_map/ppermute | solution.py:20
  (460 shorter events, 208.7 us)
Async XLA Ops:
  12.8 38.9 %collective-permute-start.1 = (f32[224,128]{1,0:T(8,128)S(1)}, f32[224,128]{1,0:T(8,128)S(1)}, u32[]{:S(2)}, u32[]{:S(2)}) collective-permute-start(f32[224,128]{1,0:T(8,128)S(1)} %pad_maximum_fusion.1), channel_id=1, source_target_pairs={{128,0},{256,128},{384,256},{129,1},{257,129},{385,257},{130,2},{2... | collective-permute-start | bytes 344072 | tf_op jit(solution)/shard_map/ppermute | solution.py:20
  54.3 8.9 %collective-permute-start = (f32[224,128]{1,0:T(8,128)S(1)}, f32[224,128]{1,0:T(8,128)S(1)}, u32[]{:S(2)}, u32[]{:S(2)}) collective-permute-start(f32[224,128]{1,0:T(8,128)S(1)} %pad_maximum_fusion), channel_id=1, source_target_pairs={{0,128},{128,256},{256,384},{1,129},{129,257},{257,385},{2,130},{1... | collective-permute-start | bytes 344072 | tf_op jit(solution)/shard_map/ppermute | solution.py:20
  78.7 11.2 %collective-permute-start.5 = (f32[224,128]{1,0:T(8,128)}, f32[224,128]{1,0:T(8,128)S(1)}, u32[]{:S(2)}, u32[]{:S(2)}) collective-permute-start(f32[224,128]{1,0:T(8,128)} %get-tuple-element.228), channel_id=1, source_target_pairs={{1,0},{2,1},{3,2},{4,3},{5,4},{6,5},{7,6},{8,7},{9,8},{10,9},{11,1... | collective-permute-start | bytes 344072 | tf_op jit(solution)/shard_map/ppermute | solution.py:20
  81.4 8.4 %collective-permute-start.4 = (f32[224,128]{1,0:T(8,128)}, f32[224,128]{1,0:T(8,128)S(1)}, u32[]{:S(2)}, u32[]{:S(2)}) collective-permute-start(f32[224,128]{1,0:T(8,128)} %get-tuple-element.229), channel_id=1, source_target_pairs={{0,1},{1,2},{2,3},{3,4},{4,5},{5,6},{6,7},{7,8},{8,9},{9,10},{10,1... | collective-permute-start | bytes 344072 | tf_op jit(solution)/shard_map/ppermute | solution.py:20
  112.6 8.3 %collective-permute-start.7 = (f32[224,128]{1,0:T(8,128)S(1)}, f32[224,128]{1,0:T(8,128)S(1)}, u32[]{:S(2)}, u32[]{:S(2)}) collective-permute-start(f32[224,128]{1,0:T(8,128)S(1)} %pad_maximum_fusion.3), channel_id=1, source_target_pairs={{128,0},{256,128},{384,256},{129,1},{257,129},{385,257},{130,2},{2... | collective-permute-start | bytes 344072 | tf_op jit(solution)/shard_map/ppermute | solution.py:20
  122.9 18.8 %collective-permute-start.6 = (f32[224,128]{1,0:T(8,128)S(1)}, f32[224,128]{1,0:T(8,128)S(1)}, u32[]{:S(2)}, u32[]{:S(2)}) collective-permute-start(f32[224,128]{1,0:T(8,128)S(1)} %pad_maximum_fusion.2), channel_id=1, source_target_pairs={{0,128},{128,256},{256,384},{1,129},{129,257},{257,385},{2,130},{1... | collective-permute-start | bytes 344072 | tf_op jit(solution)/shard_map/ppermute | solution.py:20
  158.0 11.1 %collective-permute-start.11 = (f32[224,128]{1,0:T(8,128)}, f32[224,128]{1,0:T(8,128)S(1)}, u32[]{:S(2)}, u32[]{:S(2)}) collective-permute-start(f32[224,128]{1,0:T(8,128)} %get-tuple-element.204), channel_id=1, source_target_pairs={{1,0},{2,1},{3,2},{4,3},{5,4},{6,5},{7,6},{8,7},{9,8},{10,9},{11,1... | collective-permute-start | bytes 344072 | tf_op jit(solution)/shard_map/ppermute | solution.py:20
  160.7 8.4 %collective-permute-start.10 = (f32[224,128]{1,0:T(8,128)}, f32[224,128]{1,0:T(8,128)S(1)}, u32[]{:S(2)}, u32[]{:S(2)}) collective-permute-start(f32[224,128]{1,0:T(8,128)} %get-tuple-element.205), channel_id=1, source_target_pairs={{0,1},{1,2},{2,3},{3,4},{4,5},{5,6},{6,7},{7,8},{8,9},{9,10},{10,1... | collective-permute-start | bytes 344072 | tf_op jit(solution)/shard_map/ppermute | solution.py:20
  181.5 9.2 %collective-permute-start.12 = (f32[224,128]{1,0:T(8,128)S(1)}, f32[224,128]{1,0:T(8,128)S(1)}, u32[]{:S(2)}, u32[]{:S(2)}) collective-permute-start(f32[224,128]{1,0:T(8,128)S(1)} %pad_maximum_fusion.4), channel_id=1, source_target_pairs={{0,128},{128,256},{256,384},{1,129},{129,257},{257,385},{2,130},{1... | collective-permute-start | bytes 344072 | tf_op jit(solution)/shard_map/ppermute | solution.py:20
  200.6 10.2 %collective-permute-start.17 = (f32[224,128]{1,0:T(8,128)S(1)}, f32[224,128]{1,0:T(8,128)S(1)}, u32[]{:S(2)}, u32[]{:S(2)}) collective-permute-start(f32[224,128]{1,0:T(8,128)S(1)} %get-tuple-element.180), channel_id=1, source_target_pairs={{1,0},{2,1},{3,2},{4,3},{5,4},{6,5},{7,6},{8,7},{9,8},{10,9},{11,1... | collective-permute-start | bytes 344072 | tf_op jit(solution)/shard_map/ppermute | solution.py:20
  202.5 8.2 %collective-permute-start.16 = (f32[224,128]{1,0:T(8,128)S(1)}, f32[224,128]{1,0:T(8,128)S(1)}, u32[]{:S(2)}, u32[]{:S(2)}) collective-permute-start(f32[224,128]{1,0:T(8,128)S(1)} %get-tuple-element.181), channel_id=1, source_target_pairs={{0,1},{1,2},{2,3},{3,4},{4,5},{5,6},{6,7},{7,8},{8,9},{9,10},{10,1... | collective-permute-start | bytes 344072 | tf_op jit(solution)/shard_map/ppermute | solution.py:20
  237.1 9.6 %collective-permute-start.18 = (f32[224,128]{1,0:T(8,128)S(1)}, f32[224,128]{1,0:T(8,128)S(1)}, u32[]{:S(2)}, u32[]{:S(2)}) collective-permute-start(f32[224,128]{1,0:T(8,128)S(1)} %pad_maximum_fusion.6), channel_id=1, source_target_pairs={{0,128},{128,256},{256,384},{1,129},{129,257},{257,385},{2,130},{1... | collective-permute-start | bytes 344072 | tf_op jit(solution)/shard_map/ppermute | solution.py:20
  256.6 11.3 %collective-permute-start.23 = (f32[224,128]{1,0:T(8,128)S(1)}, f32[224,128]{1,0:T(8,128)S(1)}, u32[]{:S(2)}, u32[]{:S(2)}) collective-permute-start(f32[224,128]{1,0:T(8,128)S(1)} %get-tuple-element.156), channel_id=1, source_target_pairs={{1,0},{2,1},{3,2},{4,3},{5,4},{6,5},{7,6},{8,7},{9,8},{10,9},{11,1... | collective-permute-start | bytes 344072 | tf_op jit(solution)/shard_map/ppermute | solution.py:20
  259.6 8.2 %collective-permute-start.22 = (f32[224,128]{1,0:T(8,128)S(1)}, f32[224,128]{1,0:T(8,128)S(1)}, u32[]{:S(2)}, u32[]{:S(2)}) collective-permute-start(f32[224,128]{1,0:T(8,128)S(1)} %get-tuple-element.157), channel_id=1, source_target_pairs={{0,1},{1,2},{2,3},{3,4},{4,5},{5,6},{6,7},{7,8},{8,9},{9,10},{10,1... | collective-permute-start | bytes 344072 | tf_op jit(solution)/shard_map/ppermute | solution.py:20
  277.0 8.8 %collective-permute-start.24 = (f32[224,128]{1,0:T(8,128)S(1)}, f32[224,128]{1,0:T(8,128)S(1)}, u32[]{:S(2)}, u32[]{:S(2)}) collective-permute-start(f32[224,128]{1,0:T(8,128)S(1)} %pad_maximum_fusion.8), channel_id=1, source_target_pairs={{0,128},{128,256},{256,384},{1,129},{129,257},{257,385},{2,130},{1... | collective-permute-start | bytes 344072 | tf_op jit(solution)/shard_map/ppermute | solution.py:20
  295.7 10.2 %collective-permute-start.29 = (f32[224,128]{1,0:T(8,128)S(1)}, f32[224,128]{1,0:T(8,128)S(1)}, u32[]{:S(2)}, u32[]{:S(2)}) collective-permute-start(f32[224,128]{1,0:T(8,128)S(1)} %get-tuple-element.132), channel_id=1, source_target_pairs={{1,0},{2,1},{3,2},{4,3},{5,4},{6,5},{7,6},{8,7},{9,8},{10,9},{11,1... | collective-permute-start | bytes 344072 | tf_op jit(solution)/shard_map/ppermute | solution.py:20
  297.6 8.2 %collective-permute-start.28 = (f32[224,128]{1,0:T(8,128)S(1)}, f32[224,128]{1,0:T(8,128)S(1)}, u32[]{:S(2)}, u32[]{:S(2)}) collective-permute-start(f32[224,128]{1,0:T(8,128)S(1)} %get-tuple-element.133), channel_id=1, source_target_pairs={{0,1},{1,2},{2,3},{3,4},{4,5},{5,6},{6,7},{7,8},{8,9},{9,10},{10,1... | collective-permute-start | bytes 344072 | tf_op jit(solution)/shard_map/ppermute | solution.py:20
  325.4 8.3 %collective-permute-start.31 = (f32[224,128]{1,0:T(8,128)S(1)}, f32[224,128]{1,0:T(8,128)S(1)}, u32[]{:S(2)}, u32[]{:S(2)}) collective-permute-start(f32[224,128]{1,0:T(8,128)S(1)} %pad_maximum_fusion.11), channel_id=1, source_target_pairs={{128,0},{256,128},{384,256},{129,1},{257,129},{385,257},{130,2},{2... | collective-permute-start | bytes 344072 | tf_op jit(solution)/shard_map/ppermute | solution.py:20
  333.7 8.8 %collective-permute-start.30 = (f32[224,128]{1,0:T(8,128)S(1)}, f32[224,128]{1,0:T(8,128)S(1)}, u32[]{:S(2)}, u32[]{:S(2)}) collective-permute-start(f32[224,128]{1,0:T(8,128)S(1)} %pad_maximum_fusion.10), channel_id=1, source_target_pairs={{0,128},{128,256},{256,384},{1,129},{129,257},{257,385},{2,130},{1... | collective-permute-start | bytes 344072 | tf_op jit(solution)/shard_map/ppermute | solution.py:20
  352.4 11.5 %collective-permute-start.35 = (f32[224,128]{1,0:T(8,128)S(1)}, f32[224,128]{1,0:T(8,128)S(1)}, u32[]{:S(2)}, u32[]{:S(2)}) collective-permute-start(f32[224,128]{1,0:T(8,128)S(1)} %get-tuple-element.108), channel_id=1, source_target_pairs={{1,0},{2,1},{3,2},{4,3},{5,4},{6,5},{7,6},{8,7},{9,8},{10,9},{11,1... | collective-permute-start | bytes 344072 | tf_op jit(solution)/shard_map/ppermute | solution.py:20
  355.7 8.2 %collective-permute-start.34 = (f32[224,128]{1,0:T(8,128)S(1)}, f32[224,128]{1,0:T(8,128)S(1)}, u32[]{:S(2)}, u32[]{:S(2)}) collective-permute-start(f32[224,128]{1,0:T(8,128)S(1)} %get-tuple-element.109), channel_id=1, source_target_pairs={{0,1},{1,2},{2,3},{3,4},{4,5},{5,6},{6,7},{7,8},{8,9},{9,10},{10,1... | collective-permute-start | bytes 344072 | tf_op jit(solution)/shard_map/ppermute | solution.py:20
  373.2 8.8 %collective-permute-start.36 = (f32[224,128]{1,0:T(8,128)S(1)}, f32[224,128]{1,0:T(8,128)S(1)}, u32[]{:S(2)}, u32[]{:S(2)}) collective-permute-start(f32[224,128]{1,0:T(8,128)S(1)} %pad_maximum_fusion.12), channel_id=1, source_target_pairs={{0,128},{128,256},{256,384},{1,129},{129,257},{257,385},{2,130},{1... | collective-permute-start | bytes 344072 | tf_op jit(solution)/shard_map/ppermute | solution.py:20
  391.8 10.2 %collective-permute-start.41 = (f32[224,128]{1,0:T(8,128)S(1)}, f32[224,128]{1,0:T(8,128)S(1)}, u32[]{:S(2)}, u32[]{:S(2)}) collective-permute-start(f32[224,128]{1,0:T(8,128)S(1)} %get-tuple-element.84), channel_id=1, source_target_pairs={{1,0},{2,1},{3,2},{4,3},{5,4},{6,5},{7,6},{8,7},{9,8},{10,9},{11,1... | collective-permute-start | bytes 344072 | tf_op jit(solution)/shard_map/ppermute | solution.py:20
  393.8 8.2 %collective-permute-start.40 = (f32[224,128]{1,0:T(8,128)S(1)}, f32[224,128]{1,0:T(8,128)S(1)}, u32[]{:S(2)}, u32[]{:S(2)}) collective-permute-start(f32[224,128]{1,0:T(8,128)S(1)} %get-tuple-element.85), channel_id=1, source_target_pairs={{0,1},{1,2},{2,3},{3,4},{4,5},{5,6},{6,7},{7,8},{8,9},{9,10},{10,1... | collective-permute-start | bytes 344072 | tf_op jit(solution)/shard_map/ppermute | solution.py:20
  (39 other events, 862.0 us)
where the time goes:
time: 415 us; the launch traced here: 413 us
  waiting for transfers between devices  129 us (31%)
  starting transfers between devices  118 us (28%)
  blocking collectives  79.1 us (19%)
  local copies, waits for them, and re-layouts  60.6 us (15%)
  other arithmetic  14.5 us (3%)
  matrix products  8.21 us (2%)
    ppermute x42, waiting for transfers between devices, from_behind(): return lax.ppermute(block, axis, route)  129 us
    ppermute x42, starting transfers between devices, from_behind(): return lax.ppermute(block, axis, route)  118 us
    all_gather x3, blocking collectives, coarse_amplitude(): lax.all_gather(project, 'gz', axis=0, tiled=True)  50.2 us
    all_gather x1, blocking collectives, coarse_amplitude(): lax.all_gather(count_value, 'gz', axis=0, tiled=True)  28.9 us
    unnamed x301, local copies, waits for them, and re-layouts  24 us
  transfers between devices with their start and end apart: 42, of which 33 were waited for; matrix products, arithmetic and copies ran while one was open for 7% of the time, Pallas kernels for 0%

commit v1 on v0

v1 whole, which is shorter than its diff:
```python
import functools

import jax
import jax.numpy as jnp
import numpy as np
from jax import lax
from jax.experimental import pallas as pl
from jax.experimental.pallas import tpu as pltpu
from jax.sharding import PartitionSpec as P

FACE = 128
EDGE = 16
CORNER = 8
NMODE = 6
ITERS = 3
EIG_LOW = 0.5
EIG_HIGH = 6.0

F32 = jnp.float32
BF16 = jnp.bfloat16
HIGHEST = lax.Precision.HIGHEST
SIGNS = (1, -1, 0)
WIDTHS = {1: FACE, 2: EDGE, 3: CORNER}

BUNDLE = 224
GROUP = 8


def tables():
    begin, row = {}, 0
    for weight in (1, 2, 3):
        for o1 in (-1, 0, 1):
            for o2 in (-1, 0, 1):
                for o3 in (-1, 0, 1):
                    if abs(o1) + abs(o2) + abs(o3) == weight:
                        begin[(o1, o2, o3)] = row
                        row += WIDTHS[weight]
    slots, ours, row = [], {}, 0
    for o1 in SIGNS:
        for o2 in SIGNS:
            for o3 in SIGNS:
                offset = (o1, o2, o3)
                if any(offset):
                    width = WIDTHS[abs(o1) + abs(o2) + abs(o3)]
                    slots.append((offset, begin[offset], width))
                    ours[offset] = row
                    row += width
    return slots, ours, row


SLOTS, OURS, ROWS = tables()


def swaps(size, parity):
    pairs = [(i, i + 1) for i in range(parity, size - 1, 2)]
    return pairs + [(j, i) for i, j in pairs]


def exchange(first, second, axis):
    size = lax.axis_size(axis)
    return lax.ppermute(first, axis, swaps(size, 0)), lax.ppermute(second, axis, swaps(size, 1))


VMEM = pl.BlockSpec(memory_space=pltpu.VMEM)
SMEM = pl.BlockSpec(memory_space=pltpu.SMEM)


def call(kernel, out_shape, scalars, *args, scratch=(), name=None, limit=24):
    return pl.pallas_call(
        kernel,
        out_shape=[jax.ShapeDtypeStruct(s, t) for s, t in out_shape],
        in_specs=[SMEM] + [VMEM] * len(args),
        out_specs=[VMEM] * len(out_shape),
        scratch_shapes=list(scratch),
        compiler_params=pltpu.CompilerParams(vmem_limit_bytes=limit * 2**20),
        name=name,
    )(scalars, *args)


def split3(x):
    high = x.astype(BF16)
    rest = x - high.astype(F32)
    mid = rest.astype(BF16)
    return high, mid, (rest - mid.astype(F32)).astype(BF16)


def dot(a, b):
    return jnp.dot(a, b, preferred_element_type=F32)


def dot_t(a, b):
    return lax.dot_general(a, b, (((1,), (1,)), ((), ())), preferred_element_type=F32)


def dot_exact(a, x):
    high, mid, low = split3(x)
    return dot(a, high) + dot(a, mid) + dot(a, low)


def iota(shape, dim):
    return lax.broadcasted_iota(jnp.int32, shape, dim)


def layers(extra):
    return [(1, 0), (GROUP, BUNDLE)] if extra else [(1, 0)]


def bundle_rows(extra):
    return BUNDLE + BUNDLE // GROUP if extra else BUNDLE


def put(ref, at, pieces):
    for piece in pieces:
        ref[at : at + piece.shape[0], :] = piece
        at += piece.shape[0]


def put_pair(ref_a, ref_b, at, parity, plus, minus):
    even = parity == 0
    put(ref_a, at, [jnp.where(even, p, m) for p, m in zip(plus, minus)])
    put(ref_b, at, [jnp.where(even, m, p) for p, m in zip(plus, minus)])


def received(ref_a, ref_b, parity, scale, base):
    even = parity == 0

    def cut(ref, a, b):
        return ref[base + a // scale : base + b // scale, :]

    def up(a, b):
        return jnp.where(even, cut(ref_b, a, b), cut(ref_a, a, b))

    def down(a, b):
        return jnp.where(even, cut(ref_a, a, b), cut(ref_b, a, b))

    return up, down


def send_x(parity, values, send_a, send_b, extra):
    for value, (scale, base) in zip(values, layers(extra)):
        width = BUNDLE // scale
        put_pair(send_a, send_b, base, parity, [value[0:width, :]], [value[width : 2 * width, :]])


def route_y(extra, sc, *refs):
    count = 2 if extra else 1
    values, (xa, xb, ya, yb) = refs[:count], refs[count:]
    for value, (scale, base) in zip(values, layers(extra)):
        up, down = received(xa, xb, sc[0], scale, base)
        plus = [up(0, 32), down(0, 32), value[448 // scale : 608 // scale, :]]
        minus = [up(32, 64), down(32, 64), value[608 // scale : 768 // scale, :]]
        put_pair(ya, yb, base, sc[1], plus, minus)


def route_z(extra, sc, *refs):
    count = 2 if extra else 1
    values, (xa, xb, ya, yb, za, zb) = refs[:count], refs[count:]
    for value, (scale, base) in zip(values, layers(extra)):
        x_up, x_down = received(xa, xb, sc[0], scale, base)
        y_up, y_down = received(ya, yb, sc[1], scale, base)
        both = []
        for x_at, y_at, own in ((64, (0, 32, 64), 768), (80, (8, 40, 80), 896)):
            pieces = [x_up(x_at, x_at + EDGE), x_down(x_at, x_at + EDGE)]
            for y in (y_up, y_down):
                for at, width in zip(y_at, (CORNER, CORNER, EDGE)):
                    pieces.append(y(at, at + width))
            pieces.append(value[own // scale : (own + FACE) // scale, :])
            both.append(pieces)
        put_pair(za, zb, base, sc[2], both[0], both[1])


def partner_pieces(sc, xa, xb, ya, yb, za, zb, scale, base):
    x_up, x_down = received(xa, xb, sc[0], scale, base)
    y_up, y_down = received(ya, yb, sc[1], scale, base)
    z_up, z_down = received(za, zb, sc[2], scale, base)
    pieces = []
    for (o1, o2, o3), _, width in SLOTS:
        s1, s2, s3 = -o1, -o2, -o3
        if s3:
            reader = z_up if s3 == 1 else z_down
            if s2:
                at = 32 if s2 == 1 else 64
                at += {1: 0, -1: CORNER, 0: 2 * CORNER}[s1]
            elif s1:
                at = 0 if s1 == 1 else EDGE
            else:
                at = 96
        elif s2:
            reader = y_up if s2 == 1 else y_down
            at = {1: EDGE, -1: 32 + EDGE, 0: 96}[s1]
        else:
            reader = x_up if s1 == 1 else x_down
            at = 96
        pieces.append(reader(at, at + width))
    return pieces


def pack_kernel(sc, order_col, order_row, load, modes, sel_ref, inv_ref, load_ref, comp_ref, bt_ref, b_ref, xa, xb):
    step = 256
    for at in range(0, ROWS, step):
        lanes = iota((step, ROWS), 1)
        sel_ref[at : at + step, :] = jnp.where(order_col[at : at + step, :] == lanes, 1.0, 0.0).astype(BF16)
        subs = iota((step, ROWS), 0) + at
        inv_ref[at : at + step, :] = jnp.where(order_row[...] == subs, 1.0, 0.0).astype(BF16)
    sel = sel_ref[...]
    load_ref[...] = dot(sel, load[...])
    bt_ref[...] = dot(modes[...], inv_ref[...]).astype(BF16)
    cols = dot_t(sel, modes[...]).astype(BF16)
    b_ref[...] = cols
    spread = jnp.where(iota((16, 128), 0) == iota((16, 128), 1) % 16, 1.0, 0.0).astype(BF16)
    wide = dot(cols, spread)
    keep = iota((ROWS, 128), 0) % GROUP == iota((ROWS, 128), 1) // 16
    wide = jnp.where(keep, wide, 0.0).astype(BF16)
    fold = jnp.where(iota((ROWS // GROUP, ROWS), 0) == iota((ROWS // GROUP, ROWS), 1) // GROUP, 1.0, 0.0)
    comp_ref[...] = dot(fold.astype(BF16), wide)
    send_x(sc[0], (load_ref, comp_ref), xa, xb, True)


def permute_kernel(sc, sel, inv, dual, out):
    step = 256
    for at in range(0, ROWS, step):
        rows = dot(sel[at : at + step, :], dual[...]).astype(BF16)
        out[at : at + step, :] = dot(rows, inv[...]).astype(BF16)


def project(sc, bt, residual, out):
    block = dot_exact(bt[...], residual)[0:8, :]
    count = sc[4].astype(F32)
    block = jnp.where(iota((8, 128), 0) == NMODE, count, block)
    for t in range(out.shape[0]):
        out[t, :, :] = block


def first_kernel(sc, load, bt, xa, xb, ya, yb, za, zb, res_ref, comp_ref, out):
    pieces = partner_pieces(sc, xa, xb, ya, yb, za, zb, 1, 0)
    at = 0
    for piece in pieces:
        end = at + piece.shape[0]
        res_ref[at:end, :] = load[at:end, :] + piece
        at = end
    project(sc, bt, res_ref[...], out)
    put(comp_ref, 0, partner_pieces(sc, xa, xb, ya, yb, za, zb, GROUP, BUNDLE))


def next_residual(sc, res, val, bundles, out):
    at = 0
    for piece in partner_pieces(sc, *bundles, 1, 0):
        end = at + piece.shape[0]
        out[at:end, :] = res[at:end, :] - (val[at:end, :] + piece)
        at = end


def step_kernel(sc, res, val, bt, xa, xb, ya, yb, za, zb, res_ref, out):
    next_residual(sc, res, val, (xa, xb, ya, yb, za, zb), res_ref)
    project(sc, bt, res_ref[...], out)


def last_kernel(sc, res, val, inv, xa, xb, ya, yb, za, zb, out, scratch):
    next_residual(sc, res, val, (xa, xb, ya, yb, za, zb), scratch)
    out[...] = dot_exact(inv[...], scratch[...])


def unpack_kernel(sc, inv, val, out):
    out[...] = dot_exact(inv[...], val[...])


def mode_kernel(sc, cols, comp, block, out):
    pick = jnp.where(iota((ROWS, 128), 0) // GROUP == iota((ROWS, 128), 1), 1.0, 0.0).astype(BF16)
    wide = dot(pick, comp[...].astype(BF16))
    keep = iota((ROWS, 128), 0) % GROUP == iota((ROWS, 128), 1) // 16
    wide = jnp.where(keep, wide, 0.0).astype(BF16)
    mode = iota((128, 256), 0) % 16
    fold = jnp.where((mode == iota((128, 256), 1) % 8) & (mode < NMODE), 1.0, 0.0).astype(BF16)
    theirs = dot(wide, fold)
    mode = iota((16, 256), 0)
    own = jnp.where((mode == iota((16, 256), 1) % 8) & (mode < NMODE), 1.0, 0.0).astype(BF16)
    mine = dot(cols[...], own)
    x_even, y_even = sc[0] == 0, sc[1] == 0
    which = jnp.where(
        x_even,
        jnp.where(y_even, block[:, 0:1], block[:, 1:2]),
        jnp.where(y_even, block[:, 2:3], block[:, 3:4]),
    )
    at = iota((ROWS, 256), 1) // 8
    out[...] = (jnp.where(at == which, theirs, 0.0) + jnp.where(at == 1, mine, 0.0)).astype(BF16)


def line_kernel(sc, line, inverse, mat_ref, out):
    everyone = line[...]
    size, coarse = everyone.shape[0], inverse.shape[0]

    def selection(rows, first):
        row = iota((rows, size), 0) + first
        col = iota((rows, size), 1)
        is_count = col % 8 == NMODE
        here = jnp.where(is_count & (col // 8 == row // 8), 1.0, 0.0)
        before = jnp.where(is_count & (col // 8 < row // 8), 1.0, 0.0)
        count = jnp.dot(here, everyone, precision=HIGHEST, preferred_element_type=F32)
        offset = jnp.dot(before, everyone, precision=HIGHEST, preferred_element_type=F32)
        mode = ((iota((rows, 128), 0) + first) % 8).astype(F32)
        compact = iota((rows, 128), 1).astype(F32)
        hit = (compact == offset + mode) & (mode < count)
        return jnp.where(hit, 1.0, 0.0)[:, 0:coarse]

    everywhere = selection(size, 0)
    near = selection(24, 8 * sc[3] - 8)
    rows = jnp.dot(near, inverse[...], precision=HIGHEST, preferred_element_type=F32)
    matrix = lax.dot_general(rows, everywhere, (((1,), (1,)), ((), ())), precision=HIGHEST, preferred_element_type=F32)
    mat_ref[...] = matrix
    out[...] = jnp.dot(matrix, everyone, precision=HIGHEST, preferred_element_type=F32)


def solve_kernel(sc, line, matrix, out):
    out[...] = jnp.dot(matrix[...], line[...], precision=HIGHEST, preferred_element_type=F32)


def advance_kernel(keep, take, sc, *refs):
    if keep:
        res, modes, dual, own, ya, yb, xa, xb, old_dir, old_mul, dir_ref, mul_ref, val_ref, sa, sb, stack = refs
    else:
        res, modes, dual, own, ya, yb, xa, xb, dir_ref, val_ref, sa, sb, stack = refs
    put(stack, 0, [own[...], ya[...], yb[...], xa[...], xb[...], jnp.zeros((40, 128), F32)])
    corrected = res[...] - dot_exact(modes[...], stack[...])
    if keep:
        direction = keep * old_dir[...] + take * corrected
        mul_ref[...] = old_mul[...] + direction
    else:
        direction = corrected / take
    dir_ref[...] = direction
    val_ref[...] = dot(dual[...], direction.astype(BF16))
    send_x(sc[0], (val_ref,), sa, sb, False)


def cross(sc, values, sent, extra):
    rows = bundle_rows(extra)
    pair = [((rows, 128), F32)] * 2
    x = exchange(*sent, "gx")
    y = exchange(*call(functools.partial(route_y, extra), pair, sc, *values, *x, name="route_y"), "gy")
    z = exchange(*call(functools.partial(route_z, extra), pair, sc, *values, *x, *y, name="route_z"), "gz")
    return (*x, *y, *z)


def amplitude_blocks():
    out = np.zeros((ROWS, 4), np.int32)
    for x_odd in (0, 1):
        for y_odd in (0, 1):
            for (o1, o2, o3), _, width in SLOTS:
                at = OURS[(o1, o2, o3)]
                lab1 = 0 if o1 == 0 else 1 + ((o1 == -1) ^ x_odd)
                lab2 = 0 if o2 == 0 else 1 + ((o2 == -1) ^ y_odd)
                out[at : at + width, 2 * x_odd + y_odd] = 3 * (3 * lab1 + lab2) + o3 + 1
    return out


def local(dual_blocks, load_terms, row_order, mode_rows, mode_count, coarse_inverse):
    line_length = lax.axis_size("gz")
    pos = [lax.axis_index(axis) for axis in ("gx", "gy", "gz")]
    sc = jnp.stack([p % 2 for p in pos] + [pos[2], mode_count[0, 0, 0]]).astype(jnp.int32)
    packing = row_order[0, 0, 0]
    order = jnp.concatenate([packing[begin : begin + width] for _, begin, width in SLOTS])
    modes = jnp.pad(mode_rows[0, 0, 0].T, ((0, 16 - NMODE), (0, 0)))
    inverse = coarse_inverse[0, 0]
    bundle = [((BUNDLE, 128), F32)] * 2
    vector = ((ROWS, 128), F32)
    square = ((ROWS, ROWS), BF16)
    wide = [((bundle_rows(True), 128), F32)] * 2
    gathered = ((line_length, 8, 128), F32)

    sel, inv, load_rows, comp, bt, cols, sa, sb = call(
        pack_kernel,
        [square, square, vector, ((ROWS // GROUP, 128), F32), ((16, ROWS), BF16), ((ROWS, 16), BF16), *wide],
        sc,
        order[:, None],
        order[None, :],
        load_terms[0, 0, 0],
        modes,
        name="pack",
    )
    (dual,) = call(permute_kernel, [square], sc, sel, inv, dual_blocks[0, 0, 0], name="permute")
    received_rows = cross(sc, (load_rows, comp), (sa, sb), True)
    residual, their_comp, proj = call(
        first_kernel,
        [vector, ((ROWS // GROUP, 128), F32), gathered],
        sc,
        load_rows,
        bt,
        *received_rows,
        name="first",
    )
    (modes_near,) = call(
        mode_kernel, [((ROWS, 256), BF16)], sc, cols, their_comp, jnp.asarray(amplitude_blocks()), name="modes"
    )

    center_value = 0.5 * (EIG_HIGH + EIG_LOW)
    half_width = 0.5 * (EIG_HIGH - EIG_LOW)
    rho_prev = half_width / center_value
    amp = ((24, 128), F32)
    for iteration in range(ITERS):
        line = lax.all_to_all(proj, "gz", 0, 0, tiled=True).reshape(8 * line_length, 128)
        if iteration == 0:
            matrix, own = call(line_kernel, [((24, 8 * line_length), F32), amp], sc, line, inverse, name="line")
        else:
            (own,) = call(solve_kernel, [amp], sc, line, matrix, name="solve")
        ya, yb = exchange(own, own, "gy")
        column = jnp.concatenate([own, ya, yb], axis=0)
        xa, xb = exchange(column, column, "gx")
        near = (modes_near, dual, own, ya, yb, xa, xb)
        scratch = [pltpu.VMEM((256, 128), F32)]
        if iteration == 0:
            direction, value, sa, sb = call(
                functools.partial(advance_kernel, None, center_value),
                [vector, vector, *bundle],
                sc,
                residual,
                *near,
                scratch=scratch,
                name="advance0",
            )
            multipliers = direction
        else:
            rho_now = 1.0 / (2.0 * center_value / half_width - rho_prev)
            direction, multipliers, value, sa, sb = call(
                functools.partial(advance_kernel, rho_now * rho_prev, 2.0 * rho_now / half_width),
                [vector, vector, vector, *bundle],
                sc,
                residual,
                *near,
                direction,
                multipliers,
                scratch=scratch,
                name="advance",
            )
            rho_prev = rho_now
        received_rows = cross(sc, (value,), (sa, sb), False)
        if iteration < ITERS - 1:
            residual, proj = call(
                step_kernel, [vector, gathered], sc, residual, value, bt, *received_rows, name="step"
            )
    (out_mul,) = call(unpack_kernel, [vector], sc, inv, multipliers, name="unpack")
    (out_res,) = call(
        last_kernel,
        [vector],
        sc,
        residual,
        value,
        inv,
        *received_rows,
        scratch=[pltpu.VMEM((ROWS, 128), F32)],
        name="last",
    )
    return out_mul[None, None, None], out_res[None, None, None]


def solution(mesh):
    in_specs = (
        P("gx", "gy", "gz", None, None),
        P("gx", "gy", "gz", None, None),
        P("gx", "gy", "gz", None),
        P("gx", "gy", "gz", None, None),
        P("gx", "gy", "gz"),
        P("gx", "gy", None, None),
    )
    out_specs = (P("gx", "gy", "gz", None, None), P("gx", "gy", "gz", None, None))
    return jax.shard_map(local, mesh=mesh, in_specs=in_specs, out_specs=out_specs, check_vma=False)
```

time: 415 us -> 257 us (0.62)
  the two profiles are of different devices: /device:TPU:296 before, /device:TPU:87 now
where the time goes in v1:
time: 257 us; the launch traced here: 256 us
  starting transfers between devices  128 us (50%)
  waiting for transfers between devices  63.9 us (25%)
  Pallas kernels  32.7 us (13%)
  blocking collectives  25 us (10%)
  local copies, waits for them, and re-layouts  4.9 us (2%)
    ppermute x18, starting transfers between devices, exchange(): lax.ppermute(second, axis, swaps(size, 1))  71.6 us
    ppermute x18, starting transfers between devices, exchange(): lax.ppermute(first, axis, swaps(size, 0))  56.2 us
    ppermute x18, waiting for transfers between devices, exchange(): lax.ppermute(second, axis, swaps(size, 1))  51 us
    pallas_call x22, Pallas kernels, call(): pl.pallas_call(kernel, out_shape=[jax.ShapeDtypeStruct(s, t) for s, t in...  32.7 us
    all_to_all x3, blocking collectives, local(): lax.all_to_all(proj, 'gz', 0, 0, tiled=True).reshape(8 * line_length, 128)  25 us
    ppermute x18, waiting for transfers between devices, exchange(): lax.ppermute(first, axis, swaps(size, 0))  13 us
  transfers between devices with their start and end apart: 36, of which 21 were waited for; matrix products, arithmetic and copies ran while one was open for 0% of the time, Pallas kernels for 4%

profile of v1, /device:TPU:87, one launch (start us, length us, event | category | flops | bytes accessed | tf_op | source)
XLA Modules:
  0.0 256.2 jit_solution(8915905705603052658)
XLA Ops:
  11.2 5.9 %collective-permute-start.1 = (f32[252,128]{1,0:T(8,128)S(1)}, f32[252,128]{1,0:T(8,128)S(1)}, u32[]{:S(2)}, u32[]{:S(2)}) collective-permute-start(f32[252,128]{1,0:T(8,128)S(1)} %get-tuple-element.52), channel_id=1, source_target_pairs={{128,256},{256,128},{129,257},{257,129},{130,258},{258,130},{131,2... | collective-permute-start | bytes 387080 | tf_op jit(solution)/shard_map/ppermute | solution.py:61
  17.1 5.4 %collective-permute-done.1.refs_3_.xb = f32[252,128]{1,0:T(8,128)S(1)} collective-permute-done((f32[252,128]{1,0:T(8,128)S(1)}, f32[252,128]{1,0:T(8,128)S(1)}, u32[]{:S(2)}, u32[]{:S(2)}) %collective-permute-start.1) | collective-permute-done | bytes 129056 | tf_op jit(solution)/shard_map/ppermute | solution.py:61
  25.0 6.1 %collective-permute-start.3 = (f32[252,128]{1,0:T(8,128)S(1)}, f32[252,128]{1,0:T(8,128)S(1)}, u32[]{:S(2)}, u32[]{:S(2)}) collective-permute-start(f32[252,128]{1,0:T(8,128)S(1)} %get-tuple-element.55), channel_id=1, source_target_pairs={{16,32},{48,64},{80,96},{32,16},{64,48},{96,80},{17,33},{49,65},{8... | collective-permute-start | bytes 387080 | tf_op jit(solution)/shard_map/ppermute | solution.py:61
  34.0 4.2 %collective-permute-start.4 = (f32[252,128]{1,0:T(8,128)S(1)}, f32[252,128]{1,0:T(8,128)S(1)}, u32[]{:S(2)}, u32[]{:S(2)}) collective-permute-start(f32[252,128]{1,0:T(8,128)S(1)} %get-tuple-element.56), channel_id=1, source_target_pairs={{0,1},{2,3},{4,5},{6,7},{8,9},{10,11},{12,13},{14,15},{1,0},{3,2},... | collective-permute-start | bytes 387080 | tf_op jit(solution)/shard_map/ppermute | solution.py:61
  41.3 5.2 %collective-permute-done.5.zb = f32[252,128]{1,0:T(8,128)S(1)} collective-permute-done((f32[252,128]{1,0:T(8,128)S(1)}, f32[252,128]{1,0:T(8,128)S(1)}, u32[]{:S(2)}, u32[]{:S(2)}) %collective-permute-start.5) | collective-permute-done | bytes 129056 | tf_op jit(solution)/shard_map/ppermute | solution.py:61
  47.4 8.3 %all_to_all.15 = f32[16,8,128]{2,1,0:T(8,128)S(1)} all-to-all(f32[16,8,128]{2,1,0:T(8,128)S(1)} %get-tuple-element.62), channel_id=1, replica_groups=mesh['gx'=4,'gy'=8,'gz'=16] {'gz'}, dimensions={0} | all-to-all | bytes 131072 | tf_op jit(solution)/shard_map/all_to_all | solution.py:399
  57.3 3.6 %collective-permute-start.7 = (f32[24,128]{1,0:T(8,128)S(1)}, f32[24,128]{1,0:T(8,128)S(1)}, u32[]{:S(2)}, u32[]{:S(2)}) collective-permute-start(f32[24,128]{1,0:T(8,128)S(1)} %get-tuple-element.63.refs_3_), channel_id=1, source_target_pairs={{16,32},{48,64},{80,96},{32,16},{64,48},{96,80},{17,33},{49,65},{8... | collective-permute-start | bytes 36872 | tf_op jit(solution)/shard_map/ppermute | solution.py:61
  65.4 5.3 %collective-permute-start.9 = (f32[72,128]{1,0:T(8,128)S(1)}, f32[72,128]{1,0:T(8,128)S(1)}, u32[]{:S(2)}, u32[]{:S(2)}) collective-permute-start(f32[72,128]{1,0:T(8,128)S(1)} %constant_dynamic-update-slice_fusion), channel_id=1, source_target_pairs={{128,256},{256,128},{129,257},{257,129},{130,258},{258,130},{131,2... | collective-permute-start | bytes 110600 | tf_op jit(solution)/shard_map/ppermute | solution.py:61
  72.7 5.1 %permute.1.refs_2_ = bf16[1024,1024]{1,0:T(8,128)(2,1)S(1)} custom-call(s32[5]{0:T(128)S(1)} %stack.19.sc, bf16[1024,1024]{1,0:T(8,128)(2,1)S(1)} %get-tuple-element.61.sel, bf16[1024,1024]{1,0:T(8,128)(2,1)S(1)} %get-tuple-element.48.inv, bf16[1024,1024]{1,0:T(8,128)(2,1)S(1)} %bitcast.71), custom_call_target="tpu_custom_call" | custom-call | tf_op jit(solution)/shard_map/permute/pallas_call | solution.py:69
  81.4 4.3 %collective-permute-start.10 = (f32[224,128]{1,0:T(8,128)S(1)}, f32[224,128]{1,0:T(8,128)S(1)}, u32[]{:S(2)}, u32[]{:S(2)}) collective-permute-start(f32[224,128]{1,0:T(8,128)S(1)} %get-tuple-element.65), channel_id=1, source_target_pairs={{0,128},{256,384},{128,0},{384,256},{1,129},{257,385},{129,1},{385... | collective-permute-start | bytes 344072 | tf_op jit(solution)/shard_map/ppermute | solution.py:61
  88.6 5.9 %collective-permute-done.11.refs_2_.xb = f32[224,128]{1,0:T(8,128)S(1)} collective-permute-done((f32[224,128]{1,0:T(8,128)S(1)}, f32[224,128]{1,0:T(8,128)S(1)}, u32[]{:S(2)}, u32[]{:S(2)}) %collective-permute-start.11) | collective-permute-done | bytes 114720 | tf_op jit(solution)/shard_map/ppermute | solution.py:61
  97.0 7.6 %collective-permute-start.13 = (f32[224,128]{1,0:T(8,128)S(1)}, f32[224,128]{1,0:T(8,128)S(1)}, u32[]{:S(2)}, u32[]{:S(2)}) collective-permute-start(f32[224,128]{1,0:T(8,128)S(1)} %get-tuple-element.68), channel_id=1, source_target_pairs={{16,32},{48,64},{80,96},{32,16},{64,48},{96,80},{17,33},{49,65},{8... | collective-permute-start | bytes 344072 | tf_op jit(solution)/shard_map/ppermute | solution.py:61
  107.4 6.9 %collective-permute-start.14 = (f32[224,128]{1,0:T(8,128)S(1)}, f32[224,128]{1,0:T(8,128)S(1)}, u32[]{:S(2)}, u32[]{:S(2)}) collective-permute-start(f32[224,128]{1,0:T(8,128)S(1)} %get-tuple-element.69), channel_id=1, source_target_pairs={{0,1},{2,3},{4,5},{6,7},{8,9},{10,11},{12,13},{14,15},{1,0},{3,2},... | collective-permute-start | bytes 344072 | tf_op jit(solution)/shard_map/ppermute | solution.py:61
  116.7 5.8 %collective-permute-done.15.zb = f32[224,128]{1,0:T(8,128)S(1)} collective-permute-done((f32[224,128]{1,0:T(8,128)S(1)}, f32[224,128]{1,0:T(8,128)S(1)}, u32[]{:S(2)}, u32[]{:S(2)}) %collective-permute-start.15) | collective-permute-done | bytes 114720 | tf_op jit(solution)/shard_map/ppermute | solution.py:61
  123.3 8.3 %all_to_all.16 = f32[16,8,128]{2,1,0:T(8,128)S(1)} all-to-all(f32[16,8,128]{2,1,0:T(8,128)S(1)} %get-tuple-element.72), channel_id=1, replica_groups=mesh['gx'=4,'gy'=8,'gz'=16] {'gz'}, dimensions={0} | all-to-all | bytes 131072 | tf_op jit(solution)/shard_map/all_to_all | solution.py:399
  152.7 5.5 %collective-permute-start.21 = (f32[224,128]{1,0:T(8,128)S(1)}, f32[224,128]{1,0:T(8,128)S(1)}, u32[]{:S(2)}, u32[]{:S(2)}) collective-permute-start(f32[224,128]{1,0:T(8,128)S(1)} %get-tuple-element.77), channel_id=1, source_target_pairs={{128,256},{256,128},{129,257},{257,129},{130,258},{258,130},{131,2... | collective-permute-start | bytes 344072 | tf_op jit(solution)/shard_map/ppermute | solution.py:61
  163.9 4.3 %collective-permute-start.23 = (f32[224,128]{1,0:T(8,128)S(1)}, f32[224,128]{1,0:T(8,128)S(1)}, u32[]{:S(2)}, u32[]{:S(2)}) collective-permute-start(f32[224,128]{1,0:T(8,128)S(1)} %get-tuple-element.79), channel_id=1, source_target_pairs={{16,32},{48,64},{80,96},{32,16},{64,48},{96,80},{17,33},{49,65},{8... | collective-permute-start | bytes 344072 | tf_op jit(solution)/shard_map/ppermute | solution.py:61
  170.9 7.4 %collective-permute-start.24 = (f32[224,128]{1,0:T(8,128)S(1)}, f32[224,128]{1,0:T(8,128)S(1)}, u32[]{:S(2)}, u32[]{:S(2)}) collective-permute-start(f32[224,128]{1,0:T(8,128)S(1)} %get-tuple-element.80), channel_id=1, source_target_pairs={{0,1},{2,3},{4,5},{6,7},{8,9},{10,11},{12,13},{14,15},{1,0},{3,2},... | collective-permute-start | bytes 344072 | tf_op jit(solution)/shard_map/ppermute | solution.py:61
  180.6 5.9 %collective-permute-done.25.zb = f32[224,128]{1,0:T(8,128)S(1)} collective-permute-done((f32[224,128]{1,0:T(8,128)S(1)}, f32[224,128]{1,0:T(8,128)S(1)}, u32[]{:S(2)}, u32[]{:S(2)}) %collective-permute-start.25) | collective-permute-done | bytes 114720 | tf_op jit(solution)/shard_map/ppermute | solution.py:61
  187.4 8.3 %all_to_all.17 = f32[16,8,128]{2,1,0:T(8,128)S(1)} all-to-all(f32[16,8,128]{2,1,0:T(8,128)S(1)} %get-tuple-element.83), channel_id=1, replica_groups=mesh['gx'=4,'gy'=8,'gz'=16] {'gz'}, dimensions={0} | all-to-all | bytes 131072 | tf_op jit(solution)/shard_map/all_to_all | solution.py:399
  204.5 4.7 %collective-permute-start.29 = (f32[72,128]{1,0:T(8,128)S(1)}, f32[72,128]{1,0:T(8,128)S(1)}, u32[]{:S(2)}, u32[]{:S(2)}) collective-permute-start(f32[72,128]{1,0:T(8,128)S(1)} %pad_maximum_fusion.1), channel_id=1, source_target_pairs={{128,256},{256,128},{129,257},{257,129},{130,258},{258,130},{131,2... | collective-permute-start | bytes 110600 | tf_op jit(solution)/shard_map/ppermute | solution.py:61
  223.7 4.3 %collective-permute-done.31.refs_2_.xb = f32[224,128]{1,0:T(8,128)S(1)} collective-permute-done((f32[224,128]{1,0:T(8,128)S(1)}, f32[224,128]{1,0:T(8,128)S(1)}, u32[]{:S(2)}, u32[]{:S(2)}) %collective-permute-start.31) | collective-permute-done | bytes 114720 | tf_op jit(solution)/shard_map/ppermute | solution.py:61
  230.6 4.0 %collective-permute-start.33 = (f32[224,128]{1,0:T(8,128)S(1)}, f32[224,128]{1,0:T(8,128)S(1)}, u32[]{:S(2)}, u32[]{:S(2)}) collective-permute-start(f32[224,128]{1,0:T(8,128)S(1)} %get-tuple-element.91), channel_id=1, source_target_pairs={{16,32},{48,64},{80,96},{32,16},{64,48},{96,80},{17,33},{49,65},{8... | collective-permute-start | bytes 344072 | tf_op jit(solution)/shard_map/ppermute | solution.py:61
  237.3 7.5 %collective-permute-start.34 = (f32[224,128]{1,0:T(8,128)S(1)}, f32[224,128]{1,0:T(8,128)S(1)}, u32[]{:S(2)}, u32[]{:S(2)}) collective-permute-start(f32[224,128]{1,0:T(8,128)S(1)} %get-tuple-element.92), channel_id=1, source_target_pairs={{0,1},{2,3},{4,5},{6,7},{8,9},{10,11},{12,13},{14,15},{1,0},{3,2},... | collective-permute-start | bytes 344072 | tf_op jit(solution)/shard_map/ppermute | solution.py:61
  (93 shorter events, 114.5 us)
Async XLA Ops:
  9.2 7.9 %collective-permute-start = (f32[252,128]{1,0:T(8,128)S(1)}, f32[252,128]{1,0:T(8,128)S(1)}, u32[]{:S(2)}, u32[]{:S(2)}) collective-permute-start(f32[252,128]{1,0:T(8,128)S(1)} %get-tuple-element.51), channel_id=1, source_target_pairs={{0,128},{256,384},{128,0},{384,256},{1,129},{257,385},{129,1},{385... | collective-permute-start | bytes 387080 | tf_op jit(solution)/shard_map/ppermute | solution.py:61
  11.2 11.3 %collective-permute-start.1 = (f32[252,128]{1,0:T(8,128)S(1)}, f32[252,128]{1,0:T(8,128)S(1)}, u32[]{:S(2)}, u32[]{:S(2)}) collective-permute-start(f32[252,128]{1,0:T(8,128)S(1)} %get-tuple-element.52), channel_id=1, source_target_pairs={{128,256},{256,128},{129,257},{257,129},{130,258},{258,130},{131,2... | collective-permute-start | bytes 387080 | tf_op jit(solution)/shard_map/ppermute | solution.py:61
  23.1 8.0 %collective-permute-start.2 = (f32[252,128]{1,0:T(8,128)S(1)}, f32[252,128]{1,0:T(8,128)S(1)}, u32[]{:S(2)}, u32[]{:S(2)}) collective-permute-start(f32[252,128]{1,0:T(8,128)S(1)} %get-tuple-element.54), channel_id=1, source_target_pairs={{0,16},{32,48},{64,80},{96,112},{16,0},{48,32},{80,64},{112,96},{1... | collective-permute-start | bytes 387080 | tf_op jit(solution)/shard_map/ppermute | solution.py:61
  25.0 8.4 %collective-permute-start.3 = (f32[252,128]{1,0:T(8,128)S(1)}, f32[252,128]{1,0:T(8,128)S(1)}, u32[]{:S(2)}, u32[]{:S(2)}) collective-permute-start(f32[252,128]{1,0:T(8,128)S(1)} %get-tuple-element.55), channel_id=1, source_target_pairs={{16,32},{48,64},{80,96},{32,16},{64,48},{96,80},{17,33},{49,65},{8... | collective-permute-start | bytes 387080 | tf_op jit(solution)/shard_map/ppermute | solution.py:61
  34.0 7.3 %collective-permute-start.4 = (f32[252,128]{1,0:T(8,128)S(1)}, f32[252,128]{1,0:T(8,128)S(1)}, u32[]{:S(2)}, u32[]{:S(2)}) collective-permute-start(f32[252,128]{1,0:T(8,128)S(1)} %get-tuple-element.56), channel_id=1, source_target_pairs={{0,1},{2,3},{4,5},{6,7},{8,9},{10,11},{12,13},{14,15},{1,0},{3,2},... | collective-permute-start | bytes 387080 | tf_op jit(solution)/shard_map/ppermute | solution.py:61
  38.2 8.4 %collective-permute-start.5 = (f32[252,128]{1,0:T(8,128)S(1)}, f32[252,128]{1,0:T(8,128)S(1)}, u32[]{:S(2)}, u32[]{:S(2)}) collective-permute-start(f32[252,128]{1,0:T(8,128)S(1)} %get-tuple-element.57), channel_id=1, source_target_pairs={{1,2},{3,4},{5,6},{7,8},{9,10},{11,12},{13,14},{2,1},{4,3},{6,5},{... | collective-permute-start | bytes 387080 | tf_op jit(solution)/shard_map/ppermute | solution.py:61
  57.3 8.1 %collective-permute-start.7 = (f32[24,128]{1,0:T(8,128)S(1)}, f32[24,128]{1,0:T(8,128)S(1)}, u32[]{:S(2)}, u32[]{:S(2)}) collective-permute-start(f32[24,128]{1,0:T(8,128)S(1)} %get-tuple-element.63.refs_3_), channel_id=1, source_target_pairs={{16,32},{48,64},{80,96},{32,16},{64,48},{96,80},{17,33},{49,65},{8... | collective-permute-start | bytes 36872 | tf_op jit(solution)/shard_map/ppermute | solution.py:61
  65.4 13.5 %collective-permute-start.9 = (f32[72,128]{1,0:T(8,128)S(1)}, f32[72,128]{1,0:T(8,128)S(1)}, u32[]{:S(2)}, u32[]{:S(2)}) collective-permute-start(f32[72,128]{1,0:T(8,128)S(1)} %constant_dynamic-update-slice_fusion), channel_id=1, source_target_pairs={{128,256},{256,128},{129,257},{257,129},{130,258},{258,130},{131,2... | collective-permute-start | bytes 110600 | tf_op jit(solution)/shard_map/ppermute | solution.py:61
  70.8 8.2 %collective-permute-start.8 = (f32[72,128]{1,0:T(8,128)S(1)}, f32[72,128]{1,0:T(8,128)S(1)}, u32[]{:S(2)}, u32[]{:S(2)}) collective-permute-start(f32[72,128]{1,0:T(8,128)S(1)} %constant_dynamic-update-slice_fusion), channel_id=1, source_target_pairs={{0,128},{256,384},{128,0},{384,256},{1,129},{257,385},{129,1},{385... | collective-permute-start | bytes 110600 | tf_op jit(solution)/shard_map/ppermute | solution.py:61
  81.4 7.2 %collective-permute-start.10 = (f32[224,128]{1,0:T(8,128)S(1)}, f32[224,128]{1,0:T(8,128)S(1)}, u32[]{:S(2)}, u32[]{:S(2)}) collective-permute-start(f32[224,128]{1,0:T(8,128)S(1)} %get-tuple-element.65), channel_id=1, source_target_pairs={{0,128},{256,384},{128,0},{384,256},{1,129},{257,385},{129,1},{385... | collective-permute-start | bytes 344072 | tf_op jit(solution)/shard_map/ppermute | solution.py:61
  85.6 8.9 %collective-permute-start.11 = (f32[224,128]{1,0:T(8,128)S(1)}, f32[224,128]{1,0:T(8,128)S(1)}, u32[]{:S(2)}, u32[]{:S(2)}) collective-permute-start(f32[224,128]{1,0:T(8,128)S(1)} %get-tuple-element.66), channel_id=1, source_target_pairs={{128,256},{256,128},{129,257},{257,129},{130,258},{258,130},{131,2... | collective-permute-start | bytes 344072 | tf_op jit(solution)/shard_map/ppermute | solution.py:61
  95.1 9.5 %collective-permute-start.12 = (f32[224,128]{1,0:T(8,128)S(1)}, f32[224,128]{1,0:T(8,128)S(1)}, u32[]{:S(2)}, u32[]{:S(2)}) collective-permute-start(f32[224,128]{1,0:T(8,128)S(1)} %get-tuple-element.67), channel_id=1, source_target_pairs={{0,16},{32,48},{64,80},{96,112},{16,0},{48,32},{80,64},{112,96},{1... | collective-permute-start | bytes 344072 | tf_op jit(solution)/shard_map/ppermute | solution.py:61
  97.0 9.8 %collective-permute-start.13 = (f32[224,128]{1,0:T(8,128)S(1)}, f32[224,128]{1,0:T(8,128)S(1)}, u32[]{:S(2)}, u32[]{:S(2)}) collective-permute-start(f32[224,128]{1,0:T(8,128)S(1)} %get-tuple-element.68), channel_id=1, source_target_pairs={{16,32},{48,64},{80,96},{32,16},{64,48},{96,80},{17,33},{49,65},{8... | collective-permute-start | bytes 344072 | tf_op jit(solution)/shard_map/ppermute | solution.py:61
  107.4 9.3 %collective-permute-start.14 = (f32[224,128]{1,0:T(8,128)S(1)}, f32[224,128]{1,0:T(8,128)S(1)}, u32[]{:S(2)}, u32[]{:S(2)}) collective-permute-start(f32[224,128]{1,0:T(8,128)S(1)} %get-tuple-element.69), channel_id=1, source_target_pairs={{0,1},{2,3},{4,5},{6,7},{8,9},{10,11},{12,13},{14,15},{1,0},{3,2},... | collective-permute-start | bytes 344072 | tf_op jit(solution)/shard_map/ppermute | solution.py:61
  114.2 8.2 %collective-permute-start.15 = (f32[224,128]{1,0:T(8,128)S(1)}, f32[224,128]{1,0:T(8,128)S(1)}, u32[]{:S(2)}, u32[]{:S(2)}) collective-permute-start(f32[224,128]{1,0:T(8,128)S(1)} %get-tuple-element.70), channel_id=1, source_target_pairs={{1,2},{3,4},{5,6},{7,8},{9,10},{11,12},{13,14},{2,1},{4,3},{6,5},{... | collective-permute-start | bytes 344072 | tf_op jit(solution)/shard_map/ppermute | solution.py:61
  140.5 7.2 %collective-permute-start.19 = (f32[72,128]{1,0:T(8,128)S(1)}, f32[72,128]{1,0:T(8,128)S(1)}, u32[]{:S(2)}, u32[]{:S(2)}) collective-permute-start(f32[72,128]{1,0:T(8,128)S(1)} %pad_maximum_fusion), channel_id=1, source_target_pairs={{128,256},{256,128},{129,257},{257,129},{130,258},{258,130},{131,2... | collective-permute-start | bytes 110600 | tf_op jit(solution)/shard_map/ppermute | solution.py:61
  150.3 7.8 %collective-permute-start.20 = (f32[224,128]{1,0:T(8,128)S(1)}, f32[224,128]{1,0:T(8,128)S(1)}, u32[]{:S(2)}, u32[]{:S(2)}) collective-permute-start(f32[224,128]{1,0:T(8,128)S(1)} %get-tuple-element.76), channel_id=1, source_target_pairs={{0,128},{256,384},{128,0},{384,256},{1,129},{257,385},{129,1},{385... | collective-permute-start | bytes 344072 | tf_op jit(solution)/shard_map/ppermute | solution.py:61
  152.7 8.5 %collective-permute-start.21 = (f32[224,128]{1,0:T(8,128)S(1)}, f32[224,128]{1,0:T(8,128)S(1)}, u32[]{:S(2)}, u32[]{:S(2)}) collective-permute-start(f32[224,128]{1,0:T(8,128)S(1)} %get-tuple-element.77), channel_id=1, source_target_pairs={{128,256},{256,128},{129,257},{257,129},{130,258},{258,130},{131,2... | collective-permute-start | bytes 344072 | tf_op jit(solution)/shard_map/ppermute | solution.py:61
  170.9 9.7 %collective-permute-start.24 = (f32[224,128]{1,0:T(8,128)S(1)}, f32[224,128]{1,0:T(8,128)S(1)}, u32[]{:S(2)}, u32[]{:S(2)}) collective-permute-start(f32[224,128]{1,0:T(8,128)S(1)} %get-tuple-element.80), channel_id=1, source_target_pairs={{0,1},{2,3},{4,5},{6,7},{8,9},{10,11},{12,13},{14,15},{1,0},{3,2},... | collective-permute-start | bytes 344072 | tf_op jit(solution)/shard_map/ppermute | solution.py:61
  178.3 8.2 %collective-permute-start.25 = (f32[224,128]{1,0:T(8,128)S(1)}, f32[224,128]{1,0:T(8,128)S(1)}, u32[]{:S(2)}, u32[]{:S(2)}) collective-permute-start(f32[224,128]{1,0:T(8,128)S(1)} %get-tuple-element.81), channel_id=1, source_target_pairs={{1,2},{3,4},{5,6},{7,8},{9,10},{11,12},{13,14},{2,1},{4,3},{6,5},{... | collective-permute-start | bytes 344072 | tf_op jit(solution)/shard_map/ppermute | solution.py:61
  204.5 7.2 %collective-permute-start.29 = (f32[72,128]{1,0:T(8,128)S(1)}, f32[72,128]{1,0:T(8,128)S(1)}, u32[]{:S(2)}, u32[]{:S(2)}) collective-permute-start(f32[72,128]{1,0:T(8,128)S(1)} %pad_maximum_fusion.1), channel_id=1, source_target_pairs={{128,256},{256,128},{129,257},{257,129},{130,258},{258,130},{131,2... | collective-permute-start | bytes 110600 | tf_op jit(solution)/shard_map/ppermute | solution.py:61
  219.5 8.5 %collective-permute-start.31 = (f32[224,128]{1,0:T(8,128)S(1)}, f32[224,128]{1,0:T(8,128)S(1)}, u32[]{:S(2)}, u32[]{:S(2)}) collective-permute-start(f32[224,128]{1,0:T(8,128)S(1)} %get-tuple-element.89), channel_id=1, source_target_pairs={{128,256},{256,128},{129,257},{257,129},{130,258},{258,130},{131,2... | collective-permute-start | bytes 344072 | tf_op jit(solution)/shard_map/ppermute | solution.py:61
  237.3 13.1 %collective-permute-start.34 = (f32[224,128]{1,0:T(8,128)S(1)}, f32[224,128]{1,0:T(8,128)S(1)}, u32[]{:S(2)}, u32[]{:S(2)}) collective-permute-start(f32[224,128]{1,0:T(8,128)S(1)} %get-tuple-element.92), channel_id=1, source_target_pairs={{0,1},{2,3},{4,5},{6,7},{8,9},{10,11},{12,13},{14,15},{1,0},{3,2},... | collective-permute-start | bytes 344072 | tf_op jit(solution)/shard_map/ppermute | solution.py:61
  244.8 8.2 %collective-permute-start.35 = (f32[224,128]{1,0:T(8,128)S(1)}, f32[224,128]{1,0:T(8,128)S(1)}, u32[]{:S(2)}, u32[]{:S(2)}) collective-permute-start(f32[224,128]{1,0:T(8,128)S(1)} %get-tuple-element.93), channel_id=1, source_target_pairs={{1,2},{3,4},{5,6},{7,8},{9,10},{11,12},{13,14},{2,1},{4,3},{6,5},{... | collective-permute-start | bytes 344072 | tf_op jit(solution)/shard_map/ppermute | solution.py:61
  (16 other events, 189.4 us)

commit v2 on v1

--- a/solution.py
+++ b/solution.py
@@ -58,14 +58,22 @@
 
 def exchange(first, second, axis):
     size = lax.axis_size(axis)
+    groups = [[i, i + 1] for i in range(0, size, 2)]
+    other = lax.ppermute(second, axis, swaps(size, 1))
+    return lax.all_gather(first, axis, axis_index_groups=groups, tiled=True), other
+
+
+def exchange_async(first, second, axis):
+    size = lax.axis_size(axis)
     return lax.ppermute(first, axis, swaps(size, 0)), lax.ppermute(second, axis, swaps(size, 1))
 
 
 VMEM = pl.BlockSpec(memory_space=pltpu.VMEM)
+HBM = pl.BlockSpec(memory_space=pltpu.HBM)
 SMEM = pl.BlockSpec(memory_space=pltpu.SMEM)
 
 
-def call(kernel, out_shape, scalars, *args, scratch=(), name=None, limit=24):
+def call(kernel, out_shape, scalars, *args, scratch=(), name=None, limit=12):
     return pl.pallas_call(
         kernel,
         out_shape=[jax.ShapeDtypeStruct(s, t) for s, t in out_shape],
@@ -77,6 +85,10 @@
     )(scalars, *args)
 
 
+def in_hbm(x):
+    return pltpu.with_memory_space_constraint(x, pltpu.HBM)
+
+
 def split3(x):
     high = x.astype(BF16)
     rest = x - high.astype(F32)
@@ -93,8 +105,9 @@
 
 
 def dot_exact(a, x):
-    high, mid, low = split3(x)
-    return dot(a, high) + dot(a, mid) + dot(a, low)
+    out = dot(a, jnp.concatenate(split3(x), axis=1))
+    width = x.shape[1]
+    return out[:, 0:width] + out[:, width : 2 * width] + out[:, 2 * width :]
 
 
 def iota(shape, dim):
@@ -123,15 +136,17 @@
 
 def received(ref_a, ref_b, parity, scale, base):
     even = parity == 0
-
-    def cut(ref, a, b):
-        return ref[base + a // scale : base + b // scale, :]
+    rows = ref_b.shape[0]
+    paired = ref_a.shape[0] > rows
+
+    def cut(ref, a, b, shift=0):
+        return ref[shift + base + a // scale : shift + base + b // scale, :]
 
     def up(a, b):
         return jnp.where(even, cut(ref_b, a, b), cut(ref_a, a, b))
 
     def down(a, b):
-        return jnp.where(even, cut(ref_a, a, b), cut(ref_b, a, b))
+        return jnp.where(even, cut(ref_a, a, b, rows if paired else 0), cut(ref_b, a, b))
 
     return up, down
 
@@ -195,32 +210,50 @@
     return pieces
 
 
-def pack_kernel(sc, order_col, order_row, load, modes, sel_ref, inv_ref, load_ref, comp_ref, bt_ref, b_ref, xa, xb):
+def pack_kernel(sc, order, load, modes, sel_ref, load_ref, comp_ref, mode, row_ref, xa, xb, col, buf, mbuf, sems):
+    copy = pltpu.make_async_copy(load, buf, sems.at[0])
+    copy.start()
+    copy_modes = pltpu.make_async_copy(modes, mbuf, sems.at[1])
+    copy_modes.start()
+    for offset, begin, width in SLOTS:
+        col[OURS[offset] : OURS[offset] + width, :] = order[begin : begin + width, :]
     step = 256
     for at in range(0, ROWS, step):
         lanes = iota((step, ROWS), 1)
-        sel_ref[at : at + step, :] = jnp.where(order_col[at : at + step, :] == lanes, 1.0, 0.0).astype(BF16)
-        subs = iota((step, ROWS), 0) + at
-        inv_ref[at : at + step, :] = jnp.where(order_row[...] == subs, 1.0, 0.0).astype(BF16)
+        sel_ref[at : at + step, :] = jnp.where(col[at : at + step, :] == lanes, 1.0, 0.0).astype(BF16)
+    lane = iota((8, ROWS), 1)
+    digits = jnp.where(iota((8, ROWS), 0) == 0, lane // 256, jnp.where(iota((8, ROWS), 0) == 1, lane % 256, 0))
+    copy_modes.wait()
+    top = jnp.concatenate([mbuf[...].astype(F32), jnp.zeros((8 - NMODE, ROWS), F32)], axis=0)
+    mode[...] = jnp.concatenate([top, digits.astype(F32)], axis=0).astype(BF16)
     sel = sel_ref[...]
-    load_ref[...] = dot(sel, load[...])
-    bt_ref[...] = dot(modes[...], inv_ref[...]).astype(BF16)
-    cols = dot_t(sel, modes[...]).astype(BF16)
-    b_ref[...] = cols
+    rows = dot_t(mode[...], sel)
+    row_ref[...] = (rows[8:9, :] * 256.0 + rows[9:10, :]).astype(jnp.int32)
+    cols = dot_t(sel, mode[...]).astype(BF16)
     spread = jnp.where(iota((16, 128), 0) == iota((16, 128), 1) % 16, 1.0, 0.0).astype(BF16)
     wide = dot(cols, spread)
     keep = iota((ROWS, 128), 0) % GROUP == iota((ROWS, 128), 1) // 16
     wide = jnp.where(keep, wide, 0.0).astype(BF16)
     fold = jnp.where(iota((ROWS // GROUP, ROWS), 0) == iota((ROWS // GROUP, ROWS), 1) // GROUP, 1.0, 0.0)
     comp_ref[...] = dot(fold.astype(BF16), wide)
+    copy.wait()
+    load_ref[...] = dot(sel, buf[...])
     send_x(sc[0], (load_ref, comp_ref), xa, xb, True)
 
 
-def permute_kernel(sc, sel, inv, dual, out):
+def permute_kernel(sel, mode, order_row, dual, out, inv_ref, bt_ref, cols_ref, buf, sem):
+    copy = pltpu.make_async_copy(dual, buf, sem)
+    copy.start()
     step = 256
     for at in range(0, ROWS, step):
-        rows = dot(sel[at : at + step, :], dual[...]).astype(BF16)
-        out[at : at + step, :] = dot(rows, inv[...]).astype(BF16)
+        subs = iota((step, ROWS), 0) + at
+        inv_ref[at : at + step, :] = jnp.where(order_row[...] == subs, 1.0, 0.0).astype(BF16)
+    bt_ref[...] = dot(mode[...], inv_ref[...]).astype(BF16)
+    cols_ref[...] = dot_t(sel[...], mode[...]).astype(BF16)
+    copy.wait()
+    for at in range(0, ROWS, step):
+        rows = dot(sel[at : at + step, :], buf[...]).astype(BF16)
+        out[at : at + step, :] = dot(rows, inv_ref[...]).astype(BF16)
 
 
 def project(sc, bt, residual, out):
@@ -282,7 +315,8 @@
         jnp.where(y_even, block[:, 2:3], block[:, 3:4]),
     )
     at = iota((ROWS, 256), 1) // 8
-    out[...] = (jnp.where(at == which, theirs, 0.0) + jnp.where(at == 1, mine, 0.0)).astype(BF16)
+    home = 9 * sc[0] + 3 * sc[1] + 1
+    out[...] = (jnp.where(at == which, theirs, 0.0) + jnp.where(at == home, mine, 0.0)).astype(BF16)
 
 
 def line_kernel(sc, line, inverse, mat_ref, out):
@@ -316,10 +350,10 @@
 
 def advance_kernel(keep, take, sc, *refs):
     if keep:
-        res, modes, dual, own, ya, yb, xa, xb, old_dir, old_mul, dir_ref, mul_ref, val_ref, sa, sb, stack = refs
+        res, modes, dual, xa, xb, old_dir, old_mul, dir_ref, mul_ref, val_ref, sa, sb, stack = refs
     else:
-        res, modes, dual, own, ya, yb, xa, xb, dir_ref, val_ref, sa, sb, stack = refs
-    put(stack, 0, [own[...], ya[...], yb[...], xa[...], xb[...], jnp.zeros((40, 128), F32)])
+        res, modes, dual, xa, xb, dir_ref, val_ref, sa, sb, stack = refs
+    put(stack, 0, [xa[...], xb[...], jnp.zeros((40, 128), F32)])
     corrected = res[...] - dot_exact(modes[...], stack[...])
     if keep:
         direction = keep * old_dir[...] + take * corrected
@@ -331,13 +365,10 @@
     send_x(sc[0], (val_ref,), sa, sb, False)
 
 
-def cross(sc, values, sent, extra):
-    rows = bundle_rows(extra)
-    pair = [((rows, 128), F32)] * 2
-    x = exchange(*sent, "gx")
-    y = exchange(*call(functools.partial(route_y, extra), pair, sc, *values, *x, name="route_y"), "gy")
-    z = exchange(*call(functools.partial(route_z, extra), pair, sc, *values, *x, *y, name="route_z"), "gz")
-    return (*x, *y, *z)
+def label(sign, odd):
+    if sign == 0:
+        return odd
+    return 1 - odd if (sign == 1) != odd else 2
 
 
 def amplitude_blocks():
@@ -346,19 +377,23 @@
         for y_odd in (0, 1):
             for (o1, o2, o3), _, width in SLOTS:
                 at = OURS[(o1, o2, o3)]
-                lab1 = 0 if o1 == 0 else 1 + ((o1 == -1) ^ x_odd)
-                lab2 = 0 if o2 == 0 else 1 + ((o2 == -1) ^ y_odd)
-                out[at : at + width, 2 * x_odd + y_odd] = 3 * (3 * lab1 + lab2) + o3 + 1
+                block = 3 * (3 * label(o1, x_odd) + label(o2, y_odd)) + o3 + 1
+                out[at : at + width, 2 * x_odd + y_odd] = block
     return out
+
+
+def cross(sc, values, x, extra):
+    rows = bundle_rows(extra)
+    pair = [((rows, 128), F32)] * 2
+    y = exchange(*call(functools.partial(route_y, extra), pair, sc, *values, *x, name="route_y"), "gy")
+    z = exchange(*call(functools.partial(route_z, extra), pair, sc, *values, *x, *y, name="route_z"), "gz")
+    return (*x, *y, *z)
 
 
 def local(dual_blocks, load_terms, row_order, mode_rows, mode_count, coarse_inverse):
     line_length = lax.axis_size("gz")
     pos = [lax.axis_index(axis) for axis in ("gx", "gy", "gz")]
     sc = jnp.stack([p % 2 for p in pos] + [pos[2], mode_count[0, 0, 0]]).astype(jnp.int32)
-    packing = row_order[0, 0, 0]
-    order = jnp.concatenate([packing[begin : begin + width] for _, begin, width in SLOTS])
-    modes = jnp.pad(mode_rows[0, 0, 0].T, ((0, 16 - NMODE), (0, 0)))
     inverse = coarse_inverse[0, 0]
     bundle = [((BUNDLE, 128), F32)] * 2
     vector = ((ROWS, 128), F32)
@@ -366,18 +401,42 @@
     wide = [((bundle_rows(True), 128), F32)] * 2
     gathered = ((line_length, 8, 128), F32)
 
-    sel, inv, load_rows, comp, bt, cols, sa, sb = call(
+    sel, load_rows, comp, mode, order_row, sa, sb = pl.pallas_call(
         pack_kernel,
-        [square, square, vector, ((ROWS // GROUP, 128), F32), ((16, ROWS), BF16), ((ROWS, 16), BF16), *wide],
-        sc,
-        order[:, None],
-        order[None, :],
-        load_terms[0, 0, 0],
-        modes,
+        out_shape=[
+            jax.ShapeDtypeStruct(*v)
+            for v in (
+                square,
+                vector,
+                ((ROWS // GROUP, 128), F32),
+                ((16, ROWS), BF16),
+                ((1, ROWS), jnp.int32),
+                *wide,
+            )
+        ],
+        in_specs=[SMEM, VMEM, HBM, HBM],
+        out_specs=[VMEM] * 7,
+        scratch_shapes=[
+            pltpu.VMEM((ROWS, 1), jnp.int32),
+            pltpu.VMEM((ROWS, 128), BF16),
+            pltpu.VMEM((NMODE, ROWS), BF16),
+            pltpu.SemaphoreType.DMA((2,)),
+        ],
+        compiler_params=pltpu.CompilerParams(vmem_limit_bytes=16 * 2**20),
         name="pack",
-    )
-    (dual,) = call(permute_kernel, [square], sc, sel, inv, dual_blocks[0, 0, 0], name="permute")
-    received_rows = cross(sc, (load_rows, comp), (sa, sb), True)
+    )(sc, row_order[0, 0, 0][:, None], in_hbm(load_terms[0, 0, 0]), in_hbm(mode_rows[0, 0, 0].T))
+    x = exchange_async(sa, sb, "gx")
+    dual, inv, bt, cols = pl.pallas_call(
+        permute_kernel,
+        out_shape=[jax.ShapeDtypeStruct(*v) for v in (square, square, ((16, ROWS), BF16), ((ROWS, 16), BF16))],
+        in_specs=[VMEM, VMEM, VMEM, HBM],
+        out_specs=[VMEM] * 4,
+        scratch_shapes=[pltpu.VMEM((ROWS, ROWS), BF16), pltpu.SemaphoreType.DMA],
+        compiler_params=pltpu.CompilerParams(vmem_limit_bytes=16 * 2**20),
+        name="permute",
+    )(sel, mode, order_row, in_hbm(dual_blocks[0, 0, 0]))
+    *x, dual, inv, bt, cols = lax.optimization_barrier((*x, dual, inv, bt, cols))
+    received_rows = cross(sc, (load_rows, comp), x, True)
     residual, their_comp, proj = call(
         first_kernel,
         [vector, ((ROWS // GROUP, 128), F32), gathered],
@@ -401,10 +460,8 @@
             matrix, own = call(line_kernel, [((24, 8 * line_length), F32), amp], sc, line, inverse, name="line")
         else:
             (own,) = call(solve_kernel, [amp], sc, line, matrix, name="solve")
-        ya, yb = exchange(own, own, "gy")
-        column = jnp.concatenate([own, ya, yb], axis=0)
-        xa, xb = exchange(column, column, "gx")
-        near = (modes_near, dual, own, ya, yb, xa, xb)
+        column = jnp.concatenate(exchange(own, own, "gy"), axis=0)
+        near = (modes_near, dual, *exchange(column, column, "gx"))
         scratch = [pltpu.VMEM((256, 128), F32)]
         if iteration == 0:
             direction, value, sa, sb = call(
@@ -431,7 +488,7 @@
                 name="advance",
             )
             rho_prev = rho_now
-        received_rows = cross(sc, (value,), (sa, sb), False)
+        received_rows = cross(sc, (value,), exchange(sa, sb, "gx"), False)
         if iteration < ITERS - 1:
             residual, proj = call(
                 step_kernel, [vector, gathered], sc, residual, value, bt, *received_rows, name="step"

time: 257 us -> 230 us (0.89)
  the two profiles are of different devices: /device:TPU:87 before, /device:TPU:1 now
where the time goes in v2:
time: 230 us; the launch traced here: 229 us
  blocking collectives  144 us (63%)
  starting transfers between devices  41.2 us (18%)
  Pallas kernels  35.4 us (15%)
  local copies, waits for them, and re-layouts  5.92 us (3%)
    all_gather x17, blocking collectives, exchange(): lax.all_gather(first, axis, axis_index_groups=groups, tiled=True)  111 us
    ppermute x17, starting transfers between devices, exchange(): other = lax.ppermute(second, axis, swaps(size, 1))  35.5 us
    all_to_all x3, blocking collectives, local(): lax.all_to_all(proj, 'gz', 0, 0, tiled=True).reshape(8 * line_length, 128)  32.7 us
    pallas_call x20, Pallas kernels, call(): pl.pallas_call(kernel, out_shape=[jax.ShapeDtypeStruct(s, t) for s, t in...  24.2 us
    pallas_call x1, Pallas kernels, local(): pl.pallas_call(permute_kernel, out_shape=[jax.ShapeDtypeStruct(*v) for v...  6.72 us
    ppermute x1, starting transfers between devices, exchange_async(): lax.ppermute(first, axis, swaps(size, 0))  5.04 us
    unnamed x23, local copies, waits for them, and re-layouts  4.92 us
  transfers between devices with their start and end apart: 19, of which 2 were waited for; matrix products, arithmetic and copies ran while one was open for 1% of the time, Pallas kernels for 5%

profile of v2, /device:TPU:1, one launch (start us, length us, event | category | flops | bytes accessed | tf_op | source)
XLA Modules:
  0.0 228.9 jit_solution(12764008450121203419)
XLA Ops:
  2.3 4.5 %pack.1 = (bf16[1024,1024]{1,0:T(8,128)(2,1)S(1)}, f32[1024,128]{1,0:T(8,128)S(1)}, f32[128,128]{1,0:T(8,128)S(1)}, bf16[16,1024]{1,0:T(8,128)(2,1)S(1)}, s32[1,...) custom-call(s32[5]{0:T(128)S(1)} %stack.19.sc, s32[1024,1]{1,0:T(8,128)S(1)} %copy.10.order, ...), custom_call_target="tpu_custom_call" | custom-call | tf_op jit(solution)/shard_map/pack/pallas_call | solution.py:404
  6.8 5.0 %collective-permute-start = (f32[252,128]{1,0:T(8,128)S(1)}, f32[252,128]{1,0:T(8,128)S(1)}, u32[]{:S(2)}, u32[]{:S(2)}) collective-permute-start(f32[252,128]{1,0:T(8,128)S(1)} %get-tuple-element.57), channel_id=1, source_target_pairs={{0,128},{256,384},{128,0},{384,256},{1,129},{257,385},{129,1},{385... | collective-permute-start | bytes 387080 | tf_op jit(solution)/shard_map/ppermute | solution.py:68
  12.5 6.7 %permute.1 = (bf16[1024,1024]{1,0:T(8,128)(2,1)S(1)}, bf16[1024,1024]{1,0:T(8,128)(2,1)S(1)}, bf16[16,1024]{1,0:T(8,128)(2,1)S(1)}, bf16[1024,16]{1,0:T(8,128)(2,1)S(1)}) custom-call(bf16[1024,1024]{1,0:T(8,128)(2,1)S(1)} %get-tuple-element.59.sel, bf16[16,1024]{1,0:T(8,128)(2,1)S(1)} %get-tuple-element.60.mode, s32[1,1024]{1,0:T(1,128)S(1)} %get-tuple-element.61.order_row, ...), custom_call_target="tpu_custom_call" | custom-call | tf_op jit(solution)/shard_map/permute/pallas_call | solution.py:429
  22.5 8.5 %all-gather = f32[2,252,128]{2,1,0:T(8,128)} all-gather(f32[1,252,128]{2,1,0:T(8,128)S(1)} %bitcast.24), channel_id=1, replica_groups={{0,16},{32,48},{64,80},{96,112},{1,17},{33,49},{65,81},{97,113},{2,18},..., dimensions={0}, use_global_device_ids=true | all-gather | bytes 387072 | tf_op jit(solution)/shard_map/all_gather | solution.py:63
  33.3 5.1 %collective-permute-start.3 = (f32[252,128]{1,0:T(8,128)}, f32[252,128]{1,0:T(8,128)}, u32[]{:S(2)}, u32[]{:S(2)}) collective-permute-start(f32[252,128]{1,0:T(8,128)} %get-tuple-element.75), channel_id=1, source_target_pairs={{1,2},{3,4},{5,6},{7,8},{9,10},{11,12},{13,14},{2,1},{4,3},{6,5},{... | collective-permute-start | bytes 387080 | tf_op jit(solution)/shard_map/ppermute | solution.py:62
  43.5 11.4 %all_to_all.15 = f32[16,8,128]{2,1,0:T(8,128)S(1)} all-to-all(f32[16,8,128]{2,1,0:T(8,128)S(1)} %get-tuple-element.80), channel_id=1, replica_groups=mesh['gx'=4,'gy'=8,'gz'=16] {'gz'}, dimensions={0} | all-to-all | bytes 131072 | tf_op jit(solution)/shard_map/all_to_all | solution.py:458
  57.9 8.4 %all_gather.53 = f32[48,128]{1,0:T(8,128)S(1)} all-gather(f32[24,128]{1,0:T(8,128)S(1)} %get-tuple-element.81), channel_id=1, replica_groups={{0,16},{32,48},{64,80},{96,112},{1,17},{33,49},{65,81},{97,113},{2,18},..., dimensions={0}, use_global_device_ids=true | all-gather | bytes 36864 | tf_op jit(solution)/shard_map/all_gather | solution.py:63
  68.2 9.8 %all_gather.54.refs_3_ = f32[144,128]{1,0:T(8,128)S(1)} all-gather(f32[72,128]{1,0:T(8,128)S(1)} %constant_dynamic-update-slice_fusion), channel_id=1, replica_groups={{0,128},{256,384},{1,129},{257,385},{2,130},{258,386},{3,131},{259,387}..., dimensions={0}, use_global_device_ids=true | all-gather | bytes 110592 | tf_op jit(solution)/shard_map/all_gather | solution.py:63
  80.7 9.5 %all_gather.55.refs_1_.xa = f32[448,128]{1,0:T(8,128)S(1)} all-gather(f32[224,128]{1,0:T(8,128)S(1)} %get-tuple-element.83), channel_id=1, replica_groups={{0,128},{256,384},{1,129},{257,385},{2,130},{258,386},{3,131},{259,387}..., dimensions={0}, use_global_device_ids=true | all-gather | bytes 344064 | tf_op jit(solution)/shard_map/all_gather | solution.py:63
  91.4 6.5 %all_gather.56.refs_3_.ya = f32[448,128]{1,0:T(8,128)S(1)} all-gather(f32[224,128]{1,0:T(8,128)S(1)} %get-tuple-element.85), channel_id=1, replica_groups={{0,16},{32,48},{64,80},{96,112},{1,17},{33,49},{65,81},{97,113},{2,18},..., dimensions={0}, use_global_device_ids=true | all-gather | bytes 344064 | tf_op jit(solution)/shard_map/all_gather | solution.py:63
  98.5 7.4 %collective-permute-start.8 = (f32[224,128]{1,0:T(8,128)S(1)}, f32[224,128]{1,0:T(8,128)S(1)}, u32[]{:S(2)}, u32[]{:S(2)}) collective-permute-start(f32[224,128]{1,0:T(8,128)S(1)} %get-tuple-element.88), channel_id=1, source_target_pairs={{1,2},{3,4},{5,6},{7,8},{9,10},{11,12},{13,14},{2,1},{4,3},{6,5},{... | collective-permute-start | bytes 344072 | tf_op jit(solution)/shard_map/ppermute | solution.py:62
  109.2 10.2 %all_to_all.16 = f32[16,8,128]{2,1,0:T(8,128)S(1)} all-to-all(f32[16,8,128]{2,1,0:T(8,128)S(1)} %get-tuple-element.90), channel_id=1, replica_groups=mesh['gx'=4,'gy'=8,'gz'=16] {'gz'}, dimensions={0} | all-to-all | bytes 131072 | tf_op jit(solution)/shard_map/all_to_all | solution.py:458
  120.8 7.7 %all_gather.58 = f32[48,128]{1,0:T(8,128)S(1)} all-gather(f32[24,128]{1,0:T(8,128)S(1)} %solve.2), channel_id=1, replica_groups={{0,16},{32,48},{64,80},{96,112},{1,17},{33,49},{65,81},{97,113},{2,18},..., dimensions={0}, use_global_device_ids=true | all-gather | bytes 36864 | tf_op jit(solution)/shard_map/all_gather | solution.py:63
  129.2 6.5 %all_gather.59.refs_3_ = f32[144,128]{1,0:T(8,128)S(1)} all-gather(f32[72,128]{1,0:T(8,128)S(1)} %constant_dynamic-update-slice_fusion.2), channel_id=1, replica_groups={{0,128},{256,384},{1,129},{257,385},{2,130},{258,386},{3,131},{259,387}..., dimensions={0}, use_global_device_ids=true | all-gather | bytes 110592 | tf_op jit(solution)/shard_map/all_gather | solution.py:63
  138.5 9.8 %all_gather.60.refs_1_.xa = f32[448,128]{1,0:T(8,128)S(1)} all-gather(f32[224,128]{1,0:T(8,128)S(1)} %get-tuple-element.94), channel_id=1, replica_groups={{0,128},{256,384},{1,129},{257,385},{2,130},{258,386},{3,131},{259,387}..., dimensions={0}, use_global_device_ids=true | all-gather | bytes 344064 | tf_op jit(solution)/shard_map/all_gather | solution.py:63
  149.5 6.5 %all_gather.61.refs_3_.ya = f32[448,128]{1,0:T(8,128)S(1)} all-gather(f32[224,128]{1,0:T(8,128)S(1)} %get-tuple-element.96), channel_id=1, replica_groups={{0,16},{32,48},{64,80},{96,112},{1,17},{33,49},{65,81},{97,113},{2,18},..., dimensions={0}, use_global_device_ids=true | all-gather | bytes 344064 | tf_op jit(solution)/shard_map/all_gather | solution.py:63
  156.6 7.1 %collective-permute-start.13 = (f32[224,128]{1,0:T(8,128)S(1)}, f32[224,128]{1,0:T(8,128)S(1)}, u32[]{:S(2)}, u32[]{:S(2)}) collective-permute-start(f32[224,128]{1,0:T(8,128)S(1)} %get-tuple-element.99), channel_id=1, source_target_pairs={{1,2},{3,4},{5,6},{7,8},{9,10},{11,12},{13,14},{2,1},{4,3},{6,5},{... | collective-permute-start | bytes 344072 | tf_op jit(solution)/shard_map/ppermute | solution.py:62
  167.0 11.1 %all_to_all.17 = f32[16,8,128]{2,1,0:T(8,128)S(1)} all-to-all(f32[16,8,128]{2,1,0:T(8,128)S(1)} %get-tuple-element.101), channel_id=1, replica_groups=mesh['gx'=4,'gy'=8,'gz'=16] {'gz'}, dimensions={0} | all-to-all | bytes 131072 | tf_op jit(solution)/shard_map/all_to_all | solution.py:458
  179.5 6.8 %all_gather.63 = f32[48,128]{1,0:T(8,128)S(1)} all-gather(f32[24,128]{1,0:T(8,128)S(1)} %solve.3), channel_id=1, replica_groups={{0,16},{32,48},{64,80},{96,112},{1,17},{33,49},{65,81},{97,113},{2,18},..., dimensions={0}, use_global_device_ids=true | all-gather | bytes 36864 | tf_op jit(solution)/shard_map/all_gather | solution.py:63
  187.0 6.5 %all_gather.64.refs_3_ = f32[144,128]{1,0:T(8,128)S(1)} all-gather(f32[72,128]{1,0:T(8,128)S(1)} %constant_dynamic-update-slice_fusion.4), channel_id=1, replica_groups={{0,128},{256,384},{1,129},{257,385},{2,130},{258,386},{3,131},{259,387}..., dimensions={0}, use_global_device_ids=true | all-gather | bytes 110592 | tf_op jit(solution)/shard_map/all_gather | solution.py:63
  196.4 9.8 %all_gather.65.refs_1_.xa = f32[448,128]{1,0:T(8,128)S(1)} all-gather(f32[224,128]{1,0:T(8,128)S(1)} %get-tuple-element.106), channel_id=1, replica_groups={{0,128},{256,384},{1,129},{257,385},{2,130},{258,386},{3,131},{259,387}..., dimensions={0}, use_global_device_ids=true | all-gather | bytes 344064 | tf_op jit(solution)/shard_map/all_gather | solution.py:63
  207.5 6.5 %all_gather.66.refs_3_.ya = f32[448,128]{1,0:T(8,128)S(1)} all-gather(f32[224,128]{1,0:T(8,128)S(1)} %get-tuple-element.108), channel_id=1, replica_groups={{0,16},{32,48},{64,80},{96,112},{1,17},{33,49},{65,81},{97,113},{2,18},..., dimensions={0}, use_global_device_ids=true | all-gather | bytes 344064 | tf_op jit(solution)/shard_map/all_gather | solution.py:63
  214.6 7.1 %collective-permute-start.18 = (f32[224,128]{1,0:T(8,128)S(1)}, f32[224,128]{1,0:T(8,128)S(1)}, u32[]{:S(2)}, u32[]{:S(2)}) collective-permute-start(f32[224,128]{1,0:T(8,128)S(1)} %get-tuple-element.111), channel_id=1, source_target_pairs={{1,2},{3,4},{5,6},{7,8},{9,10},{11,12},{13,14},{2,1},{4,3},{6,5},{... | collective-permute-start | bytes 344072 | tf_op jit(solution)/shard_map/ppermute | solution.py:62
  226.3 2.6 %last.1 = f32[1024,128]{1,0:T(8,128)} custom-call(s32[5]{0:T(128)S(1)} %stack.19.sc, f32[1024,128]{1,0:T(8,128)S(1)} %get-tuple-element.100.refs_0_.res, f32[1024,128]{1,0:T(8,128)S(1)} %get-tuple-element.105.refs_0_.val, bf16[1024,1024]{1,0:T(8,128)(2,1)S(1)} %copy-done.1, f32[448,128]{1,0:T(8,128)S(1)} %all_gather.65.refs_1_.xa, ...), custom_call_target="tpu_custom_call" | custom-call | tf_op jit(solution)/shard_map/last/pallas_call | solution.py:77
  (84 shorter events, 46.0 us)
Async XLA Ops:
  6.8 13.8 %collective-permute-start = (f32[252,128]{1,0:T(8,128)S(1)}, f32[252,128]{1,0:T(8,128)S(1)}, u32[]{:S(2)}, u32[]{:S(2)}) collective-permute-start(f32[252,128]{1,0:T(8,128)S(1)} %get-tuple-element.57), channel_id=1, source_target_pairs={{0,128},{256,384},{128,0},{384,256},{1,129},{257,385},{129,1},{385... | collective-permute-start | bytes 387080 | tf_op jit(solution)/shard_map/ppermute | solution.py:68
  11.8 8.8 %collective-permute-start.1 = (f32[252,128]{1,0:T(8,128)S(1)}, f32[252,128]{1,0:T(8,128)S(1)}, u32[]{:S(2)}, u32[]{:S(2)}) collective-permute-start(f32[252,128]{1,0:T(8,128)S(1)} %get-tuple-element.58), channel_id=1, source_target_pairs={{128,256},{256,128},{129,257},{257,129},{130,258},{258,130},{131,2... | collective-permute-start | bytes 387080 | tf_op jit(solution)/shard_map/ppermute | solution.py:68
  20.6 1.9 copy-start.6
  21.8 10.2 %collective-permute-start.2 = (f32[252,128]{1,0:T(8,128)}, f32[252,128]{1,0:T(8,128)S(1)}, u32[]{:S(2)}, u32[]{:S(2)}) collective-permute-start(f32[252,128]{1,0:T(8,128)} %get-tuple-element.73), channel_id=1, source_target_pairs={{16,32},{48,64},{80,96},{32,16},{64,48},{96,80},{17,33},{49,65},{8... | collective-permute-start | bytes 387080 | tf_op jit(solution)/shard_map/ppermute | solution.py:62
  33.3 8.2 %collective-permute-start.3 = (f32[252,128]{1,0:T(8,128)}, f32[252,128]{1,0:T(8,128)}, u32[]{:S(2)}, u32[]{:S(2)}) collective-permute-start(f32[252,128]{1,0:T(8,128)} %get-tuple-element.75), channel_id=1, source_target_pairs={{1,2},{3,4},{5,6},{7,8},{9,10},{11,12},{13,14},{2,1},{4,3},{6,5},{... | collective-permute-start | bytes 387080 | tf_op jit(solution)/shard_map/ppermute | solution.py:62
  41.5 25.6 %copy-start.2 = (s32[1024,4]{1,0:T(8,128)S(1)}, s32[1024,4]{1,0:T(8,128)}, u32[]{:S(2)}) copy-start(s32[1024,4]{1,0:T(8,128)} %constant.37.clone.block) | copy-start | bytes 49156
  42.3 24.7 %copy-start.7 = (bf16[1024,16]{1,0:T(8,128)(2,1)S(1)}, bf16[1024,16]{1,0:T(8,128)(2,1)}, u32[]{:S(2)}) copy-start(bf16[1024,16]{1,0:T(8,128)(2,1)} %copy-done.6) | copy-start | bytes 98308
  57.3 9.1 %collective-permute-start.4 = (f32[24,128]{1,0:T(8,128)S(1)}, f32[24,128]{1,0:T(8,128)S(1)}, u32[]{:S(2)}, u32[]{:S(2)}) collective-permute-start(f32[24,128]{1,0:T(8,128)S(1)} %get-tuple-element.81), channel_id=1, source_target_pairs={{16,32},{48,64},{80,96},{32,16},{64,48},{96,80},{17,33},{49,65},{8... | collective-permute-start | bytes 36872 | tf_op jit(solution)/shard_map/ppermute | solution.py:62
  66.4 11.6 %collective-permute-start.5 = (f32[72,128]{1,0:T(8,128)S(1)}, f32[72,128]{1,0:T(8,128)S(1)}, u32[]{:S(2)}, u32[]{:S(2)}) collective-permute-start(f32[72,128]{1,0:T(8,128)S(1)} %constant_dynamic-update-slice_fusion), channel_id=1, source_target_pairs={{128,256},{256,128},{129,257},{257,129},{130,258},{258,130},{131,2... | collective-permute-start | bytes 110600 | tf_op jit(solution)/shard_map/ppermute | solution.py:62
  80.0 28.4 %copy-start.5 = (bf16[16,1024]{1,0:T(8,128)(2,1)S(1)}, bf16[16,1024]{1,0:T(8,128)(2,1)}, u32[]{:S(2)}) copy-start(bf16[16,1024]{1,0:T(8,128)(2,1)} %copy-done.3) | copy-start | bytes 98308
  80.0 10.2 %collective-permute-start.6 = (f32[224,128]{1,0:T(8,128)S(1)}, f32[224,128]{1,0:T(8,128)S(1)}, u32[]{:S(2)}, u32[]{:S(2)}) collective-permute-start(f32[224,128]{1,0:T(8,128)S(1)} %get-tuple-element.84), channel_id=1, source_target_pairs={{128,256},{256,128},{129,257},{257,129},{130,258},{258,130},{131,2... | collective-permute-start | bytes 344072 | tf_op jit(solution)/shard_map/ppermute | solution.py:62
  90.8 7.1 %collective-permute-start.7 = (f32[224,128]{1,0:T(8,128)S(1)}, f32[224,128]{1,0:T(8,128)S(1)}, u32[]{:S(2)}, u32[]{:S(2)}) collective-permute-start(f32[224,128]{1,0:T(8,128)S(1)} %get-tuple-element.86), channel_id=1, source_target_pairs={{16,32},{48,64},{80,96},{32,16},{64,48},{96,80},{17,33},{49,65},{8... | collective-permute-start | bytes 344072 | tf_op jit(solution)/shard_map/ppermute | solution.py:62
  98.5 9.9 %collective-permute-start.8 = (f32[224,128]{1,0:T(8,128)S(1)}, f32[224,128]{1,0:T(8,128)S(1)}, u32[]{:S(2)}, u32[]{:S(2)}) collective-permute-start(f32[224,128]{1,0:T(8,128)S(1)} %get-tuple-element.88), channel_id=1, source_target_pairs={{1,2},{3,4},{5,6},{7,8},{9,10},{11,12},{13,14},{2,1},{4,3},{6,5},{... | collective-permute-start | bytes 344072 | tf_op jit(solution)/shard_map/ppermute | solution.py:62
  120.2 8.4 %collective-permute-start.9 = (f32[24,128]{1,0:T(8,128)S(1)}, f32[24,128]{1,0:T(8,128)S(1)}, u32[]{:S(2)}, u32[]{:S(2)}) collective-permute-start(f32[24,128]{1,0:T(8,128)S(1)} %solve.2), channel_id=1, source_target_pairs={{16,32},{48,64},{80,96},{32,16},{64,48},{96,80},{17,33},{49,65},{8... | collective-permute-start | bytes 36872 | tf_op jit(solution)/shard_map/ppermute | solution.py:62
  128.5 7.2 %collective-permute-start.10 = (f32[72,128]{1,0:T(8,128)S(1)}, f32[72,128]{1,0:T(8,128)S(1)}, u32[]{:S(2)}, u32[]{:S(2)}) collective-permute-start(f32[72,128]{1,0:T(8,128)S(1)} %constant_dynamic-update-slice_fusion.2), channel_id=1, source_target_pairs={{128,256},{256,128},{129,257},{257,129},{130,258},{258,130},{131,2... | collective-permute-start | bytes 110600 | tf_op jit(solution)/shard_map/ppermute | solution.py:62
  137.8 10.5 %collective-permute-start.11 = (f32[224,128]{1,0:T(8,128)S(1)}, f32[224,128]{1,0:T(8,128)S(1)}, u32[]{:S(2)}, u32[]{:S(2)}) collective-permute-start(f32[224,128]{1,0:T(8,128)S(1)} %get-tuple-element.95), channel_id=1, source_target_pairs={{128,256},{256,128},{129,257},{257,129},{130,258},{258,130},{131,2... | collective-permute-start | bytes 344072 | tf_op jit(solution)/shard_map/ppermute | solution.py:62
  148.9 7.2 %collective-permute-start.12 = (f32[224,128]{1,0:T(8,128)S(1)}, f32[224,128]{1,0:T(8,128)S(1)}, u32[]{:S(2)}, u32[]{:S(2)}) collective-permute-start(f32[224,128]{1,0:T(8,128)S(1)} %get-tuple-element.97), channel_id=1, source_target_pairs={{16,32},{48,64},{80,96},{32,16},{64,48},{96,80},{17,33},{49,65},{8... | collective-permute-start | bytes 344072 | tf_op jit(solution)/shard_map/ppermute | solution.py:62
  156.6 9.6 %collective-permute-start.13 = (f32[224,128]{1,0:T(8,128)S(1)}, f32[224,128]{1,0:T(8,128)S(1)}, u32[]{:S(2)}, u32[]{:S(2)}) collective-permute-start(f32[224,128]{1,0:T(8,128)S(1)} %get-tuple-element.99), channel_id=1, source_target_pairs={{1,2},{3,4},{5,6},{7,8},{9,10},{11,12},{13,14},{2,1},{4,3},{6,5},{... | collective-permute-start | bytes 344072 | tf_op jit(solution)/shard_map/ppermute | solution.py:62
  178.9 7.5 %collective-permute-start.14 = (f32[24,128]{1,0:T(8,128)S(1)}, f32[24,128]{1,0:T(8,128)S(1)}, u32[]{:S(2)}, u32[]{:S(2)}) collective-permute-start(f32[24,128]{1,0:T(8,128)S(1)} %solve.3), channel_id=1, source_target_pairs={{16,32},{48,64},{80,96},{32,16},{64,48},{96,80},{17,33},{49,65},{8... | collective-permute-start | bytes 36872 | tf_op jit(solution)/shard_map/ppermute | solution.py:62
  186.4 7.2 %collective-permute-start.15 = (f32[72,128]{1,0:T(8,128)S(1)}, f32[72,128]{1,0:T(8,128)S(1)}, u32[]{:S(2)}, u32[]{:S(2)}) collective-permute-start(f32[72,128]{1,0:T(8,128)S(1)} %constant_dynamic-update-slice_fusion.4), channel_id=1, source_target_pairs={{128,256},{256,128},{129,257},{257,129},{130,258},{258,130},{131,2... | collective-permute-start | bytes 110600 | tf_op jit(solution)/shard_map/ppermute | solution.py:62
  195.6 26.1 %copy-start.1 = (bf16[1024,1024]{1,0:T(8,128)(2,1)S(1)}, bf16[1024,1024]{1,0:T(8,128)(2,1)}, u32[]{:S(2)}) copy-start(bf16[1024,1024]{1,0:T(8,128)(2,1)} %copy-done) | copy-start | bytes 6291460
  195.6 10.6 %collective-permute-start.16 = (f32[224,128]{1,0:T(8,128)S(1)}, f32[224,128]{1,0:T(8,128)S(1)}, u32[]{:S(2)}, u32[]{:S(2)}) collective-permute-start(f32[224,128]{1,0:T(8,128)S(1)} %get-tuple-element.107), channel_id=1, source_target_pairs={{128,256},{256,128},{129,257},{257,129},{130,258},{258,130},{131,2... | collective-permute-start | bytes 344072 | tf_op jit(solution)/shard_map/ppermute | solution.py:62
  206.9 7.2 %collective-permute-start.17 = (f32[224,128]{1,0:T(8,128)S(1)}, f32[224,128]{1,0:T(8,128)S(1)}, u32[]{:S(2)}, u32[]{:S(2)}) collective-permute-start(f32[224,128]{1,0:T(8,128)S(1)} %get-tuple-element.109), channel_id=1, source_target_pairs={{16,32},{48,64},{80,96},{32,16},{64,48},{96,80},{17,33},{49,65},{8... | collective-permute-start | bytes 344072 | tf_op jit(solution)/shard_map/ppermute | solution.py:62
  214.6 11.7 %collective-permute-start.18 = (f32[224,128]{1,0:T(8,128)S(1)}, f32[224,128]{1,0:T(8,128)S(1)}, u32[]{:S(2)}, u32[]{:S(2)}) collective-permute-start(f32[224,128]{1,0:T(8,128)S(1)} %get-tuple-element.111), channel_id=1, source_target_pairs={{1,2},{3,4},{5,6},{7,8},{9,10},{11,12},{13,14},{2,1},{4,3},{6,5},{... | collective-permute-start | bytes 344072 | tf_op jit(solution)/shard_map/ppermute | solution.py:62
  (4 other events, 4.9 us)

commit v3 on v2

--- a/solution.py
+++ b/solution.py
@@ -23,6 +23,8 @@
 WIDTHS = {1: FACE, 2: EDGE, 3: CORNER}
 
 BUNDLE = 224
+NEAR = 32
+STACK = 16 * NEAR
 GROUP = 8
 
 
@@ -89,13 +91,6 @@
     return pltpu.with_memory_space_constraint(x, pltpu.HBM)
 
 
-def split3(x):
-    high = x.astype(BF16)
-    rest = x - high.astype(F32)
-    mid = rest.astype(BF16)
-    return high, mid, (rest - mid.astype(F32)).astype(BF16)
-
-
 def dot(a, b):
     return jnp.dot(a, b, preferred_element_type=F32)
 
@@ -104,10 +99,12 @@
     return lax.dot_general(a, b, (((1,), (1,)), ((), ())), preferred_element_type=F32)
 
 
-def dot_exact(a, x):
-    out = dot(a, jnp.concatenate(split3(x), axis=1))
+def dot_wide(a, x):
+    high = x.astype(BF16)
+    low = (x - high.astype(F32)).astype(BF16)
+    out = dot(a, jnp.concatenate([high, low], axis=1))
     width = x.shape[1]
-    return out[:, 0:width] + out[:, width : 2 * width] + out[:, 2 * width :]
+    return out[:, 0:width] + out[:, width:]
 
 
 def iota(shape, dim):
@@ -119,7 +116,7 @@
 
 
 def bundle_rows(extra):
-    return BUNDLE + BUNDLE // GROUP if extra else BUNDLE
+    return BUNDLE + 32 if extra else BUNDLE
 
 
 def put(ref, at, pieces):
@@ -151,7 +148,14 @@
     return up, down
 
 
+def blank(extra, *refs):
+    if extra:
+        for ref in refs:
+            ref[bundle_rows(extra) - 8 :, :] = jnp.zeros((8, 128), F32)
+
+
 def send_x(parity, values, send_a, send_b, extra):
+    blank(extra, send_a, send_b)
     for value, (scale, base) in zip(values, layers(extra)):
         width = BUNDLE // scale
         put_pair(send_a, send_b, base, parity, [value[0:width, :]], [value[width : 2 * width, :]])
@@ -160,6 +164,7 @@
 def route_y(extra, sc, *refs):
     count = 2 if extra else 1
     values, (xa, xb, ya, yb) = refs[:count], refs[count:]
+    blank(extra, ya, yb)
     for value, (scale, base) in zip(values, layers(extra)):
         up, down = received(xa, xb, sc[0], scale, base)
         plus = [up(0, 32), down(0, 32), value[448 // scale : 608 // scale, :]]
@@ -170,6 +175,7 @@
 def route_z(extra, sc, *refs):
     count = 2 if extra else 1
     values, (xa, xb, ya, yb, za, zb) = refs[:count], refs[count:]
+    blank(extra, za, zb)
     for value, (scale, base) in zip(values, layers(extra)):
         x_up, x_down = received(xa, xb, sc[0], scale, base)
         y_up, y_down = received(ya, yb, sc[1], scale, base)
@@ -210,7 +216,7 @@
     return pieces
 
 
-def pack_kernel(sc, order, load, modes, sel_ref, load_ref, comp_ref, mode, row_ref, xa, xb, col, buf, mbuf, sems):
+def pack_kernel(sc, order, load, modes, sel_ref, load_ref, comp_ref, mode, cols_ref, xa, xb, col, buf, mbuf, sems):
     copy = pltpu.make_async_copy(load, buf, sems.at[0])
     copy.start()
     copy_modes = pltpu.make_async_copy(modes, mbuf, sems.at[1])
@@ -221,15 +227,12 @@
     for at in range(0, ROWS, step):
         lanes = iota((step, ROWS), 1)
         sel_ref[at : at + step, :] = jnp.where(col[at : at + step, :] == lanes, 1.0, 0.0).astype(BF16)
-    lane = iota((8, ROWS), 1)
-    digits = jnp.where(iota((8, ROWS), 0) == 0, lane // 256, jnp.where(iota((8, ROWS), 0) == 1, lane % 256, 0))
     copy_modes.wait()
-    top = jnp.concatenate([mbuf[...].astype(F32), jnp.zeros((8 - NMODE, ROWS), F32)], axis=0)
-    mode[...] = jnp.concatenate([top, digits.astype(F32)], axis=0).astype(BF16)
+    top = jnp.concatenate([mbuf[...].astype(F32), jnp.zeros((16 - NMODE, ROWS), F32)], axis=0)
+    mode[...] = top.astype(BF16)
     sel = sel_ref[...]
-    rows = dot_t(mode[...], sel)
-    row_ref[...] = (rows[8:9, :] * 256.0 + rows[9:10, :]).astype(jnp.int32)
     cols = dot_t(sel, mode[...]).astype(BF16)
+    cols_ref[...] = cols
     spread = jnp.where(iota((16, 128), 0) == iota((16, 128), 1) % 16, 1.0, 0.0).astype(BF16)
     wide = dot(cols, spread)
     keep = iota((ROWS, 128), 0) % GROUP == iota((ROWS, 128), 1) // 16
@@ -241,23 +244,30 @@
     send_x(sc[0], (load_ref, comp_ref), xa, xb, True)
 
 
-def permute_kernel(sel, mode, order_row, dual, out, inv_ref, bt_ref, cols_ref, buf, sem):
+def permute_kernel(sel, mode, order_row, dual, out, inv_ref, bt_ref, buf, sem):
     copy = pltpu.make_async_copy(dual, buf, sem)
     copy.start()
+    packed = jnp.concatenate([order_row[:, begin : begin + width] for _, begin, width in SLOTS], axis=1)
     step = 256
     for at in range(0, ROWS, step):
         subs = iota((step, ROWS), 0) + at
-        inv_ref[at : at + step, :] = jnp.where(order_row[...] == subs, 1.0, 0.0).astype(BF16)
+        inv_ref[at : at + step, :] = jnp.where(packed == subs, 1.0, 0.0).astype(BF16)
     bt_ref[...] = dot(mode[...], inv_ref[...]).astype(BF16)
-    cols_ref[...] = dot_t(sel[...], mode[...]).astype(BF16)
     copy.wait()
-    for at in range(0, ROWS, step):
+    for at in range(0, out.shape[0], step):
         rows = dot(sel[at : at + step, :], buf[...]).astype(BF16)
         out[at : at + step, :] = dot(rows, inv_ref[...]).astype(BF16)
 
 
+def permute_rest_kernel(first, sel, inv, dual, out):
+    step = 256
+    for at in range(0, out.shape[0], step):
+        rows = dot(sel[first + at : first + at + step, :], dual[...]).astype(BF16)
+        out[at : at + step, :] = dot(rows, inv[...]).astype(BF16)
+
+
 def project(sc, bt, residual, out):
-    block = dot_exact(bt[...], residual)[0:8, :]
+    block = dot_wide(bt[...], residual)[0:8, :]
     count = sc[4].astype(F32)
     block = jnp.where(iota((8, 128), 0) == NMODE, count, block)
     for t in range(out.shape[0]):
@@ -290,11 +300,11 @@
 
 def last_kernel(sc, res, val, inv, xa, xb, ya, yb, za, zb, out, scratch):
     next_residual(sc, res, val, (xa, xb, ya, yb, za, zb), scratch)
-    out[...] = dot_exact(inv[...], scratch[...])
+    out[...] = dot_wide(inv[...], scratch[...])
 
 
 def unpack_kernel(sc, inv, val, out):
-    out[...] = dot_exact(inv[...], val[...])
+    out[...] = dot_wide(inv[...], val[...])
 
 
 def mode_kernel(sc, cols, comp, block, out):
@@ -302,11 +312,11 @@
     wide = dot(pick, comp[...].astype(BF16))
     keep = iota((ROWS, 128), 0) % GROUP == iota((ROWS, 128), 1) // 16
     wide = jnp.where(keep, wide, 0.0).astype(BF16)
-    mode = iota((128, 256), 0) % 16
-    fold = jnp.where((mode == iota((128, 256), 1) % 8) & (mode < NMODE), 1.0, 0.0).astype(BF16)
+    mode = iota((128, STACK), 0) % 16
+    fold = jnp.where((mode == iota((128, STACK), 1) % 8) & (mode < NMODE), 1.0, 0.0).astype(BF16)
     theirs = dot(wide, fold)
-    mode = iota((16, 256), 0)
-    own = jnp.where((mode == iota((16, 256), 1) % 8) & (mode < NMODE), 1.0, 0.0).astype(BF16)
+    mode = iota((16, STACK), 0)
+    own = jnp.where((mode == iota((16, STACK), 1) % 8) & (mode < NMODE), 1.0, 0.0).astype(BF16)
     mine = dot(cols[...], own)
     x_even, y_even = sc[0] == 0, sc[1] == 0
     which = jnp.where(
@@ -314,12 +324,15 @@
         jnp.where(y_even, block[:, 0:1], block[:, 1:2]),
         jnp.where(y_even, block[:, 2:3], block[:, 3:4]),
     )
-    at = iota((ROWS, 256), 1) // 8
-    home = 9 * sc[0] + 3 * sc[1] + 1
+    which = which + sc[2]
+    at = iota((ROWS, STACK), 1) // 8
+    home = 16 * sc[0] + 4 * sc[1] + 1 + sc[2]
     out[...] = (jnp.where(at == which, theirs, 0.0) + jnp.where(at == home, mine, 0.0)).astype(BF16)
 
 
-def line_kernel(sc, line, inverse, mat_ref, out):
+def line_kernel(sc, line, inverse, mat_ref, out, buf, sem):
+    copy = pltpu.make_async_copy(inverse, buf, sem)
+    copy.start()
     everyone = line[...]
     size, coarse = everyone.shape[0], inverse.shape[0]
 
@@ -337,8 +350,9 @@
         return jnp.where(hit, 1.0, 0.0)[:, 0:coarse]
 
     everywhere = selection(size, 0)
-    near = selection(24, 8 * sc[3] - 8)
-    rows = jnp.dot(near, inverse[...], precision=HIGHEST, preferred_element_type=F32)
+    near = selection(NEAR, 8 * (sc[3] - sc[2]) - 8)
+    copy.wait()
+    rows = jnp.dot(near, buf[...], precision=HIGHEST, preferred_element_type=F32)
     matrix = lax.dot_general(rows, everywhere, (((1,), (1,)), ((), ())), precision=HIGHEST, preferred_element_type=F32)
     mat_ref[...] = matrix
     out[...] = jnp.dot(matrix, everyone, precision=HIGHEST, preferred_element_type=F32)
@@ -350,25 +364,39 @@
 
 def advance_kernel(keep, take, sc, *refs):
     if keep:
-        res, modes, dual, xa, xb, old_dir, old_mul, dir_ref, mul_ref, val_ref, sa, sb, stack = refs
+        res, modes, dual_a, dual_b, stack, old_dir, old_mul, dir_ref, mul_ref, val_ref, sa, sb = refs
     else:
-        res, modes, dual, xa, xb, dir_ref, val_ref, sa, sb, stack = refs
-    put(stack, 0, [xa[...], xb[...], jnp.zeros((40, 128), F32)])
-    corrected = res[...] - dot_exact(modes[...], stack[...])
+        res, modes, dual_a, dual_b, stack, dir_ref, val_ref, sa, sb = refs
+    corrected = res[...] - dot_wide(modes[...], stack[...])
     if keep:
         direction = keep * old_dir[...] + take * corrected
         mul_ref[...] = old_mul[...] + direction
     else:
         direction = corrected / take
     dir_ref[...] = direction
-    val_ref[...] = dot(dual[...], direction.astype(BF16))
+    rounded = direction.astype(BF16)
+    val_ref[0 : ROWS // 2, :] = dot(dual_a[...], rounded)
+    val_ref[ROWS // 2 :, :] = dot(dual_b[...], rounded)
     send_x(sc[0], (val_ref,), sa, sb, False)
+
+
+def share(block, axis):
+    size, line = lax.axis_size(axis), lax.axis_size("gz")
+    groups = []
+    for z in range(line):
+        for even in range(0, size, 2):
+            odd = (even + 1 if z % 2 == 0 else even - 1) % size
+            groups.append([even * line + z, odd * line + z])
+    block = lax.all_gather(block, (axis, "gz"), axis_index_groups=groups, tiled=True)
+    return lax.all_gather(block, "gz", axis_index_groups=[[z, z + 1] for z in range(0, line, 2)], tiled=True)
 
 
 def label(sign, odd):
     if sign == 0:
         return odd
-    return 1 - odd if (sign == 1) != odd else 2
+    if odd:
+        return 2 if sign == 1 else 0
+    return 1 if sign == 1 else 3
 
 
 def amplitude_blocks():
@@ -377,16 +405,15 @@
         for y_odd in (0, 1):
             for (o1, o2, o3), _, width in SLOTS:
                 at = OURS[(o1, o2, o3)]
-                block = 3 * (3 * label(o1, x_odd) + label(o2, y_odd)) + o3 + 1
+                block = 4 * (4 * label(o1, x_odd) + label(o2, y_odd)) + o3 + 1
                 out[at : at + width, 2 * x_odd + y_odd] = block
     return out
 
 
-def cross(sc, values, x, extra):
-    rows = bundle_rows(extra)
-    pair = [((rows, 128), F32)] * 2
-    y = exchange(*call(functools.partial(route_y, extra), pair, sc, *values, *x, name="route_y"), "gy")
-    z = exchange(*call(functools.partial(route_z, extra), pair, sc, *values, *x, *y, name="route_z"), "gz")
+def cross(sc, value, x):
+    pair = [((BUNDLE, 128), F32)] * 2
+    y = exchange(*call(functools.partial(route_y, False), pair, sc, value, *x, name="route_y"), "gy")
+    z = exchange(*call(functools.partial(route_z, False), pair, sc, value, *x, *y, name="route_z"), "gz")
     return (*x, *y, *z)
 
 
@@ -394,14 +421,14 @@
     line_length = lax.axis_size("gz")
     pos = [lax.axis_index(axis) for axis in ("gx", "gy", "gz")]
     sc = jnp.stack([p % 2 for p in pos] + [pos[2], mode_count[0, 0, 0]]).astype(jnp.int32)
-    inverse = coarse_inverse[0, 0]
+    inverse = in_hbm(coarse_inverse[0, 0])
     bundle = [((BUNDLE, 128), F32)] * 2
     vector = ((ROWS, 128), F32)
     square = ((ROWS, ROWS), BF16)
     wide = [((bundle_rows(True), 128), F32)] * 2
     gathered = ((line_length, 8, 128), F32)
 
-    sel, load_rows, comp, mode, order_row, sa, sb = pl.pallas_call(
+    sel, load_rows, comp, mode, cols, sa, sb = pl.pallas_call(
         pack_kernel,
         out_shape=[
             jax.ShapeDtypeStruct(*v)
@@ -410,7 +437,7 @@
                 vector,
                 ((ROWS // GROUP, 128), F32),
                 ((16, ROWS), BF16),
-                ((1, ROWS), jnp.int32),
+                ((ROWS, 16), BF16),
                 *wide,
             )
         ],
@@ -425,18 +452,31 @@
         compiler_params=pltpu.CompilerParams(vmem_limit_bytes=16 * 2**20),
         name="pack",
     )(sc, row_order[0, 0, 0][:, None], in_hbm(load_terms[0, 0, 0]), in_hbm(mode_rows[0, 0, 0].T))
+    half = ((ROWS // 2, ROWS), BF16)
     x = exchange_async(sa, sb, "gx")
-    dual, inv, bt, cols = pl.pallas_call(
+    dual_a, inv, bt = pl.pallas_call(
         permute_kernel,
-        out_shape=[jax.ShapeDtypeStruct(*v) for v in (square, square, ((16, ROWS), BF16), ((ROWS, 16), BF16))],
+        out_shape=[jax.ShapeDtypeStruct(*v) for v in (half, square, ((16, ROWS), BF16))],
         in_specs=[VMEM, VMEM, VMEM, HBM],
-        out_specs=[VMEM] * 4,
+        out_specs=[VMEM] * 3,
         scratch_shapes=[pltpu.VMEM((ROWS, ROWS), BF16), pltpu.SemaphoreType.DMA],
         compiler_params=pltpu.CompilerParams(vmem_limit_bytes=16 * 2**20),
         name="permute",
-    )(sel, mode, order_row, in_hbm(dual_blocks[0, 0, 0]))
-    *x, dual, inv, bt, cols = lax.optimization_barrier((*x, dual, inv, bt, cols))
-    received_rows = cross(sc, (load_rows, comp), x, True)
+    )(sel, mode, row_order[0, 0, 0][None, :], in_hbm(dual_blocks[0, 0, 0]))
+    *x, dual_a, inv, bt = lax.optimization_barrier((*x, dual_a, inv, bt))
+    values = (load_rows, comp)
+    y = exchange_async(*call(functools.partial(route_y, True), wide, sc, *values, *x, name="route_y"), "gy")
+    (dual_b,) = pl.pallas_call(
+        functools.partial(permute_rest_kernel, ROWS // 2),
+        out_shape=[jax.ShapeDtypeStruct(*half)],
+        in_specs=[VMEM] * 3,
+        out_specs=[VMEM],
+        compiler_params=pltpu.CompilerParams(vmem_limit_bytes=12 * 2**20),
+        name="permute_rest",
+    )(sel, inv, dual_blocks[0, 0, 0])
+    *y, dual_b = lax.optimization_barrier((*y, dual_b))
+    z = exchange(*call(functools.partial(route_z, True), wide, sc, *values, *x, *y, name="route_z"), "gz")
+    received_rows = (*x, *y, *z)
     residual, their_comp, proj = call(
         first_kernel,
         [vector, ((ROWS // GROUP, 128), F32), gathered],
@@ -446,23 +486,29 @@
         *received_rows,
         name="first",
     )
-    (modes_near,) = call(
-        mode_kernel, [((ROWS, 256), BF16)], sc, cols, their_comp, jnp.asarray(amplitude_blocks()), name="modes"
-    )
-
     center_value = 0.5 * (EIG_HIGH + EIG_LOW)
     half_width = 0.5 * (EIG_HIGH - EIG_LOW)
     rho_prev = half_width / center_value
-    amp = ((24, 128), F32)
+    amp = ((NEAR, 128), F32)
     for iteration in range(ITERS):
         line = lax.all_to_all(proj, "gz", 0, 0, tiled=True).reshape(8 * line_length, 128)
         if iteration == 0:
-            matrix, own = call(line_kernel, [((24, 8 * line_length), F32), amp], sc, line, inverse, name="line")
+            matrix, own = pl.pallas_call(
+                line_kernel,
+                out_shape=[jax.ShapeDtypeStruct((NEAR, 8 * line_length), F32), jax.ShapeDtypeStruct(*amp)],
+                in_specs=[SMEM, VMEM, HBM],
+                out_specs=[VMEM] * 2,
+                scratch_shapes=[pltpu.VMEM(inverse.shape, F32), pltpu.SemaphoreType.DMA],
+                compiler_params=pltpu.CompilerParams(vmem_limit_bytes=12 * 2**20),
+                name="line",
+            )(sc, line, inverse)
+            their_comp, own = lax.optimization_barrier((their_comp, own))
+            (modes_near,) = call(
+                mode_kernel, [((ROWS, STACK), BF16)], sc, cols, their_comp, jnp.asarray(amplitude_blocks()), name="modes"
+            )
         else:
             (own,) = call(solve_kernel, [amp], sc, line, matrix, name="solve")
-        column = jnp.concatenate(exchange(own, own, "gy"), axis=0)
-        near = (modes_near, dual, *exchange(column, column, "gx"))
-        scratch = [pltpu.VMEM((256, 128), F32)]
+        near = (modes_near, dual_a, dual_b, share(share(own, "gy"), "gx"))
         if iteration == 0:
             direction, value, sa, sb = call(
                 functools.partial(advance_kernel, None, center_value),
@@ -470,7 +516,6 @@
                 sc,
                 residual,
                 *near,
-                scratch=scratch,
                 name="advance0",
             )
             multipliers = direction
@@ -484,16 +529,18 @@
                 *near,
                 direction,
                 multipliers,
-                scratch=scratch,
                 name="advance",
             )
             rho_prev = rho_now
-        received_rows = cross(sc, (value,), exchange(sa, sb, "gx"), False)
         if iteration < ITERS - 1:
+            received_rows = cross(sc, value, exchange(sa, sb, "gx"))
             residual, proj = call(
                 step_kernel, [vector, gathered], sc, residual, value, bt, *received_rows, name="step"
             )
+    x = exchange_async(sa, sb, "gx")
     (out_mul,) = call(unpack_kernel, [vector], sc, inv, multipliers, name="unpack")
+    *x, out_mul = lax.optimization_barrier((*x, out_mul))
+    received_rows = cross(sc, value, x)
     (out_res,) = call(
         last_kernel,
         [vector],

time: 230 us -> 221 us (0.961)
  the two profiles are of different devices: /device:TPU:1 before, /device:TPU:40 now
where the time goes in v3:
time: 221 us; the launch traced here: 220 us
  blocking collectives  123 us (56%)
  starting transfers between devices  40.5 us (18%)
  Pallas kernels  31.1 us (14%)
  waiting for transfers between devices  22.9 us (10%)
    all_gather x9, blocking collectives, exchange(): lax.all_gather(first, axis, axis_index_groups=groups, tiled=True)  47.2 us
    all_gather x6, blocking collectives, share(): lax.all_gather(block, (axis, 'gz'), axis_index_groups=groups, tiled=True)  35.8 us
    all_to_all x3, blocking collectives, local(): lax.all_to_all(proj, 'gz', 0, 0, tiled=True).reshape(8 * line_length, 128)  27.2 us
    ppermute x9, starting transfers between devices, exchange(): other = lax.ppermute(second, axis, swaps(size, 1))  26.1 us
    pallas_call x19, Pallas kernels, call(): pl.pallas_call(kernel, out_shape=[jax.ShapeDtypeStruct(s, t) for s, t in...  18.6 us
    all_gather x6, blocking collectives, share(): lax.all_gather(block, 'gz', axis_index_groups=[[z, z + 1] for z in range(...  12.4 us
    ppermute x9, waiting for transfers between devices, exchange(): other = lax.ppermute(second, axis, swaps(size, 1))  11.1 us
    ppermute x3, waiting for transfers between devices, exchange_async(): lax.ppermute(second, axis, swaps(size, 1))  9.88 us
  transfers between devices with their start and end apart: 15, of which 8 were waited for; matrix products, arithmetic and copies ran while one was open for 0% of the time, Pallas kernels for 4%

profile of v3, /device:TPU:40, one launch (start us, length us, event | category | flops | bytes accessed | tf_op | source)
XLA Modules:
  0.0 220.4 jit_solution(15299913463775281054)
XLA Ops:
  2.3 4.0 %pack.1 = (bf16[1024,1024]{1,0:T(8,128)(2,1)S(1)}, f32[1024,128]{1,0:T(8,128)S(1)}, f32[128,128]{1,0:T(8,128)S(1)}, bf16[16,1024]{1,0:T(8,128)(2,1)S(1)}, bf16[1...) custom-call(s32[5]{0:T(128)S(1)} %stack.19.sc, s32[1024,1]{1,0:T(8,128)S(1)} %copy.9.order, ...), custom_call_target="tpu_custom_call" | custom-call | tf_op jit(solution)/shard_map/pack/pallas_call | solution.py:431
  12.4 4.1 %permute.1 = (bf16[512,1024]{1,0:T(8,128)(2,1)S(1)}, bf16[1024,1024]{1,0:T(8,128)(2,1)S(1)}, bf16[16,1024]{1,0:T(8,128)(2,1)S(1)}) custom-call(bf16[1024,1024]{1,0:T(8,128)(2,1)S(1)} %get-tuple-element.66.sel, bf16[16,1024]{1,0:T(8,128)(2,1)S(1)} %get-tuple-element.67.mode, s32[1,1024]{1,0:T(1,128)S(1)} %bitcast.25, bf16[1024,1024]{1,0:T(8,128)(2,1)} %bitcast.19), custom_call_target="tpu_custom_call" | custom-call | tf_op jit(solution)/shard_map/permute/pallas_call | solution.py:457
  16.5 4.3 %collective-permute-done.1.refs_3_.xb = f32[256,128]{1,0:T(8,128)S(1)} collective-permute-done((f32[256,128]{1,0:T(8,128)S(1)}, f32[256,128]{1,0:T(8,128)S(1)}, u32[]{:S(2)}, u32[]{:S(2)}) %collective-permute-start.1) | collective-permute-done | bytes 131104 | tf_op jit(solution)/shard_map/ppermute | solution.py:70
  21.3 4.3 %collective-permute-start.2 = (f32[256,128]{1,0:T(8,128)S(1)}, f32[256,128]{1,0:T(8,128)S(1)}, u32[]{:S(2)}, u32[]{:S(2)}) collective-permute-start(f32[256,128]{1,0:T(8,128)S(1)} %get-tuple-element.75), channel_id=1, source_target_pairs={{0,16},{32,48},{64,80},{96,112},{16,0},{48,32},{80,64},{112,96},{1... | collective-permute-start | bytes 393224 | tf_op jit(solution)/shard_map/ppermute | solution.py:70
  29.3 4.0 %collective-permute-start.4 = (f32[256,128]{1,0:T(8,128)S(1)}, f32[256,128]{1,0:T(8,128)S(1)}, u32[]{:S(2)}, u32[]{:S(2)}) collective-permute-start(f32[256,128]{1,0:T(8,128)S(1)} %get-tuple-element.81), channel_id=1, source_target_pairs={{1,2},{3,4},{5,6},{7,8},{9,10},{11,12},{13,14},{2,1},{4,3},{6,5},{... | collective-permute-start | bytes 393224 | tf_op jit(solution)/shard_map/ppermute | solution.py:64
  38.5 8.6 %all_to_all.15 = f32[16,8,128]{2,1,0:T(8,128)S(1)} all-to-all(f32[16,8,128]{2,1,0:T(8,128)S(1)} %get-tuple-element.85), channel_id=1, replica_groups=mesh['gx'=4,'gy'=8,'gz'=16] {'gz'}, dimensions={0} | all-to-all | bytes 131072 | tf_op jit(solution)/shard_map/all_to_all | solution.py:494
  49.1 8.6 %all_gather.64 = f32[64,128]{1,0:T(8,128)S(1)} all-gather(f32[32,128]{1,0:T(8,128)S(1)} %get-tuple-element.90), channel_id=1, replica_groups={{0,16},{32,48},{64,80},{96,112},{1,113},{33,17},{65,49},{97,81},{2,18},..., dimensions={0}, use_global_device_ids=true | all-gather | bytes 49152 | tf_op jit(solution)/shard_map/all_gather | solution.py:390
  60.4 5.9 %all_gather.66 = f32[256,128]{1,0:T(8,128)S(1)} all-gather(f32[128,128]{1,0:T(8,128)S(1)} %all_gather.65), channel_id=1, replica_groups={{0,128},{256,384},{1,385},{257,129},{2,130},{258,386},{3,387},{259,131}..., dimensions={0}, use_global_device_ids=true | all-gather | bytes 196608 | tf_op jit(solution)/shard_map/all_gather | solution.py:390
  73.8 6.8 %all_gather.68.refs_1_.xa = f32[448,128]{1,0:T(8,128)S(1)} all-gather(f32[224,128]{1,0:T(8,128)S(1)} %get-tuple-element.92), channel_id=1, replica_groups={{0,128},{256,384},{1,129},{257,385},{2,130},{258,386},{3,131},{259,387}..., dimensions={0}, use_global_device_ids=true | all-gather | bytes 344064 | tf_op jit(solution)/shard_map/all_gather | solution.py:65
  83.5 8.5 %all_gather.69.refs_3_.ya = f32[448,128]{1,0:T(8,128)S(1)} all-gather(f32[224,128]{1,0:T(8,128)S(1)} %get-tuple-element.94), channel_id=1, replica_groups={{0,16},{32,48},{64,80},{96,112},{1,17},{33,49},{65,81},{97,113},{2,18},..., dimensions={0}, use_global_device_ids=true | all-gather | bytes 344064 | tf_op jit(solution)/shard_map/all_gather | solution.py:65
  92.6 3.9 %collective-permute-start.7 = (f32[224,128]{1,0:T(8,128)S(1)}, f32[224,128]{1,0:T(8,128)S(1)}, u32[]{:S(2)}, u32[]{:S(2)}) collective-permute-start(f32[224,128]{1,0:T(8,128)S(1)} %get-tuple-element.97), channel_id=1, source_target_pairs={{1,2},{3,4},{5,6},{7,8},{9,10},{11,12},{13,14},{2,1},{4,3},{6,5},{... | collective-permute-start | bytes 344072 | tf_op jit(solution)/shard_map/ppermute | solution.py:64
  101.6 8.5 %all_to_all.16 = f32[16,8,128]{2,1,0:T(8,128)S(1)} all-to-all(f32[16,8,128]{2,1,0:T(8,128)S(1)} %get-tuple-element.99), channel_id=1, replica_groups=mesh['gx'=4,'gy'=8,'gz'=16] {'gz'}, dimensions={0} | all-to-all | bytes 131072 | tf_op jit(solution)/shard_map/all_to_all | solution.py:494
  110.8 4.4 %all_gather.71 = f32[64,128]{1,0:T(8,128)S(1)} all-gather(f32[32,128]{1,0:T(8,128)S(1)} %solve.2), channel_id=1, replica_groups={{0,16},{32,48},{64,80},{96,112},{1,113},{33,17},{65,49},{97,81},{2,18},..., dimensions={0}, use_global_device_ids=true | all-gather | bytes 49152 | tf_op jit(solution)/shard_map/all_gather | solution.py:390
  117.1 6.0 %all_gather.73 = f32[256,128]{1,0:T(8,128)S(1)} all-gather(f32[128,128]{1,0:T(8,128)S(1)} %all_gather.72), channel_id=1, replica_groups={{0,128},{256,384},{1,385},{257,129},{2,130},{258,386},{3,387},{259,131}..., dimensions={0}, use_global_device_ids=true | all-gather | bytes 196608 | tf_op jit(solution)/shard_map/all_gather | solution.py:390
  126.5 6.1 %collective-permute-start.8 = (f32[224,128]{1,0:T(8,128)S(1)}, f32[224,128]{1,0:T(8,128)S(1)}, u32[]{:S(2)}, u32[]{:S(2)}) collective-permute-start(f32[224,128]{1,0:T(8,128)S(1)} %get-tuple-element.104), channel_id=1, source_target_pairs={{128,256},{256,128},{129,257},{257,129},{130,258},{258,130},{131,2... | collective-permute-start | bytes 344072 | tf_op jit(solution)/shard_map/ppermute | solution.py:64
  132.7 6.8 %all_gather.75.refs_1_.xa = f32[448,128]{1,0:T(8,128)S(1)} all-gather(f32[224,128]{1,0:T(8,128)S(1)} %get-tuple-element.103), channel_id=1, replica_groups={{0,128},{256,384},{1,129},{257,385},{2,130},{258,386},{3,131},{259,387}..., dimensions={0}, use_global_device_ids=true | all-gather | bytes 344064 | tf_op jit(solution)/shard_map/all_gather | solution.py:65
  140.7 9.7 %all_gather.76.refs_3_.ya = f32[448,128]{1,0:T(8,128)S(1)} all-gather(f32[224,128]{1,0:T(8,128)S(1)} %get-tuple-element.105), channel_id=1, replica_groups={{0,16},{32,48},{64,80},{96,112},{1,17},{33,49},{65,81},{97,113},{2,18},..., dimensions={0}, use_global_device_ids=true | all-gather | bytes 344064 | tf_op jit(solution)/shard_map/all_gather | solution.py:65
  151.0 5.6 %collective-permute-start.10 = (f32[224,128]{1,0:T(8,128)S(1)}, f32[224,128]{1,0:T(8,128)S(1)}, u32[]{:S(2)}, u32[]{:S(2)}) collective-permute-start(f32[224,128]{1,0:T(8,128)S(1)} %get-tuple-element.108), channel_id=1, source_target_pairs={{1,2},{3,4},{5,6},{7,8},{9,10},{11,12},{13,14},{2,1},{4,3},{6,5},{... | collective-permute-start | bytes 344072 | tf_op jit(solution)/shard_map/ppermute | solution.py:64
  160.0 10.1 %all_to_all.17 = f32[16,8,128]{2,1,0:T(8,128)S(1)} all-to-all(f32[16,8,128]{2,1,0:T(8,128)S(1)} %get-tuple-element.110), channel_id=1, replica_groups=mesh['gx'=4,'gy'=8,'gz'=16] {'gz'}, dimensions={0} | all-to-all | bytes 131072 | tf_op jit(solution)/shard_map/all_to_all | solution.py:494
  170.8 4.4 %all_gather.78 = f32[64,128]{1,0:T(8,128)S(1)} all-gather(f32[32,128]{1,0:T(8,128)S(1)} %solve.3), channel_id=1, replica_groups={{0,16},{32,48},{64,80},{96,112},{1,113},{33,17},{65,49},{97,81},{2,18},..., dimensions={0}, use_global_device_ids=true | all-gather | bytes 49152 | tf_op jit(solution)/shard_map/all_gather | solution.py:390
  177.1 6.5 %all_gather.80 = f32[256,128]{1,0:T(8,128)S(1)} all-gather(f32[128,128]{1,0:T(8,128)S(1)} %all_gather.79), channel_id=1, replica_groups={{0,128},{256,384},{1,385},{257,129},{2,130},{258,386},{3,387},{259,131}..., dimensions={0}, use_global_device_ids=true | all-gather | bytes 196608 | tf_op jit(solution)/shard_map/all_gather | solution.py:390
  195.4 5.6 %collective-permute-done.12.refs_2_.xb = f32[224,128]{1,0:T(8,128)S(1)} collective-permute-done((f32[224,128]{1,0:T(8,128)S(1)}, f32[224,128]{1,0:T(8,128)S(1)}, u32[]{:S(2)}, u32[]{:S(2)}) %collective-permute-start.12) | collective-permute-done | bytes 114720 | tf_op jit(solution)/shard_map/ppermute | solution.py:70
  202.3 7.2 %all_gather.82.refs_3_.ya = f32[448,128]{1,0:T(8,128)S(1)} all-gather(f32[224,128]{1,0:T(8,128)S(1)} %get-tuple-element.120), channel_id=1, replica_groups={{0,16},{32,48},{64,80},{96,112},{1,17},{33,49},{65,81},{97,113},{2,18},..., dimensions={0}, use_global_device_ids=true | all-gather | bytes 344064 | tf_op jit(solution)/shard_map/all_gather | solution.py:65
  214.2 4.1 %collective-permute-done.14.zb = f32[224,128]{1,0:T(8,128)S(1)} collective-permute-done((f32[224,128]{1,0:T(8,128)S(1)}, f32[224,128]{1,0:T(8,128)S(1)}, u32[]{:S(2)}, u32[]{:S(2)}) %collective-permute-start.14) | collective-permute-done | bytes 114720 | tf_op jit(solution)/shard_map/ppermute | solution.py:64
  (61 shorter events, 70.8 us)
Async XLA Ops:
  6.3 10.2 %collective-permute-start = (f32[256,128]{1,0:T(8,128)S(1)}, f32[256,128]{1,0:T(8,128)S(1)}, u32[]{:S(2)}, u32[]{:S(2)}) collective-permute-start(f32[256,128]{1,0:T(8,128)S(1)} %get-tuple-element.64), channel_id=1, source_target_pairs={{0,128},{256,384},{128,0},{384,256},{1,129},{257,385},{129,1},{385... | collective-permute-start | bytes 393224 | tf_op jit(solution)/shard_map/ppermute | solution.py:70
  9.0 11.8 %collective-permute-start.1 = (f32[256,128]{1,0:T(8,128)S(1)}, f32[256,128]{1,0:T(8,128)S(1)}, u32[]{:S(2)}, u32[]{:S(2)}) collective-permute-start(f32[256,128]{1,0:T(8,128)S(1)} %get-tuple-element.65), channel_id=1, source_target_pairs={{128,256},{256,128},{129,257},{257,129},{130,258},{258,130},{131,2... | collective-permute-start | bytes 393224 | tf_op jit(solution)/shard_map/ppermute | solution.py:70
  11.7 0.7 copy-start.2
  12.4 13.9 %copy-start = (bf16[1,1,1,1024,1024]{4,3,2,1,0:T(8,128)(2,1)S(1)}, bf16[1,1,1,1024,1024]{4,3,2,1,0:T(8,128)(2,1)}, u32[]{:S(2)}) copy-start(bf16[1,1,1,1024,1024]{4,3,2,1,0:T(8,128)(2,1)} %param.7) | copy-start | bytes 6291460
  21.3 7.4 %collective-permute-start.2 = (f32[256,128]{1,0:T(8,128)S(1)}, f32[256,128]{1,0:T(8,128)S(1)}, u32[]{:S(2)}, u32[]{:S(2)}) collective-permute-start(f32[256,128]{1,0:T(8,128)S(1)} %get-tuple-element.75), channel_id=1, source_target_pairs={{0,16},{32,48},{64,80},{96,112},{16,0},{48,32},{80,64},{112,96},{1... | collective-permute-start | bytes 393224 | tf_op jit(solution)/shard_map/ppermute | solution.py:70
  25.6 3.1 %collective-permute-start.3 = (f32[256,128]{1,0:T(8,128)S(1)}, f32[256,128]{1,0:T(8,128)S(1)}, u32[]{:S(2)}, u32[]{:S(2)}) collective-permute-start(f32[256,128]{1,0:T(8,128)S(1)} %get-tuple-element.76), channel_id=1, source_target_pairs={{16,32},{48,64},{80,96},{32,16},{64,48},{96,80},{17,33},{49,65},{8... | collective-permute-start | bytes 393224 | tf_op jit(solution)/shard_map/ppermute | solution.py:70
  28.7 39.6 %copy-start.1 = (s32[1024,4]{1,0:T(8,128)S(1)}, s32[1024,4]{1,0:T(8,128)}, u32[]{:S(2)}) copy-start(s32[1024,4]{1,0:T(8,128)} %constant.37.clone.block) | copy-start | bytes 49156
  29.3 8.4 %collective-permute-start.4 = (f32[256,128]{1,0:T(8,128)S(1)}, f32[256,128]{1,0:T(8,128)S(1)}, u32[]{:S(2)}, u32[]{:S(2)}) collective-permute-start(f32[256,128]{1,0:T(8,128)S(1)} %get-tuple-element.81), channel_id=1, source_target_pairs={{1,2},{3,4},{5,6},{7,8},{9,10},{11,12},{13,14},{2,1},{4,3},{6,5},{... | collective-permute-start | bytes 393224 | tf_op jit(solution)/shard_map/ppermute | solution.py:64
  71.2 11.0 %collective-permute-start.5 = (f32[224,128]{1,0:T(8,128)S(1)}, f32[224,128]{1,0:T(8,128)S(1)}, u32[]{:S(2)}, u32[]{:S(2)}) collective-permute-start(f32[224,128]{1,0:T(8,128)S(1)} %get-tuple-element.93), channel_id=1, source_target_pairs={{128,256},{256,128},{129,257},{257,129},{130,258},{258,130},{131,2... | collective-permute-start | bytes 344072 | tf_op jit(solution)/shard_map/ppermute | solution.py:64
  82.8 9.2 %collective-permute-start.6 = (f32[224,128]{1,0:T(8,128)S(1)}, f32[224,128]{1,0:T(8,128)S(1)}, u32[]{:S(2)}, u32[]{:S(2)}) collective-permute-start(f32[224,128]{1,0:T(8,128)S(1)} %get-tuple-element.95), channel_id=1, source_target_pairs={{16,32},{48,64},{80,96},{32,16},{64,48},{96,80},{17,33},{49,65},{8... | collective-permute-start | bytes 344072 | tf_op jit(solution)/shard_map/ppermute | solution.py:64
  92.6 8.2 %collective-permute-start.7 = (f32[224,128]{1,0:T(8,128)S(1)}, f32[224,128]{1,0:T(8,128)S(1)}, u32[]{:S(2)}, u32[]{:S(2)}) collective-permute-start(f32[224,128]{1,0:T(8,128)S(1)} %get-tuple-element.97), channel_id=1, source_target_pairs={{1,2},{3,4},{5,6},{7,8},{9,10},{11,12},{13,14},{2,1},{4,3},{6,5},{... | collective-permute-start | bytes 344072 | tf_op jit(solution)/shard_map/ppermute | solution.py:64
  126.5 12.9 %collective-permute-start.8 = (f32[224,128]{1,0:T(8,128)S(1)}, f32[224,128]{1,0:T(8,128)S(1)}, u32[]{:S(2)}, u32[]{:S(2)}) collective-permute-start(f32[224,128]{1,0:T(8,128)S(1)} %get-tuple-element.104), channel_id=1, source_target_pairs={{128,256},{256,128},{129,257},{257,129},{130,258},{258,130},{131,2... | collective-permute-start | bytes 344072 | tf_op jit(solution)/shard_map/ppermute | solution.py:64
  140.0 10.4 %collective-permute-start.9 = (f32[224,128]{1,0:T(8,128)S(1)}, f32[224,128]{1,0:T(8,128)S(1)}, u32[]{:S(2)}, u32[]{:S(2)}) collective-permute-start(f32[224,128]{1,0:T(8,128)S(1)} %get-tuple-element.106), channel_id=1, source_target_pairs={{16,32},{48,64},{80,96},{32,16},{64,48},{96,80},{17,33},{49,65},{8... | collective-permute-start | bytes 344072 | tf_op jit(solution)/shard_map/ppermute | solution.py:64
  151.0 8.2 %collective-permute-start.10 = (f32[224,128]{1,0:T(8,128)S(1)}, f32[224,128]{1,0:T(8,128)S(1)}, u32[]{:S(2)}, u32[]{:S(2)}) collective-permute-start(f32[224,128]{1,0:T(8,128)S(1)} %get-tuple-element.108), channel_id=1, source_target_pairs={{1,2},{3,4},{5,6},{7,8},{9,10},{11,12},{13,14},{2,1},{4,3},{6,5},{... | collective-permute-start | bytes 344072 | tf_op jit(solution)/shard_map/ppermute | solution.py:64
  187.3 8.1 %collective-permute-start.11 = (f32[224,128]{1,0:T(8,128)S(1)}, f32[224,128]{1,0:T(8,128)S(1)}, u32[]{:S(2)}, u32[]{:S(2)}) collective-permute-start(f32[224,128]{1,0:T(8,128)S(1)} %get-tuple-element.113), channel_id=1, source_target_pairs={{0,128},{256,384},{128,0},{384,256},{1,129},{257,385},{129,1},{385... | collective-permute-start | bytes 344072 | tf_op jit(solution)/shard_map/ppermute | solution.py:70
  189.4 11.6 %collective-permute-start.12 = (f32[224,128]{1,0:T(8,128)S(1)}, f32[224,128]{1,0:T(8,128)S(1)}, u32[]{:S(2)}, u32[]{:S(2)}) collective-permute-start(f32[224,128]{1,0:T(8,128)S(1)} %get-tuple-element.114), channel_id=1, source_target_pairs={{128,256},{256,128},{129,257},{257,129},{130,258},{258,130},{131,2... | collective-permute-start | bytes 344072 | tf_op jit(solution)/shard_map/ppermute | solution.py:70
  201.6 7.9 %collective-permute-start.13 = (f32[224,128]{1,0:T(8,128)S(1)}, f32[224,128]{1,0:T(8,128)S(1)}, u32[]{:S(2)}, u32[]{:S(2)}) collective-permute-start(f32[224,128]{1,0:T(8,128)S(1)} %get-tuple-element.121), channel_id=1, source_target_pairs={{16,32},{48,64},{80,96},{32,16},{64,48},{96,80},{17,33},{49,65},{8... | collective-permute-start | bytes 344072 | tf_op jit(solution)/shard_map/ppermute | solution.py:64
  210.1 8.2 %collective-permute-start.14 = (f32[224,128]{1,0:T(8,128)S(1)}, f32[224,128]{1,0:T(8,128)S(1)}, u32[]{:S(2)}, u32[]{:S(2)}) collective-permute-start(f32[224,128]{1,0:T(8,128)S(1)} %get-tuple-element.123), channel_id=1, source_target_pairs={{1,2},{3,4},{5,6},{7,8},{9,10},{11,12},{13,14},{2,1},{4,3},{6,5},{... | collective-permute-start | bytes 344072 | tf_op jit(solution)/shard_map/ppermute | solution.py:64

commit v4 on v3

--- a/solution.py
+++ b/solution.py
@@ -23,7 +23,7 @@
 WIDTHS = {1: FACE, 2: EDGE, 3: CORNER}
 
 BUNDLE = 224
-NEAR = 32
+NEAR = 4 * NMODE
 STACK = 16 * NEAR
 GROUP = 8
 
@@ -216,13 +216,18 @@
     return pieces
 
 
-def pack_kernel(sc, order, load, modes, sel_ref, load_ref, comp_ref, mode, cols_ref, xa, xb, col, buf, mbuf, sems):
+def pack_kernel(sc, order, load, modes, sel_ref, load_ref, comp_ref, mode, cols_ref, xa, xb, col, buf, mbuf, obuf, sems):
+    copy_order = pltpu.make_async_copy(order, obuf, sems.at[2])
+    copy_order.start()
     copy = pltpu.make_async_copy(load, buf, sems.at[0])
     copy.start()
     copy_modes = pltpu.make_async_copy(modes, mbuf, sems.at[1])
     copy_modes.start()
+    copy_order.wait()
+    turned = obuf[...].astype(F32).T.astype(jnp.int32)
     for offset, begin, width in SLOTS:
-        col[OURS[offset] : OURS[offset] + width, :] = order[begin : begin + width, :]
+        lane, row = begin // 128, begin % 128
+        col[OURS[offset] : OURS[offset] + width, :] = turned[row : row + width, lane : lane + 1]
     step = 256
     for at in range(0, ROWS, step):
         lanes = iota((step, ROWS), 1)
@@ -231,7 +236,10 @@
     top = jnp.concatenate([mbuf[...].astype(F32), jnp.zeros((16 - NMODE, ROWS), F32)], axis=0)
     mode[...] = top.astype(BF16)
     sel = sel_ref[...]
-    cols = dot_t(sel, mode[...]).astype(BF16)
+    copy.wait()
+    both = dot(sel, jnp.concatenate([buf[...], top.T.astype(BF16)], axis=1))
+    load_ref[...] = both[:, 0:128]
+    cols = both[:, 128:].astype(BF16)
     cols_ref[...] = cols
     spread = jnp.where(iota((16, 128), 0) == iota((16, 128), 1) % 16, 1.0, 0.0).astype(BF16)
     wide = dot(cols, spread)
@@ -239,8 +247,6 @@
     wide = jnp.where(keep, wide, 0.0).astype(BF16)
     fold = jnp.where(iota((ROWS // GROUP, ROWS), 0) == iota((ROWS // GROUP, ROWS), 1) // GROUP, 1.0, 0.0)
     comp_ref[...] = dot(fold.astype(BF16), wide)
-    copy.wait()
-    load_ref[...] = dot(sel, buf[...])
     send_x(sc[0], (load_ref, comp_ref), xa, xb, True)
 
 
@@ -259,11 +265,14 @@
         out[at : at + step, :] = dot(rows, inv_ref[...]).astype(BF16)
 
 
-def permute_rest_kernel(first, sel, inv, dual, out):
+def permute_rest_kernel(first, sel, inv, dual, inverse, out, near_inverse, sem):
+    copy = pltpu.make_async_copy(inverse, near_inverse, sem)
+    copy.start()
     step = 256
     for at in range(0, out.shape[0], step):
         rows = dot(sel[first + at : first + at + step, :], dual[...]).astype(BF16)
         out[at : at + step, :] = dot(rows, inv[...]).astype(BF16)
+    copy.wait()
 
 
 def project(sc, bt, residual, out):
@@ -313,10 +322,10 @@
     keep = iota((ROWS, 128), 0) % GROUP == iota((ROWS, 128), 1) // 16
     wide = jnp.where(keep, wide, 0.0).astype(BF16)
     mode = iota((128, STACK), 0) % 16
-    fold = jnp.where((mode == iota((128, STACK), 1) % 8) & (mode < NMODE), 1.0, 0.0).astype(BF16)
+    fold = jnp.where(mode == iota((128, STACK), 1) % NMODE, 1.0, 0.0).astype(BF16)
     theirs = dot(wide, fold)
     mode = iota((16, STACK), 0)
-    own = jnp.where((mode == iota((16, STACK), 1) % 8) & (mode < NMODE), 1.0, 0.0).astype(BF16)
+    own = jnp.where(mode == iota((16, STACK), 1) % NMODE, 1.0, 0.0).astype(BF16)
     mine = dot(cols[...], own)
     x_even, y_even = sc[0] == 0, sc[1] == 0
     which = jnp.where(
@@ -325,34 +334,32 @@
         jnp.where(y_even, block[:, 2:3], block[:, 3:4]),
     )
     which = which + sc[2]
-    at = iota((ROWS, STACK), 1) // 8
+    at = iota((ROWS, STACK), 1) // NMODE
     home = 16 * sc[0] + 4 * sc[1] + 1 + sc[2]
     out[...] = (jnp.where(at == which, theirs, 0.0) + jnp.where(at == home, mine, 0.0)).astype(BF16)
 
 
-def line_kernel(sc, line, inverse, mat_ref, out, buf, sem):
-    copy = pltpu.make_async_copy(inverse, buf, sem)
-    copy.start()
+def line_kernel(sc, line, inverse, mat_ref, out):
     everyone = line[...]
     size, coarse = everyone.shape[0], inverse.shape[0]
-
-    def selection(rows, first):
-        row = iota((rows, size), 0) + first
+    counts = jnp.where(iota((size, 128), 0) % 8 == NMODE, everyone, 0.0).astype(BF16)
+
+    def selection(rows, unit, first):
+        position = iota((rows, size), 0) // unit + first
         col = iota((rows, size), 1)
         is_count = col % 8 == NMODE
-        here = jnp.where(is_count & (col // 8 == row // 8), 1.0, 0.0)
-        before = jnp.where(is_count & (col // 8 < row // 8), 1.0, 0.0)
-        count = jnp.dot(here, everyone, precision=HIGHEST, preferred_element_type=F32)
-        offset = jnp.dot(before, everyone, precision=HIGHEST, preferred_element_type=F32)
-        mode = ((iota((rows, 128), 0) + first) % 8).astype(F32)
+        here = jnp.where(is_count & (col // 8 == position), 1.0, 0.0)
+        before = jnp.where(is_count & (col // 8 < position), 1.0, 0.0)
+        count = dot(here.astype(BF16), counts)
+        offset = dot(before.astype(BF16), counts)
+        mode = (iota((rows, 128), 0) % unit).astype(F32)
         compact = iota((rows, 128), 1).astype(F32)
         hit = (compact == offset + mode) & (mode < count)
         return jnp.where(hit, 1.0, 0.0)[:, 0:coarse]
 
-    everywhere = selection(size, 0)
-    near = selection(NEAR, 8 * (sc[3] - sc[2]) - 8)
-    copy.wait()
-    rows = jnp.dot(near, buf[...], precision=HIGHEST, preferred_element_type=F32)
+    everywhere = selection(size, 8, 0)
+    near = selection(NEAR, NMODE, sc[3] - sc[2] - 1)
+    rows = jnp.dot(near, inverse[...], precision=HIGHEST, preferred_element_type=F32)
     matrix = lax.dot_general(rows, everywhere, (((1,), (1,)), ((), ())), precision=HIGHEST, preferred_element_type=F32)
     mat_ref[...] = matrix
     out[...] = jnp.dot(matrix, everyone, precision=HIGHEST, preferred_element_type=F32)
@@ -441,17 +448,18 @@
                 *wide,
             )
         ],
-        in_specs=[SMEM, VMEM, HBM, HBM],
+        in_specs=[SMEM, HBM, HBM, HBM],
         out_specs=[VMEM] * 7,
         scratch_shapes=[
             pltpu.VMEM((ROWS, 1), jnp.int32),
             pltpu.VMEM((ROWS, 128), BF16),
             pltpu.VMEM((NMODE, ROWS), BF16),
-            pltpu.SemaphoreType.DMA((2,)),
+            pltpu.VMEM((ROWS // 128, 128), jnp.int32),
+            pltpu.SemaphoreType.DMA((3,)),
         ],
         compiler_params=pltpu.CompilerParams(vmem_limit_bytes=16 * 2**20),
         name="pack",
-    )(sc, row_order[0, 0, 0][:, None], in_hbm(load_terms[0, 0, 0]), in_hbm(mode_rows[0, 0, 0].T))
+    )(sc, in_hbm(row_order[0, 0, 0].reshape(ROWS // 128, 128)), in_hbm(load_terms[0, 0, 0]), in_hbm(mode_rows[0, 0, 0].T))
     half = ((ROWS // 2, ROWS), BF16)
     x = exchange_async(sa, sb, "gx")
     dual_a, inv, bt = pl.pallas_call(
@@ -466,15 +474,16 @@
     *x, dual_a, inv, bt = lax.optimization_barrier((*x, dual_a, inv, bt))
     values = (load_rows, comp)
     y = exchange_async(*call(functools.partial(route_y, True), wide, sc, *values, *x, name="route_y"), "gy")
-    (dual_b,) = pl.pallas_call(
+    dual_b, near_inverse = pl.pallas_call(
         functools.partial(permute_rest_kernel, ROWS // 2),
-        out_shape=[jax.ShapeDtypeStruct(*half)],
-        in_specs=[VMEM] * 3,
-        out_specs=[VMEM],
+        out_shape=[jax.ShapeDtypeStruct(*half), jax.ShapeDtypeStruct(inverse.shape, F32)],
+        in_specs=[VMEM] * 3 + [HBM],
+        out_specs=[VMEM] * 2,
+        scratch_shapes=[pltpu.SemaphoreType.DMA],
         compiler_params=pltpu.CompilerParams(vmem_limit_bytes=12 * 2**20),
         name="permute_rest",
-    )(sel, inv, dual_blocks[0, 0, 0])
-    *y, dual_b = lax.optimization_barrier((*y, dual_b))
+    )(sel, inv, dual_blocks[0, 0, 0], inverse)
+    *y, dual_b, near_inverse = lax.optimization_barrier((*y, dual_b, near_inverse))
     z = exchange(*call(functools.partial(route_z, True), wide, sc, *values, *x, *y, name="route_z"), "gz")
     received_rows = (*x, *y, *z)
     residual, their_comp, proj = call(
@@ -493,15 +502,8 @@
     for iteration in range(ITERS):
         line = lax.all_to_all(proj, "gz", 0, 0, tiled=True).reshape(8 * line_length, 128)
         if iteration == 0:
-            matrix, own = pl.pallas_call(
-                line_kernel,
-                out_shape=[jax.ShapeDtypeStruct((NEAR, 8 * line_length), F32), jax.ShapeDtypeStruct(*amp)],
-                in_specs=[SMEM, VMEM, HBM],
-                out_specs=[VMEM] * 2,
-                scratch_shapes=[pltpu.VMEM(inverse.shape, F32), pltpu.SemaphoreType.DMA],
-                compiler_params=pltpu.CompilerParams(vmem_limit_bytes=12 * 2**20),
-                name="line",
-            )(sc, line, inverse)
+            near_matrix = ((NEAR, 8 * line_length), F32)
+            matrix, own = call(line_kernel, [near_matrix, amp], sc, line, near_inverse, name="line")
             their_comp, own = lax.optimization_barrier((their_comp, own))
             (modes_near,) = call(
                 mode_kernel, [((ROWS, STACK), BF16)], sc, cols, their_comp, jnp.asarray(amplitude_blocks()), name="modes"

time: 221 us -> 218 us (0.986)
    pallas_call x19 -> x20, Pallas kernels: 18.6 us -> 19.8 us  [call(): pl.pallas_call(kernel, out_shape=[jax.ShapeDtypeStruct(s, t) for s, t in...]
where the time goes in v4:
time: 218 us; the launch traced here: 217 us
  blocking collectives  122 us (56%)
  starting transfers between devices  40.5 us (19%)
  Pallas kernels  29.5 us (14%)
  waiting for transfers between devices  22.8 us (10%)
    all_gather x9, blocking collectives, exchange(): lax.all_gather(first, axis, axis_index_groups=groups, tiled=True)  47.3 us
    all_gather x6, blocking collectives, share(): lax.all_gather(block, (axis, 'gz'), axis_index_groups=groups, tiled=True)  35 us
    all_to_all x3, blocking collectives, local(): lax.all_to_all(proj, 'gz', 0, 0, tiled=True).reshape(8 * line_length, 128)  27.1 us
    ppermute x9, starting transfers between devices, exchange(): other = lax.ppermute(second, axis, swaps(size, 1))  25.8 us
    pallas_call x20, Pallas kernels, call(): pl.pallas_call(kernel, out_shape=[jax.ShapeDtypeStruct(s, t) for s, t in...  19.8 us
    all_gather x6, blocking collectives, share(): lax.all_gather(block, 'gz', axis_index_groups=[[z, z + 1] for z in range(...  12.4 us
    ppermute x9, waiting for transfers between devices, exchange(): other = lax.ppermute(second, axis, swaps(size, 1))  11.2 us
    ppermute x3, waiting for transfers between devices, exchange_async(): lax.ppermute(second, axis, swaps(size, 1))  9.89 us
  transfers between devices with their start and end apart: 15, of which 8 were waited for; matrix products, arithmetic and copies ran while one was open for 0% of the time, Pallas kernels for 4%

profile of v4, /device:TPU:40, one launch (start us, length us, event | category | flops | bytes accessed | tf_op | source)
XLA Modules:
  0.0 217.0 jit_solution(5896146868024005282)
XLA Ops:
  1.4 3.2 %pack.1 = (bf16[1024,1024]{1,0:T(8,128)(2,1)S(1)}, f32[1024,128]{1,0:T(8,128)S(1)}, f32[128,128]{1,0:T(8,128)S(1)}, bf16[16,1024]{1,0:T(8,128)(2,1)S(1)}, bf16[1...) custom-call(s32[5]{0:T(128)S(1)} %stack.19.sc, s32[8,128]{1,0:T(8,128)} %bitcast.24, ...), custom_call_target="tpu_custom_call" | custom-call | tf_op jit(solution)/shard_map/pack/pallas_call | solution.py:438
  10.7 4.1 %permute.1 = (bf16[512,1024]{1,0:T(8,128)(2,1)S(1)}, bf16[1024,1024]{1,0:T(8,128)(2,1)S(1)}, bf16[16,1024]{1,0:T(8,128)(2,1)S(1)}) custom-call(bf16[1024,1024]{1,0:T(8,128)(2,1)S(1)} %get-tuple-element.69.sel, bf16[16,1024]{1,0:T(8,128)(2,1)S(1)} %get-tuple-element.70.mode, s32[1,1024]{1,0:T(1,128)S(1)} %bitcast.25, bf16[1024,1024]{1,0:T(8,128)(2,1)} %bitcast.19), custom_call_target="tpu_custom_call" | custom-call | tf_op jit(solution)/shard_map/permute/pallas_call | solution.py:465
  14.8 4.2 %collective-permute-done.1.refs_3_.xb = f32[256,128]{1,0:T(8,128)S(1)} collective-permute-done((f32[256,128]{1,0:T(8,128)S(1)}, f32[256,128]{1,0:T(8,128)S(1)}, u32[]{:S(2)}, u32[]{:S(2)}) %collective-permute-start.1) | collective-permute-done | bytes 131104 | tf_op jit(solution)/shard_map/ppermute | solution.py:70
  19.7 4.3 %collective-permute-start.2 = (f32[256,128]{1,0:T(8,128)S(1)}, f32[256,128]{1,0:T(8,128)S(1)}, u32[]{:S(2)}, u32[]{:S(2)}) collective-permute-start(f32[256,128]{1,0:T(8,128)S(1)} %get-tuple-element.78), channel_id=1, source_target_pairs={{0,16},{32,48},{64,80},{96,112},{16,0},{48,32},{80,64},{112,96},{1... | collective-permute-start | bytes 393224 | tf_op jit(solution)/shard_map/ppermute | solution.py:70
  27.6 4.0 %collective-permute-start.4 = (f32[256,128]{1,0:T(8,128)S(1)}, f32[256,128]{1,0:T(8,128)S(1)}, u32[]{:S(2)}, u32[]{:S(2)}) collective-permute-start(f32[256,128]{1,0:T(8,128)S(1)} %get-tuple-element.86), channel_id=1, source_target_pairs={{1,2},{3,4},{5,6},{7,8},{9,10},{11,12},{13,14},{2,1},{4,3},{6,5},{... | collective-permute-start | bytes 393224 | tf_op jit(solution)/shard_map/ppermute | solution.py:64
  36.8 8.6 %all_to_all.15 = f32[16,8,128]{2,1,0:T(8,128)S(1)} all-to-all(f32[16,8,128]{2,1,0:T(8,128)S(1)} %get-tuple-element.90), channel_id=1, replica_groups=mesh['gx'=4,'gy'=8,'gz'=16] {'gz'}, dimensions={0} | all-to-all | bytes 131072 | tf_op jit(solution)/shard_map/all_to_all | solution.py:503
  46.7 8.6 %all_gather.64 = f32[48,128]{1,0:T(8,128)S(1)} all-gather(f32[24,128]{1,0:T(8,128)S(1)} %get-tuple-element.96), channel_id=1, replica_groups={{0,16},{32,48},{64,80},{96,112},{1,113},{33,17},{65,49},{97,81},{2,18},..., dimensions={0}, use_global_device_ids=true | all-gather | bytes 36864 | tf_op jit(solution)/shard_map/all_gather | solution.py:397
  58.0 5.7 %all_gather.66 = f32[192,128]{1,0:T(8,128)S(1)} all-gather(f32[96,128]{1,0:T(8,128)S(1)} %all_gather.65), channel_id=1, replica_groups={{0,128},{256,384},{1,385},{257,129},{2,130},{258,386},{3,387},{259,131}..., dimensions={0}, use_global_device_ids=true | all-gather | bytes 147456 | tf_op jit(solution)/shard_map/all_gather | solution.py:397
  71.1 6.8 %all_gather.68.refs_1_.xa = f32[448,128]{1,0:T(8,128)S(1)} all-gather(f32[224,128]{1,0:T(8,128)S(1)} %get-tuple-element.98), channel_id=1, replica_groups={{0,128},{256,384},{1,129},{257,385},{2,130},{258,386},{3,131},{259,387}..., dimensions={0}, use_global_device_ids=true | all-gather | bytes 344064 | tf_op jit(solution)/shard_map/all_gather | solution.py:65
  80.8 8.5 %all_gather.69.refs_3_.ya = f32[448,128]{1,0:T(8,128)S(1)} all-gather(f32[224,128]{1,0:T(8,128)S(1)} %get-tuple-element.100), channel_id=1, replica_groups={{0,16},{32,48},{64,80},{96,112},{1,17},{33,49},{65,81},{97,113},{2,18},..., dimensions={0}, use_global_device_ids=true | all-gather | bytes 344064 | tf_op jit(solution)/shard_map/all_gather | solution.py:65
  89.9 3.8 %collective-permute-start.7 = (f32[224,128]{1,0:T(8,128)S(1)}, f32[224,128]{1,0:T(8,128)S(1)}, u32[]{:S(2)}, u32[]{:S(2)}) collective-permute-start(f32[224,128]{1,0:T(8,128)S(1)} %get-tuple-element.103), channel_id=1, source_target_pairs={{1,2},{3,4},{5,6},{7,8},{9,10},{11,12},{13,14},{2,1},{4,3},{6,5},{... | collective-permute-start | bytes 344072 | tf_op jit(solution)/shard_map/ppermute | solution.py:64
  98.9 8.4 %all_to_all.16 = f32[16,8,128]{2,1,0:T(8,128)S(1)} all-to-all(f32[16,8,128]{2,1,0:T(8,128)S(1)} %get-tuple-element.105), channel_id=1, replica_groups=mesh['gx'=4,'gy'=8,'gz'=16] {'gz'}, dimensions={0} | all-to-all | bytes 131072 | tf_op jit(solution)/shard_map/all_to_all | solution.py:503
  108.0 4.4 %all_gather.71 = f32[48,128]{1,0:T(8,128)S(1)} all-gather(f32[24,128]{1,0:T(8,128)S(1)} %solve.2), channel_id=1, replica_groups={{0,16},{32,48},{64,80},{96,112},{1,113},{33,17},{65,49},{97,81},{2,18},..., dimensions={0}, use_global_device_ids=true | all-gather | bytes 36864 | tf_op jit(solution)/shard_map/all_gather | solution.py:397
  114.3 5.8 %all_gather.73 = f32[192,128]{1,0:T(8,128)S(1)} all-gather(f32[96,128]{1,0:T(8,128)S(1)} %all_gather.72), channel_id=1, replica_groups={{0,128},{256,384},{1,385},{257,129},{2,130},{258,386},{3,387},{259,131}..., dimensions={0}, use_global_device_ids=true | all-gather | bytes 147456 | tf_op jit(solution)/shard_map/all_gather | solution.py:397
  123.5 5.9 %collective-permute-start.8 = (f32[224,128]{1,0:T(8,128)S(1)}, f32[224,128]{1,0:T(8,128)S(1)}, u32[]{:S(2)}, u32[]{:S(2)}) collective-permute-start(f32[224,128]{1,0:T(8,128)S(1)} %get-tuple-element.110), channel_id=1, source_target_pairs={{128,256},{256,128},{129,257},{257,129},{130,258},{258,130},{131,2... | collective-permute-start | bytes 344072 | tf_op jit(solution)/shard_map/ppermute | solution.py:64
  129.5 6.8 %all_gather.75.refs_1_.xa = f32[448,128]{1,0:T(8,128)S(1)} all-gather(f32[224,128]{1,0:T(8,128)S(1)} %get-tuple-element.109), channel_id=1, replica_groups={{0,128},{256,384},{1,129},{257,385},{2,130},{258,386},{3,131},{259,387}..., dimensions={0}, use_global_device_ids=true | all-gather | bytes 344064 | tf_op jit(solution)/shard_map/all_gather | solution.py:65
  137.5 9.8 %all_gather.76.refs_3_.ya = f32[448,128]{1,0:T(8,128)S(1)} all-gather(f32[224,128]{1,0:T(8,128)S(1)} %get-tuple-element.111), channel_id=1, replica_groups={{0,16},{32,48},{64,80},{96,112},{1,17},{33,49},{65,81},{97,113},{2,18},..., dimensions={0}, use_global_device_ids=true | all-gather | bytes 344064 | tf_op jit(solution)/shard_map/all_gather | solution.py:65
  147.8 5.6 %collective-permute-start.10 = (f32[224,128]{1,0:T(8,128)S(1)}, f32[224,128]{1,0:T(8,128)S(1)}, u32[]{:S(2)}, u32[]{:S(2)}) collective-permute-start(f32[224,128]{1,0:T(8,128)S(1)} %get-tuple-element.114), channel_id=1, source_target_pairs={{1,2},{3,4},{5,6},{7,8},{9,10},{11,12},{13,14},{2,1},{4,3},{6,5},{... | collective-permute-start | bytes 344072 | tf_op jit(solution)/shard_map/ppermute | solution.py:64
  156.8 10.2 %all_to_all.17 = f32[16,8,128]{2,1,0:T(8,128)S(1)} all-to-all(f32[16,8,128]{2,1,0:T(8,128)S(1)} %get-tuple-element.116), channel_id=1, replica_groups=mesh['gx'=4,'gy'=8,'gz'=16] {'gz'}, dimensions={0} | all-to-all | bytes 131072 | tf_op jit(solution)/shard_map/all_to_all | solution.py:503
  167.7 4.4 %all_gather.78 = f32[48,128]{1,0:T(8,128)S(1)} all-gather(f32[24,128]{1,0:T(8,128)S(1)} %solve.3), channel_id=1, replica_groups={{0,16},{32,48},{64,80},{96,112},{1,113},{33,17},{65,49},{97,81},{2,18},..., dimensions={0}, use_global_device_ids=true | all-gather | bytes 36864 | tf_op jit(solution)/shard_map/all_gather | solution.py:397
  173.9 6.1 %all_gather.80 = f32[192,128]{1,0:T(8,128)S(1)} all-gather(f32[96,128]{1,0:T(8,128)S(1)} %all_gather.79), channel_id=1, replica_groups={{0,128},{256,384},{1,385},{257,129},{2,130},{258,386},{3,387},{259,131}..., dimensions={0}, use_global_device_ids=true | all-gather | bytes 147456 | tf_op jit(solution)/shard_map/all_gather | solution.py:397
  192.0 5.6 %collective-permute-done.12.refs_2_.xb = f32[224,128]{1,0:T(8,128)S(1)} collective-permute-done((f32[224,128]{1,0:T(8,128)S(1)}, f32[224,128]{1,0:T(8,128)S(1)}, u32[]{:S(2)}, u32[]{:S(2)}) %collective-permute-start.12) | collective-permute-done | bytes 114720 | tf_op jit(solution)/shard_map/ppermute | solution.py:70
  198.9 7.2 %all_gather.82.refs_3_.ya = f32[448,128]{1,0:T(8,128)S(1)} all-gather(f32[224,128]{1,0:T(8,128)S(1)} %get-tuple-element.126), channel_id=1, replica_groups={{0,16},{32,48},{64,80},{96,112},{1,17},{33,49},{65,81},{97,113},{2,18},..., dimensions={0}, use_global_device_ids=true | all-gather | bytes 344064 | tf_op jit(solution)/shard_map/all_gather | solution.py:65
  210.8 4.1 %collective-permute-done.14.zb = f32[224,128]{1,0:T(8,128)S(1)} collective-permute-done((f32[224,128]{1,0:T(8,128)S(1)}, f32[224,128]{1,0:T(8,128)S(1)}, u32[]{:S(2)}, u32[]{:S(2)}) %collective-permute-start.14) | collective-permute-done | bytes 114720 | tf_op jit(solution)/shard_map/ppermute | solution.py:64
  (60 shorter events, 69.3 us)
Async XLA Ops:
  4.6 10.2 %collective-permute-start = (f32[256,128]{1,0:T(8,128)S(1)}, f32[256,128]{1,0:T(8,128)S(1)}, u32[]{:S(2)}, u32[]{:S(2)}) collective-permute-start(f32[256,128]{1,0:T(8,128)S(1)} %get-tuple-element.67), channel_id=1, source_target_pairs={{0,128},{256,384},{128,0},{384,256},{1,129},{257,385},{129,1},{385... | collective-permute-start | bytes 393224 | tf_op jit(solution)/shard_map/ppermute | solution.py:70
  7.3 11.8 %collective-permute-start.1 = (f32[256,128]{1,0:T(8,128)S(1)}, f32[256,128]{1,0:T(8,128)S(1)}, u32[]{:S(2)}, u32[]{:S(2)}) collective-permute-start(f32[256,128]{1,0:T(8,128)S(1)} %get-tuple-element.68), channel_id=1, source_target_pairs={{128,256},{256,128},{129,257},{257,129},{130,258},{258,130},{131,2... | collective-permute-start | bytes 393224 | tf_op jit(solution)/shard_map/ppermute | solution.py:70
  10.0 0.7 copy-start.2
  10.7 13.9 %copy-start = (bf16[1,1,1,1024,1024]{4,3,2,1,0:T(8,128)(2,1)S(1)}, bf16[1,1,1,1024,1024]{4,3,2,1,0:T(8,128)(2,1)}, u32[]{:S(2)}) copy-start(bf16[1,1,1,1024,1024]{4,3,2,1,0:T(8,128)(2,1)} %param.7) | copy-start | bytes 6291460
  19.7 7.4 %collective-permute-start.2 = (f32[256,128]{1,0:T(8,128)S(1)}, f32[256,128]{1,0:T(8,128)S(1)}, u32[]{:S(2)}, u32[]{:S(2)}) collective-permute-start(f32[256,128]{1,0:T(8,128)S(1)} %get-tuple-element.78), channel_id=1, source_target_pairs={{0,16},{32,48},{64,80},{96,112},{16,0},{48,32},{80,64},{112,96},{1... | collective-permute-start | bytes 393224 | tf_op jit(solution)/shard_map/ppermute | solution.py:70
  24.0 3.1 %collective-permute-start.3 = (f32[256,128]{1,0:T(8,128)S(1)}, f32[256,128]{1,0:T(8,128)S(1)}, u32[]{:S(2)}, u32[]{:S(2)}) collective-permute-start(f32[256,128]{1,0:T(8,128)S(1)} %get-tuple-element.79), channel_id=1, source_target_pairs={{16,32},{48,64},{80,96},{32,16},{64,48},{96,80},{17,33},{49,65},{8... | collective-permute-start | bytes 393224 | tf_op jit(solution)/shard_map/ppermute | solution.py:70
  27.0 38.7 %copy-start.1 = (s32[1024,4]{1,0:T(8,128)S(1)}, s32[1024,4]{1,0:T(8,128)}, u32[]{:S(2)}) copy-start(s32[1024,4]{1,0:T(8,128)} %constant.37.clone.block) | copy-start | bytes 49156
  27.6 8.4 %collective-permute-start.4 = (f32[256,128]{1,0:T(8,128)S(1)}, f32[256,128]{1,0:T(8,128)S(1)}, u32[]{:S(2)}, u32[]{:S(2)}) collective-permute-start(f32[256,128]{1,0:T(8,128)S(1)} %get-tuple-element.86), channel_id=1, source_target_pairs={{1,2},{3,4},{5,6},{7,8},{9,10},{11,12},{13,14},{2,1},{4,3},{6,5},{... | collective-permute-start | bytes 393224 | tf_op jit(solution)/shard_map/ppermute | solution.py:64
  68.5 11.1 %collective-permute-start.5 = (f32[224,128]{1,0:T(8,128)S(1)}, f32[224,128]{1,0:T(8,128)S(1)}, u32[]{:S(2)}, u32[]{:S(2)}) collective-permute-start(f32[224,128]{1,0:T(8,128)S(1)} %get-tuple-element.99), channel_id=1, source_target_pairs={{128,256},{256,128},{129,257},{257,129},{130,258},{258,130},{131,2... | collective-permute-start | bytes 344072 | tf_op jit(solution)/shard_map/ppermute | solution.py:64
  80.1 9.2 %collective-permute-start.6 = (f32[224,128]{1,0:T(8,128)S(1)}, f32[224,128]{1,0:T(8,128)S(1)}, u32[]{:S(2)}, u32[]{:S(2)}) collective-permute-start(f32[224,128]{1,0:T(8,128)S(1)} %get-tuple-element.101), channel_id=1, source_target_pairs={{16,32},{48,64},{80,96},{32,16},{64,48},{96,80},{17,33},{49,65},{8... | collective-permute-start | bytes 344072 | tf_op jit(solution)/shard_map/ppermute | solution.py:64
  89.9 8.2 %collective-permute-start.7 = (f32[224,128]{1,0:T(8,128)S(1)}, f32[224,128]{1,0:T(8,128)S(1)}, u32[]{:S(2)}, u32[]{:S(2)}) collective-permute-start(f32[224,128]{1,0:T(8,128)S(1)} %get-tuple-element.103), channel_id=1, source_target_pairs={{1,2},{3,4},{5,6},{7,8},{9,10},{11,12},{13,14},{2,1},{4,3},{6,5},{... | collective-permute-start | bytes 344072 | tf_op jit(solution)/shard_map/ppermute | solution.py:64
  123.5 12.7 %collective-permute-start.8 = (f32[224,128]{1,0:T(8,128)S(1)}, f32[224,128]{1,0:T(8,128)S(1)}, u32[]{:S(2)}, u32[]{:S(2)}) collective-permute-start(f32[224,128]{1,0:T(8,128)S(1)} %get-tuple-element.110), channel_id=1, source_target_pairs={{128,256},{256,128},{129,257},{257,129},{130,258},{258,130},{131,2... | collective-permute-start | bytes 344072 | tf_op jit(solution)/shard_map/ppermute | solution.py:64
  136.8 10.4 %collective-permute-start.9 = (f32[224,128]{1,0:T(8,128)S(1)}, f32[224,128]{1,0:T(8,128)S(1)}, u32[]{:S(2)}, u32[]{:S(2)}) collective-permute-start(f32[224,128]{1,0:T(8,128)S(1)} %get-tuple-element.112), channel_id=1, source_target_pairs={{16,32},{48,64},{80,96},{32,16},{64,48},{96,80},{17,33},{49,65},{8... | collective-permute-start | bytes 344072 | tf_op jit(solution)/shard_map/ppermute | solution.py:64
  147.8 8.2 %collective-permute-start.10 = (f32[224,128]{1,0:T(8,128)S(1)}, f32[224,128]{1,0:T(8,128)S(1)}, u32[]{:S(2)}, u32[]{:S(2)}) collective-permute-start(f32[224,128]{1,0:T(8,128)S(1)} %get-tuple-element.114), channel_id=1, source_target_pairs={{1,2},{3,4},{5,6},{7,8},{9,10},{11,12},{13,14},{2,1},{4,3},{6,5},{... | collective-permute-start | bytes 344072 | tf_op jit(solution)/shard_map/ppermute | solution.py:64
  183.9 8.1 %collective-permute-start.11 = (f32[224,128]{1,0:T(8,128)S(1)}, f32[224,128]{1,0:T(8,128)S(1)}, u32[]{:S(2)}, u32[]{:S(2)}) collective-permute-start(f32[224,128]{1,0:T(8,128)S(1)} %get-tuple-element.119), channel_id=1, source_target_pairs={{0,128},{256,384},{128,0},{384,256},{1,129},{257,385},{129,1},{385... | collective-permute-start | bytes 344072 | tf_op jit(solution)/shard_map/ppermute | solution.py:70
  186.0 11.6 %collective-permute-start.12 = (f32[224,128]{1,0:T(8,128)S(1)}, f32[224,128]{1,0:T(8,128)S(1)}, u32[]{:S(2)}, u32[]{:S(2)}) collective-permute-start(f32[224,128]{1,0:T(8,128)S(1)} %get-tuple-element.120), channel_id=1, source_target_pairs={{128,256},{256,128},{129,257},{257,129},{130,258},{258,130},{131,2... | collective-permute-start | bytes 344072 | tf_op jit(solution)/shard_map/ppermute | solution.py:70
  198.2 7.9 %collective-permute-start.13 = (f32[224,128]{1,0:T(8,128)S(1)}, f32[224,128]{1,0:T(8,128)S(1)}, u32[]{:S(2)}, u32[]{:S(2)}) collective-permute-start(f32[224,128]{1,0:T(8,128)S(1)} %get-tuple-element.127), channel_id=1, source_target_pairs={{16,32},{48,64},{80,96},{32,16},{64,48},{96,80},{17,33},{49,65},{8... | collective-permute-start | bytes 344072 | tf_op jit(solution)/shard_map/ppermute | solution.py:64
  206.7 8.2 %collective-permute-start.14 = (f32[224,128]{1,0:T(8,128)S(1)}, f32[224,128]{1,0:T(8,128)S(1)}, u32[]{:S(2)}, u32[]{:S(2)}) collective-permute-start(f32[224,128]{1,0:T(8,128)S(1)} %get-tuple-element.129), channel_id=1, source_target_pairs={{1,2},{3,4},{5,6},{7,8},{9,10},{11,12},{13,14},{2,1},{4,3},{6,5},{... | collective-permute-start | bytes 344072 | tf_op jit(solution)/shard_map/ppermute | solution.py:64

commit v5 on v4

--- a/solution.py
+++ b/solution.py
@@ -216,15 +216,15 @@
     return pieces
 
 
-def pack_kernel(sc, order, load, modes, sel_ref, load_ref, comp_ref, mode, cols_ref, xa, xb, col, buf, mbuf, obuf, sems):
-    copy_order = pltpu.make_async_copy(order, obuf, sems.at[2])
+def pack_kernel(sc, order, load, modes, sel_ref, load_ref, comp_ref, mode, cols_ref, order_ref, xa, xb, col, buf, mbuf, sems):
+    copy_order = pltpu.make_async_copy(order, order_ref, sems.at[2])
     copy_order.start()
     copy = pltpu.make_async_copy(load, buf, sems.at[0])
     copy.start()
     copy_modes = pltpu.make_async_copy(modes, mbuf, sems.at[1])
     copy_modes.start()
     copy_order.wait()
-    turned = obuf[...].astype(F32).T.astype(jnp.int32)
+    turned = order_ref[...].astype(F32).T.astype(jnp.int32)
     for offset, begin, width in SLOTS:
         lane, row = begin // 128, begin % 128
         col[OURS[offset] : OURS[offset] + width, :] = turned[row : row + width, lane : lane + 1]
@@ -250,10 +250,14 @@
     send_x(sc[0], (load_ref, comp_ref), xa, xb, True)
 
 
-def permute_kernel(sel, mode, order_row, dual, out, inv_ref, bt_ref, buf, sem):
+def permute_kernel(sel, mode, order, dual, out, inv_ref, bt_ref, buf, sem):
     copy = pltpu.make_async_copy(dual, buf, sem)
     copy.start()
-    packed = jnp.concatenate([order_row[:, begin : begin + width] for _, begin, width in SLOTS], axis=1)
+    pieces = []
+    for _, begin, width in SLOTS:
+        row, lane = begin // 128, begin % 128
+        pieces.append(order[row : row + 1, lane : lane + width])
+    packed = jnp.concatenate(pieces, axis=1)
     step = 256
     for at in range(0, ROWS, step):
         subs = iota((step, ROWS), 0) + at
@@ -435,7 +439,7 @@
     wide = [((bundle_rows(True), 128), F32)] * 2
     gathered = ((line_length, 8, 128), F32)
 
-    sel, load_rows, comp, mode, cols, sa, sb = pl.pallas_call(
+    sel, load_rows, comp, mode, cols, order, sa, sb = pl.pallas_call(
         pack_kernel,
         out_shape=[
             jax.ShapeDtypeStruct(*v)
@@ -445,16 +449,16 @@
                 ((ROWS // GROUP, 128), F32),
                 ((16, ROWS), BF16),
                 ((ROWS, 16), BF16),
+                ((ROWS // 128, 128), jnp.int32),
                 *wide,
             )
         ],
         in_specs=[SMEM, HBM, HBM, HBM],
-        out_specs=[VMEM] * 7,
+        out_specs=[VMEM] * 8,
         scratch_shapes=[
             pltpu.VMEM((ROWS, 1), jnp.int32),
             pltpu.VMEM((ROWS, 128), BF16),
             pltpu.VMEM((NMODE, ROWS), BF16),
-            pltpu.VMEM((ROWS // 128, 128), jnp.int32),
             pltpu.SemaphoreType.DMA((3,)),
         ],
         compiler_params=pltpu.CompilerParams(vmem_limit_bytes=16 * 2**20),
@@ -470,7 +474,7 @@
         scratch_shapes=[pltpu.VMEM((ROWS, ROWS), BF16), pltpu.SemaphoreType.DMA],
         compiler_params=pltpu.CompilerParams(vmem_limit_bytes=16 * 2**20),
         name="permute",
-    )(sel, mode, row_order[0, 0, 0][None, :], in_hbm(dual_blocks[0, 0, 0]))
+    )(sel, mode, order, in_hbm(dual_blocks[0, 0, 0]))
     *x, dual_a, inv, bt = lax.optimization_barrier((*x, dual_a, inv, bt))
     values = (load_rows, comp)
     y = exchange_async(*call(functools.partial(route_y, True), wide, sc, *values, *x, name="route_y"), "gy")

time: 218 us -> 218 us (level)
  no operation moved by 1% of the time
where the time goes in v5:
time: 218 us; the launch traced here: 217 us
  blocking collectives  122 us (56%)
  starting transfers between devices  40.5 us (19%)
  Pallas kernels  29.5 us (14%)
  waiting for transfers between devices  23.5 us (11%)
    all_gather x9, blocking collectives, exchange(): lax.all_gather(first, axis, axis_index_groups=groups, tiled=True)  47.3 us
    all_gather x6, blocking collectives, share(): lax.all_gather(block, (axis, 'gz'), axis_index_groups=groups, tiled=True)  35 us
    all_to_all x3, blocking collectives, local(): lax.all_to_all(proj, 'gz', 0, 0, tiled=True).reshape(8 * line_length, 128)  27.1 us
    ppermute x9, starting transfers between devices, exchange(): other = lax.ppermute(second, axis, swaps(size, 1))  25.8 us
    pallas_call x20, Pallas kernels, call(): pl.pallas_call(kernel, out_shape=[jax.ShapeDtypeStruct(s, t) for s, t in...  19.8 us
    all_gather x6, blocking collectives, share(): lax.all_gather(block, 'gz', axis_index_groups=[[z, z + 1] for z in range(...  12.4 us
    ppermute x9, waiting for transfers between devices, exchange(): other = lax.ppermute(second, axis, swaps(size, 1))  11.2 us
    ppermute x3, waiting for transfers between devices, exchange_async(): lax.ppermute(second, axis, swaps(size, 1))  10.6 us
  transfers between devices with their start and end apart: 15, of which 8 were waited for; matrix products, arithmetic and copies ran while one was open for 0% of the time, Pallas kernels for 4%

profile of v5, /device:TPU:40, one launch (start us, length us, event | category | flops | bytes accessed | tf_op | source)
XLA Modules:
  0.0 217.0 jit_solution(3914207040106552454)
XLA Ops:
  1.4 3.2 %pack.1 = (bf16[1024,1024]{1,0:T(8,128)(2,1)S(1)}, f32[1024,128]{1,0:T(8,128)S(1)}, f32[128,128]{1,0:T(8,128)S(1)}, bf16[16,1024]{1,0:T(8,128)(2,1)S(1)}, bf16[1...) custom-call(s32[5]{0:T(128)S(1)} %stack.19.sc, ...), custom_call_target="tpu_custom_call" | custom-call | tf_op jit(solution)/shard_map/pack/pallas_call | solution.py:442
  10.0 4.1 %permute.1 = (bf16[512,1024]{1,0:T(8,128)(2,1)S(1)}, bf16[1024,1024]{1,0:T(8,128)(2,1)S(1)}, bf16[16,1024]{1,0:T(8,128)(2,1)S(1)}) custom-call(bf16[1024,1024]{1,0:T(8,128)(2,1)S(1)} %get-tuple-element.70.sel, bf16[16,1024]{1,0:T(8,128)(2,1)S(1)} %get-tuple-element.71.mode, s32[8,128]{1,0:T(8,128)S(1)} %get-tuple-element.72.order, bf16[1024,1024]{1,0:T(8,128)(2,1)} %bitcast.18), custom_call_target="tpu_custom_call" | custom-call | tf_op jit(solution)/shard_map/permute/pallas_call | solution.py:469
  14.2 4.9 %collective-permute-done.1.refs_3_.xb = f32[256,128]{1,0:T(8,128)S(1)} collective-permute-done((f32[256,128]{1,0:T(8,128)S(1)}, f32[256,128]{1,0:T(8,128)S(1)}, u32[]{:S(2)}, u32[]{:S(2)}) %collective-permute-start.1) | collective-permute-done | bytes 131104 | tf_op jit(solution)/shard_map/ppermute | solution.py:70
  19.7 4.3 %collective-permute-start.2 = (f32[256,128]{1,0:T(8,128)S(1)}, f32[256,128]{1,0:T(8,128)S(1)}, u32[]{:S(2)}, u32[]{:S(2)}) collective-permute-start(f32[256,128]{1,0:T(8,128)S(1)} %get-tuple-element.80), channel_id=1, source_target_pairs={{0,16},{32,48},{64,80},{96,112},{16,0},{48,32},{80,64},{112,96},{1... | collective-permute-start | bytes 393224 | tf_op jit(solution)/shard_map/ppermute | solution.py:70
  27.6 4.0 %collective-permute-start.4 = (f32[256,128]{1,0:T(8,128)S(1)}, f32[256,128]{1,0:T(8,128)S(1)}, u32[]{:S(2)}, u32[]{:S(2)}) collective-permute-start(f32[256,128]{1,0:T(8,128)S(1)} %get-tuple-element.88), channel_id=1, source_target_pairs={{1,2},{3,4},{5,6},{7,8},{9,10},{11,12},{13,14},{2,1},{4,3},{6,5},{... | collective-permute-start | bytes 393224 | tf_op jit(solution)/shard_map/ppermute | solution.py:64
  36.8 8.6 %all_to_all.15 = f32[16,8,128]{2,1,0:T(8,128)S(1)} all-to-all(f32[16,8,128]{2,1,0:T(8,128)S(1)} %get-tuple-element.92), channel_id=1, replica_groups=mesh['gx'=4,'gy'=8,'gz'=16] {'gz'}, dimensions={0} | all-to-all | bytes 131072 | tf_op jit(solution)/shard_map/all_to_all | solution.py:507
  46.7 8.6 %all_gather.64 = f32[48,128]{1,0:T(8,128)S(1)} all-gather(f32[24,128]{1,0:T(8,128)S(1)} %get-tuple-element.98), channel_id=1, replica_groups={{0,16},{32,48},{64,80},{96,112},{1,113},{33,17},{65,49},{97,81},{2,18},..., dimensions={0}, use_global_device_ids=true | all-gather | bytes 36864 | tf_op jit(solution)/shard_map/all_gather | solution.py:401
  58.0 5.7 %all_gather.66 = f32[192,128]{1,0:T(8,128)S(1)} all-gather(f32[96,128]{1,0:T(8,128)S(1)} %all_gather.65), channel_id=1, replica_groups={{0,128},{256,384},{1,385},{257,129},{2,130},{258,386},{3,387},{259,131}..., dimensions={0}, use_global_device_ids=true | all-gather | bytes 147456 | tf_op jit(solution)/shard_map/all_gather | solution.py:401
  71.1 6.8 %all_gather.68.refs_1_.xa = f32[448,128]{1,0:T(8,128)S(1)} all-gather(f32[224,128]{1,0:T(8,128)S(1)} %get-tuple-element.100), channel_id=1, replica_groups={{0,128},{256,384},{1,129},{257,385},{2,130},{258,386},{3,131},{259,387}..., dimensions={0}, use_global_device_ids=true | all-gather | bytes 344064 | tf_op jit(solution)/shard_map/all_gather | solution.py:65
  80.8 8.5 %all_gather.69.refs_3_.ya = f32[448,128]{1,0:T(8,128)S(1)} all-gather(f32[224,128]{1,0:T(8,128)S(1)} %get-tuple-element.102), channel_id=1, replica_groups={{0,16},{32,48},{64,80},{96,112},{1,17},{33,49},{65,81},{97,113},{2,18},..., dimensions={0}, use_global_device_ids=true | all-gather | bytes 344064 | tf_op jit(solution)/shard_map/all_gather | solution.py:65
  89.9 3.8 %collective-permute-start.7 = (f32[224,128]{1,0:T(8,128)S(1)}, f32[224,128]{1,0:T(8,128)S(1)}, u32[]{:S(2)}, u32[]{:S(2)}) collective-permute-start(f32[224,128]{1,0:T(8,128)S(1)} %get-tuple-element.105), channel_id=1, source_target_pairs={{1,2},{3,4},{5,6},{7,8},{9,10},{11,12},{13,14},{2,1},{4,3},{6,5},{... | collective-permute-start | bytes 344072 | tf_op jit(solution)/shard_map/ppermute | solution.py:64
  98.9 8.4 %all_to_all.16 = f32[16,8,128]{2,1,0:T(8,128)S(1)} all-to-all(f32[16,8,128]{2,1,0:T(8,128)S(1)} %get-tuple-element.107), channel_id=1, replica_groups=mesh['gx'=4,'gy'=8,'gz'=16] {'gz'}, dimensions={0} | all-to-all | bytes 131072 | tf_op jit(solution)/shard_map/all_to_all | solution.py:507
  108.0 4.4 %all_gather.71 = f32[48,128]{1,0:T(8,128)S(1)} all-gather(f32[24,128]{1,0:T(8,128)S(1)} %solve.2), channel_id=1, replica_groups={{0,16},{32,48},{64,80},{96,112},{1,113},{33,17},{65,49},{97,81},{2,18},..., dimensions={0}, use_global_device_ids=true | all-gather | bytes 36864 | tf_op jit(solution)/shard_map/all_gather | solution.py:401
  114.3 5.8 %all_gather.73 = f32[192,128]{1,0:T(8,128)S(1)} all-gather(f32[96,128]{1,0:T(8,128)S(1)} %all_gather.72), channel_id=1, replica_groups={{0,128},{256,384},{1,385},{257,129},{2,130},{258,386},{3,387},{259,131}..., dimensions={0}, use_global_device_ids=true | all-gather | bytes 147456 | tf_op jit(solution)/shard_map/all_gather | solution.py:401
  123.5 5.9 %collective-permute-start.8 = (f32[224,128]{1,0:T(8,128)S(1)}, f32[224,128]{1,0:T(8,128)S(1)}, u32[]{:S(2)}, u32[]{:S(2)}) collective-permute-start(f32[224,128]{1,0:T(8,128)S(1)} %get-tuple-element.112), channel_id=1, source_target_pairs={{128,256},{256,128},{129,257},{257,129},{130,258},{258,130},{131,2... | collective-permute-start | bytes 344072 | tf_op jit(solution)/shard_map/ppermute | solution.py:64
  129.5 6.8 %all_gather.75.refs_1_.xa = f32[448,128]{1,0:T(8,128)S(1)} all-gather(f32[224,128]{1,0:T(8,128)S(1)} %get-tuple-element.111), channel_id=1, replica_groups={{0,128},{256,384},{1,129},{257,385},{2,130},{258,386},{3,131},{259,387}..., dimensions={0}, use_global_device_ids=true | all-gather | bytes 344064 | tf_op jit(solution)/shard_map/all_gather | solution.py:65
  137.5 9.8 %all_gather.76.refs_3_.ya = f32[448,128]{1,0:T(8,128)S(1)} all-gather(f32[224,128]{1,0:T(8,128)S(1)} %get-tuple-element.113), channel_id=1, replica_groups={{0,16},{32,48},{64,80},{96,112},{1,17},{33,49},{65,81},{97,113},{2,18},..., dimensions={0}, use_global_device_ids=true | all-gather | bytes 344064 | tf_op jit(solution)/shard_map/all_gather | solution.py:65
  147.8 5.6 %collective-permute-start.10 = (f32[224,128]{1,0:T(8,128)S(1)}, f32[224,128]{1,0:T(8,128)S(1)}, u32[]{:S(2)}, u32[]{:S(2)}) collective-permute-start(f32[224,128]{1,0:T(8,128)S(1)} %get-tuple-element.116), channel_id=1, source_target_pairs={{1,2},{3,4},{5,6},{7,8},{9,10},{11,12},{13,14},{2,1},{4,3},{6,5},{... | collective-permute-start | bytes 344072 | tf_op jit(solution)/shard_map/ppermute | solution.py:64
  156.8 10.2 %all_to_all.17 = f32[16,8,128]{2,1,0:T(8,128)S(1)} all-to-all(f32[16,8,128]{2,1,0:T(8,128)S(1)} %get-tuple-element.118), channel_id=1, replica_groups=mesh['gx'=4,'gy'=8,'gz'=16] {'gz'}, dimensions={0} | all-to-all | bytes 131072 | tf_op jit(solution)/shard_map/all_to_all | solution.py:507
  167.7 4.4 %all_gather.78 = f32[48,128]{1,0:T(8,128)S(1)} all-gather(f32[24,128]{1,0:T(8,128)S(1)} %solve.3), channel_id=1, replica_groups={{0,16},{32,48},{64,80},{96,112},{1,113},{33,17},{65,49},{97,81},{2,18},..., dimensions={0}, use_global_device_ids=true | all-gather | bytes 36864 | tf_op jit(solution)/shard_map/all_gather | solution.py:401
  173.9 6.1 %all_gather.80 = f32[192,128]{1,0:T(8,128)S(1)} all-gather(f32[96,128]{1,0:T(8,128)S(1)} %all_gather.79), channel_id=1, replica_groups={{0,128},{256,384},{1,385},{257,129},{2,130},{258,386},{3,387},{259,131}..., dimensions={0}, use_global_device_ids=true | all-gather | bytes 147456 | tf_op jit(solution)/shard_map/all_gather | solution.py:401
  192.0 5.6 %collective-permute-done.12.refs_2_.xb = f32[224,128]{1,0:T(8,128)S(1)} collective-permute-done((f32[224,128]{1,0:T(8,128)S(1)}, f32[224,128]{1,0:T(8,128)S(1)}, u32[]{:S(2)}, u32[]{:S(2)}) %collective-permute-start.12) | collective-permute-done | bytes 114720 | tf_op jit(solution)/shard_map/ppermute | solution.py:70
  198.9 7.2 %all_gather.82.refs_3_.ya = f32[448,128]{1,0:T(8,128)S(1)} all-gather(f32[224,128]{1,0:T(8,128)S(1)} %get-tuple-element.128), channel_id=1, replica_groups={{0,16},{32,48},{64,80},{96,112},{1,17},{33,49},{65,81},{97,113},{2,18},..., dimensions={0}, use_global_device_ids=true | all-gather | bytes 344064 | tf_op jit(solution)/shard_map/all_gather | solution.py:65
  210.8 4.1 %collective-permute-done.14.zb = f32[224,128]{1,0:T(8,128)S(1)} collective-permute-done((f32[224,128]{1,0:T(8,128)S(1)}, f32[224,128]{1,0:T(8,128)S(1)}, u32[]{:S(2)}, u32[]{:S(2)}) %collective-permute-start.14) | collective-permute-done | bytes 114720 | tf_op jit(solution)/shard_map/ppermute | solution.py:64
  (58 shorter events, 68.6 us)
Async XLA Ops:
  4.6 9.5 %collective-permute-start = (f32[256,128]{1,0:T(8,128)S(1)}, f32[256,128]{1,0:T(8,128)S(1)}, u32[]{:S(2)}, u32[]{:S(2)}) collective-permute-start(f32[256,128]{1,0:T(8,128)S(1)} %get-tuple-element.68), channel_id=1, source_target_pairs={{0,128},{256,384},{128,0},{384,256},{1,129},{257,385},{129,1},{385... | collective-permute-start | bytes 393224 | tf_op jit(solution)/shard_map/ppermute | solution.py:70
  7.3 11.8 %collective-permute-start.1 = (f32[256,128]{1,0:T(8,128)S(1)}, f32[256,128]{1,0:T(8,128)S(1)}, u32[]{:S(2)}, u32[]{:S(2)}) collective-permute-start(f32[256,128]{1,0:T(8,128)S(1)} %get-tuple-element.69), channel_id=1, source_target_pairs={{128,256},{256,128},{129,257},{257,129},{130,258},{258,130},{131,2... | collective-permute-start | bytes 393224 | tf_op jit(solution)/shard_map/ppermute | solution.py:70
  10.0 14.6 %copy-start = (bf16[1,1,1,1024,1024]{4,3,2,1,0:T(8,128)(2,1)S(1)}, bf16[1,1,1,1024,1024]{4,3,2,1,0:T(8,128)(2,1)}, u32[]{:S(2)}) copy-start(bf16[1,1,1,1024,1024]{4,3,2,1,0:T(8,128)(2,1)} %param.7) | copy-start | bytes 6291460
  19.7 7.4 %collective-permute-start.2 = (f32[256,128]{1,0:T(8,128)S(1)}, f32[256,128]{1,0:T(8,128)S(1)}, u32[]{:S(2)}, u32[]{:S(2)}) collective-permute-start(f32[256,128]{1,0:T(8,128)S(1)} %get-tuple-element.80), channel_id=1, source_target_pairs={{0,16},{32,48},{64,80},{96,112},{16,0},{48,32},{80,64},{112,96},{1... | collective-permute-start | bytes 393224 | tf_op jit(solution)/shard_map/ppermute | solution.py:70
  24.0 3.1 %collective-permute-start.3 = (f32[256,128]{1,0:T(8,128)S(1)}, f32[256,128]{1,0:T(8,128)S(1)}, u32[]{:S(2)}, u32[]{:S(2)}) collective-permute-start(f32[256,128]{1,0:T(8,128)S(1)} %get-tuple-element.81), channel_id=1, source_target_pairs={{16,32},{48,64},{80,96},{32,16},{64,48},{96,80},{17,33},{49,65},{8... | collective-permute-start | bytes 393224 | tf_op jit(solution)/shard_map/ppermute | solution.py:70
  27.0 38.7 %copy-start.1 = (s32[1024,4]{1,0:T(8,128)S(1)}, s32[1024,4]{1,0:T(8,128)}, u32[]{:S(2)}) copy-start(s32[1024,4]{1,0:T(8,128)} %constant.37.clone.block) | copy-start | bytes 49156
  27.6 8.4 %collective-permute-start.4 = (f32[256,128]{1,0:T(8,128)S(1)}, f32[256,128]{1,0:T(8,128)S(1)}, u32[]{:S(2)}, u32[]{:S(2)}) collective-permute-start(f32[256,128]{1,0:T(8,128)S(1)} %get-tuple-element.88), channel_id=1, source_target_pairs={{1,2},{3,4},{5,6},{7,8},{9,10},{11,12},{13,14},{2,1},{4,3},{6,5},{... | collective-permute-start | bytes 393224 | tf_op jit(solution)/shard_map/ppermute | solution.py:64
  68.5 11.1 %collective-permute-start.5 = (f32[224,128]{1,0:T(8,128)S(1)}, f32[224,128]{1,0:T(8,128)S(1)}, u32[]{:S(2)}, u32[]{:S(2)}) collective-permute-start(f32[224,128]{1,0:T(8,128)S(1)} %get-tuple-element.101), channel_id=1, source_target_pairs={{128,256},{256,128},{129,257},{257,129},{130,258},{258,130},{131,2... | collective-permute-start | bytes 344072 | tf_op jit(solution)/shard_map/ppermute | solution.py:64
  80.1 9.2 %collective-permute-start.6 = (f32[224,128]{1,0:T(8,128)S(1)}, f32[224,128]{1,0:T(8,128)S(1)}, u32[]{:S(2)}, u32[]{:S(2)}) collective-permute-start(f32[224,128]{1,0:T(8,128)S(1)} %get-tuple-element.103), channel_id=1, source_target_pairs={{16,32},{48,64},{80,96},{32,16},{64,48},{96,80},{17,33},{49,65},{8... | collective-permute-start | bytes 344072 | tf_op jit(solution)/shard_map/ppermute | solution.py:64
  89.9 8.2 %collective-permute-start.7 = (f32[224,128]{1,0:T(8,128)S(1)}, f32[224,128]{1,0:T(8,128)S(1)}, u32[]{:S(2)}, u32[]{:S(2)}) collective-permute-start(f32[224,128]{1,0:T(8,128)S(1)} %get-tuple-element.105), channel_id=1, source_target_pairs={{1,2},{3,4},{5,6},{7,8},{9,10},{11,12},{13,14},{2,1},{4,3},{6,5},{... | collective-permute-start | bytes 344072 | tf_op jit(solution)/shard_map/ppermute | solution.py:64
  123.5 12.7 %collective-permute-start.8 = (f32[224,128]{1,0:T(8,128)S(1)}, f32[224,128]{1,0:T(8,128)S(1)}, u32[]{:S(2)}, u32[]{:S(2)}) collective-permute-start(f32[224,128]{1,0:T(8,128)S(1)} %get-tuple-element.112), channel_id=1, source_target_pairs={{128,256},{256,128},{129,257},{257,129},{130,258},{258,130},{131,2... | collective-permute-start | bytes 344072 | tf_op jit(solution)/shard_map/ppermute | solution.py:64
  136.8 10.4 %collective-permute-start.9 = (f32[224,128]{1,0:T(8,128)S(1)}, f32[224,128]{1,0:T(8,128)S(1)}, u32[]{:S(2)}, u32[]{:S(2)}) collective-permute-start(f32[224,128]{1,0:T(8,128)S(1)} %get-tuple-element.114), channel_id=1, source_target_pairs={{16,32},{48,64},{80,96},{32,16},{64,48},{96,80},{17,33},{49,65},{8... | collective-permute-start | bytes 344072 | tf_op jit(solution)/shard_map/ppermute | solution.py:64
  147.8 8.2 %collective-permute-start.10 = (f32[224,128]{1,0:T(8,128)S(1)}, f32[224,128]{1,0:T(8,128)S(1)}, u32[]{:S(2)}, u32[]{:S(2)}) collective-permute-start(f32[224,128]{1,0:T(8,128)S(1)} %get-tuple-element.116), channel_id=1, source_target_pairs={{1,2},{3,4},{5,6},{7,8},{9,10},{11,12},{13,14},{2,1},{4,3},{6,5},{... | collective-permute-start | bytes 344072 | tf_op jit(solution)/shard_map/ppermute | solution.py:64
  183.9 8.1 %collective-permute-start.11 = (f32[224,128]{1,0:T(8,128)S(1)}, f32[224,128]{1,0:T(8,128)S(1)}, u32[]{:S(2)}, u32[]{:S(2)}) collective-permute-start(f32[224,128]{1,0:T(8,128)S(1)} %get-tuple-element.121), channel_id=1, source_target_pairs={{0,128},{256,384},{128,0},{384,256},{1,129},{257,385},{129,1},{385... | collective-permute-start | bytes 344072 | tf_op jit(solution)/shard_map/ppermute | solution.py:70
  186.0 11.6 %collective-permute-start.12 = (f32[224,128]{1,0:T(8,128)S(1)}, f32[224,128]{1,0:T(8,128)S(1)}, u32[]{:S(2)}, u32[]{:S(2)}) collective-permute-start(f32[224,128]{1,0:T(8,128)S(1)} %get-tuple-element.122), channel_id=1, source_target_pairs={{128,256},{256,128},{129,257},{257,129},{130,258},{258,130},{131,2... | collective-permute-start | bytes 344072 | tf_op jit(solution)/shard_map/ppermute | solution.py:70
  198.2 7.9 %collective-permute-start.13 = (f32[224,128]{1,0:T(8,128)S(1)}, f32[224,128]{1,0:T(8,128)S(1)}, u32[]{:S(2)}, u32[]{:S(2)}) collective-permute-start(f32[224,128]{1,0:T(8,128)S(1)} %get-tuple-element.129), channel_id=1, source_target_pairs={{16,32},{48,64},{80,96},{32,16},{64,48},{96,80},{17,33},{49,65},{8... | collective-permute-start | bytes 344072 | tf_op jit(solution)/shard_map/ppermute | solution.py:64
  206.7 8.2 %collective-permute-start.14 = (f32[224,128]{1,0:T(8,128)S(1)}, f32[224,128]{1,0:T(8,128)S(1)}, u32[]{:S(2)}, u32[]{:S(2)}) collective-permute-start(f32[224,128]{1,0:T(8,128)S(1)} %get-tuple-element.131), channel_id=1, source_target_pairs={{1,2},{3,4},{5,6},{7,8},{9,10},{11,12},{13,14},{2,1},{4,3},{6,5},{... | collective-permute-start | bytes 344072 | tf_op jit(solution)/shard_map/ppermute | solution.py:64

commit v6 on v5

--- a/solution.py
+++ b/solution.py
@@ -396,8 +396,14 @@
     groups = []
     for z in range(line):
         for even in range(0, size, 2):
-            odd = (even + 1 if z % 2 == 0 else even - 1) % size
-            groups.append([even * line + z, odd * line + z])
+            odd = even + 1 if z % 2 == 0 else even - 1
+            if odd >= 0:
+                groups.append([even * line + z, odd * line + z])
+            elif line % 4:
+                groups.append([z, (size - 1) * line + z])
+            elif z % 4 == 1:
+                for end in (0, size - 1):
+                    groups.append([end * line + z, end * line + z + 2])
     block = lax.all_gather(block, (axis, "gz"), axis_index_groups=groups, tiled=True)
     return lax.all_gather(block, "gz", axis_index_groups=[[z, z + 1] for z in range(0, line, 2)], tiled=True)
 

time: 218 us -> 217 us (level)
  no operation moved by 1% of the time
where the time goes in v6:
time: 217 us
  blocking collectives  122 us (56%)
  starting transfers between devices  40.6 us (19%)
  Pallas kernels  29.5 us (14%)
  waiting for transfers between devices  23.1 us (11%)
    all_gather x9, blocking collectives, exchange(): lax.all_gather(first, axis, axis_index_groups=groups, tiled=True)  48.7 us
    all_gather x6, blocking collectives, share(): lax.all_gather(block, (axis, 'gz'), axis_index_groups=groups, tiled=True)  34.6 us
    all_to_all x3, blocking collectives, local(): lax.all_to_all(proj, 'gz', 0, 0, tiled=True).reshape(8 * line_length, 128)  27 us
    ppermute x9, starting transfers between devices, exchange(): other = lax.ppermute(second, axis, swaps(size, 1))  25.6 us
    pallas_call x20, Pallas kernels, call(): pl.pallas_call(kernel, out_shape=[jax.ShapeDtypeStruct(s, t) for s, t in...  19.8 us
    all_gather x6, blocking collectives, share(): lax.all_gather(block, 'gz', axis_index_groups=[[z, z + 1] for z in range(...  11.5 us
    ppermute x9, waiting for transfers between devices, exchange(): other = lax.ppermute(second, axis, swaps(size, 1))  11.2 us
    ppermute x3, waiting for transfers between devices, exchange_async(): lax.ppermute(second, axis, swaps(size, 1))  10.6 us
  transfers between devices with their start and end apart: 15, of which 8 were waited for; matrix products, arithmetic and copies ran while one was open for 0% of the time, Pallas kernels for 4%

profile of v6, /device:TPU:40, one launch (start us, length us, event | category | flops | bytes accessed | tf_op | source)
XLA Modules:
  0.0 216.6 jit_solution(14931623667081726361)
XLA Ops:
  1.4 3.2 %pack.1 = (bf16[1024,1024]{1,0:T(8,128)(2,1)S(1)}, f32[1024,128]{1,0:T(8,128)S(1)}, f32[128,128]{1,0:T(8,128)S(1)}, bf16[16,1024]{1,0:T(8,128)(2,1)S(1)}, bf16[1...) custom-call(s32[5]{0:T(128)S(1)} %stack.19.sc, ...), custom_call_target="tpu_custom_call" | custom-call | tf_op jit(solution)/shard_map/pack/pallas_call | solution.py:448
  10.0 4.1 %permute.1 = (bf16[512,1024]{1,0:T(8,128)(2,1)S(1)}, bf16[1024,1024]{1,0:T(8,128)(2,1)S(1)}, bf16[16,1024]{1,0:T(8,128)(2,1)S(1)}) custom-call(bf16[1024,1024]{1,0:T(8,128)(2,1)S(1)} %get-tuple-element.70.sel, bf16[16,1024]{1,0:T(8,128)(2,1)S(1)} %get-tuple-element.71.mode, s32[8,128]{1,0:T(8,128)S(1)} %get-tuple-element.72.order, bf16[1024,1024]{1,0:T(8,128)(2,1)} %bitcast.18), custom_call_target="tpu_custom_call" | custom-call | tf_op jit(solution)/shard_map/permute/pallas_call | solution.py:475
  14.2 4.9 %collective-permute-done.1.refs_3_.xb = f32[256,128]{1,0:T(8,128)S(1)} collective-permute-done((f32[256,128]{1,0:T(8,128)S(1)}, f32[256,128]{1,0:T(8,128)S(1)}, u32[]{:S(2)}, u32[]{:S(2)}) %collective-permute-start.1) | collective-permute-done | bytes 131104 | tf_op jit(solution)/shard_map/ppermute | solution.py:70
  19.7 4.3 %collective-permute-start.2 = (f32[256,128]{1,0:T(8,128)S(1)}, f32[256,128]{1,0:T(8,128)S(1)}, u32[]{:S(2)}, u32[]{:S(2)}) collective-permute-start(f32[256,128]{1,0:T(8,128)S(1)} %get-tuple-element.80), channel_id=1, source_target_pairs={{0,16},{32,48},{64,80},{96,112},{16,0},{48,32},{80,64},{112,96},{1... | collective-permute-start | bytes 393224 | tf_op jit(solution)/shard_map/ppermute | solution.py:70
  27.6 4.0 %collective-permute-start.4 = (f32[256,128]{1,0:T(8,128)S(1)}, f32[256,128]{1,0:T(8,128)S(1)}, u32[]{:S(2)}, u32[]{:S(2)}) collective-permute-start(f32[256,128]{1,0:T(8,128)S(1)} %get-tuple-element.88), channel_id=1, source_target_pairs={{1,2},{3,4},{5,6},{7,8},{9,10},{11,12},{13,14},{2,1},{4,3},{6,5},{... | collective-permute-start | bytes 393224 | tf_op jit(solution)/shard_map/ppermute | solution.py:64
  36.8 8.6 %all_to_all.15 = f32[16,8,128]{2,1,0:T(8,128)S(1)} all-to-all(f32[16,8,128]{2,1,0:T(8,128)S(1)} %get-tuple-element.92), channel_id=1, replica_groups=mesh['gx'=4,'gy'=8,'gz'=16] {'gz'}, dimensions={0} | all-to-all | bytes 131072 | tf_op jit(solution)/shard_map/all_to_all | solution.py:513
  46.7 8.6 %all_gather.64 = f32[48,128]{1,0:T(8,128)S(1)} all-gather(f32[24,128]{1,0:T(8,128)S(1)} %get-tuple-element.98), channel_id=1, replica_groups={{0,16},{32,48},{64,80},{96,112},{1,3},{113,115},{33,17},{65,49},{97,81}..., dimensions={0}, use_global_device_ids=true | all-gather | bytes 36864 | tf_op jit(solution)/shard_map/all_gather | solution.py:407
  57.1 5.7 %all_gather.66 = f32[192,128]{1,0:T(8,128)S(1)} all-gather(f32[96,128]{1,0:T(8,128)S(1)} %all_gather.65), channel_id=1, replica_groups={{0,128},{256,384},{1,3},{385,387},{257,129},{2,130},{258,386},{259,131}..., dimensions={0}, use_global_device_ids=true | all-gather | bytes 147456 | tf_op jit(solution)/shard_map/all_gather | solution.py:407
  70.0 6.8 %all_gather.68.refs_1_.xa = f32[448,128]{1,0:T(8,128)S(1)} all-gather(f32[224,128]{1,0:T(8,128)S(1)} %get-tuple-element.100), channel_id=1, replica_groups={{0,128},{256,384},{1,129},{257,385},{2,130},{258,386},{3,131},{259,387}..., dimensions={0}, use_global_device_ids=true | all-gather | bytes 344064 | tf_op jit(solution)/shard_map/all_gather | solution.py:65
  79.6 9.7 %all_gather.69.refs_3_.ya = f32[448,128]{1,0:T(8,128)S(1)} all-gather(f32[224,128]{1,0:T(8,128)S(1)} %get-tuple-element.102), channel_id=1, replica_groups={{0,16},{32,48},{64,80},{96,112},{1,17},{33,49},{65,81},{97,113},{2,18},..., dimensions={0}, use_global_device_ids=true | all-gather | bytes 344064 | tf_op jit(solution)/shard_map/all_gather | solution.py:65
  89.9 3.8 %collective-permute-start.7 = (f32[224,128]{1,0:T(8,128)S(1)}, f32[224,128]{1,0:T(8,128)S(1)}, u32[]{:S(2)}, u32[]{:S(2)}) collective-permute-start(f32[224,128]{1,0:T(8,128)S(1)} %get-tuple-element.105), channel_id=1, source_target_pairs={{1,2},{3,4},{5,6},{7,8},{9,10},{11,12},{13,14},{2,1},{4,3},{6,5},{... | collective-permute-start | bytes 344072 | tf_op jit(solution)/shard_map/ppermute | solution.py:64
  98.9 8.4 %all_to_all.16 = f32[16,8,128]{2,1,0:T(8,128)S(1)} all-to-all(f32[16,8,128]{2,1,0:T(8,128)S(1)} %get-tuple-element.107), channel_id=1, replica_groups=mesh['gx'=4,'gy'=8,'gz'=16] {'gz'}, dimensions={0} | all-to-all | bytes 131072 | tf_op jit(solution)/shard_map/all_to_all | solution.py:513
  108.0 4.4 %all_gather.71 = f32[48,128]{1,0:T(8,128)S(1)} all-gather(f32[24,128]{1,0:T(8,128)S(1)} %solve.2), channel_id=1, replica_groups={{0,16},{32,48},{64,80},{96,112},{1,3},{113,115},{33,17},{65,49},{97,81}..., dimensions={0}, use_global_device_ids=true | all-gather | bytes 36864 | tf_op jit(solution)/shard_map/all_gather | solution.py:407
  114.2 5.7 %all_gather.73 = f32[192,128]{1,0:T(8,128)S(1)} all-gather(f32[96,128]{1,0:T(8,128)S(1)} %all_gather.72), channel_id=1, replica_groups={{0,128},{256,384},{1,3},{385,387},{257,129},{2,130},{258,386},{259,131}..., dimensions={0}, use_global_device_ids=true | all-gather | bytes 147456 | tf_op jit(solution)/shard_map/all_gather | solution.py:407
  123.4 6.0 %collective-permute-start.8 = (f32[224,128]{1,0:T(8,128)S(1)}, f32[224,128]{1,0:T(8,128)S(1)}, u32[]{:S(2)}, u32[]{:S(2)}) collective-permute-start(f32[224,128]{1,0:T(8,128)S(1)} %get-tuple-element.112), channel_id=1, source_target_pairs={{128,256},{256,128},{129,257},{257,129},{130,258},{258,130},{131,2... | collective-permute-start | bytes 344072 | tf_op jit(solution)/shard_map/ppermute | solution.py:64
  129.4 6.8 %all_gather.75.refs_1_.xa = f32[448,128]{1,0:T(8,128)S(1)} all-gather(f32[224,128]{1,0:T(8,128)S(1)} %get-tuple-element.111), channel_id=1, replica_groups={{0,128},{256,384},{1,129},{257,385},{2,130},{258,386},{3,131},{259,387}..., dimensions={0}, use_global_device_ids=true | all-gather | bytes 344064 | tf_op jit(solution)/shard_map/all_gather | solution.py:65
  137.4 9.9 %all_gather.76.refs_3_.ya = f32[448,128]{1,0:T(8,128)S(1)} all-gather(f32[224,128]{1,0:T(8,128)S(1)} %get-tuple-element.113), channel_id=1, replica_groups={{0,16},{32,48},{64,80},{96,112},{1,17},{33,49},{65,81},{97,113},{2,18},..., dimensions={0}, use_global_device_ids=true | all-gather | bytes 344064 | tf_op jit(solution)/shard_map/all_gather | solution.py:65
  148.0 5.5 %collective-permute-start.10 = (f32[224,128]{1,0:T(8,128)S(1)}, f32[224,128]{1,0:T(8,128)S(1)}, u32[]{:S(2)}, u32[]{:S(2)}) collective-permute-start(f32[224,128]{1,0:T(8,128)S(1)} %get-tuple-element.116), channel_id=1, source_target_pairs={{1,2},{3,4},{5,6},{7,8},{9,10},{11,12},{13,14},{2,1},{4,3},{6,5},{... | collective-permute-start | bytes 344072 | tf_op jit(solution)/shard_map/ppermute | solution.py:64
  157.0 10.1 %all_to_all.17 = f32[16,8,128]{2,1,0:T(8,128)S(1)} all-to-all(f32[16,8,128]{2,1,0:T(8,128)S(1)} %get-tuple-element.118), channel_id=1, replica_groups=mesh['gx'=4,'gy'=8,'gz'=16] {'gz'}, dimensions={0} | all-to-all | bytes 131072 | tf_op jit(solution)/shard_map/all_to_all | solution.py:513
  167.7 4.4 %all_gather.78 = f32[48,128]{1,0:T(8,128)S(1)} all-gather(f32[24,128]{1,0:T(8,128)S(1)} %solve.3), channel_id=1, replica_groups={{0,16},{32,48},{64,80},{96,112},{1,3},{113,115},{33,17},{65,49},{97,81}..., dimensions={0}, use_global_device_ids=true | all-gather | bytes 36864 | tf_op jit(solution)/shard_map/all_gather | solution.py:407
  173.9 5.7 %all_gather.80 = f32[192,128]{1,0:T(8,128)S(1)} all-gather(f32[96,128]{1,0:T(8,128)S(1)} %all_gather.79), channel_id=1, replica_groups={{0,128},{256,384},{1,3},{385,387},{257,129},{2,130},{258,386},{259,131}..., dimensions={0}, use_global_device_ids=true | all-gather | bytes 147456 | tf_op jit(solution)/shard_map/all_gather | solution.py:407
  191.7 5.6 %collective-permute-done.12.refs_2_.xb = f32[224,128]{1,0:T(8,128)S(1)} collective-permute-done((f32[224,128]{1,0:T(8,128)S(1)}, f32[224,128]{1,0:T(8,128)S(1)}, u32[]{:S(2)}, u32[]{:S(2)}) %collective-permute-start.12) | collective-permute-done | bytes 114720 | tf_op jit(solution)/shard_map/ppermute | solution.py:70
  198.5 7.2 %all_gather.82.refs_3_.ya = f32[448,128]{1,0:T(8,128)S(1)} all-gather(f32[224,128]{1,0:T(8,128)S(1)} %get-tuple-element.128), channel_id=1, replica_groups={{0,16},{32,48},{64,80},{96,112},{1,17},{33,49},{65,81},{97,113},{2,18},..., dimensions={0}, use_global_device_ids=true | all-gather | bytes 344064 | tf_op jit(solution)/shard_map/all_gather | solution.py:65
  210.5 4.0 %collective-permute-done.14.zb = f32[224,128]{1,0:T(8,128)S(1)} collective-permute-done((f32[224,128]{1,0:T(8,128)S(1)}, f32[224,128]{1,0:T(8,128)S(1)}, u32[]{:S(2)}, u32[]{:S(2)}) %collective-permute-start.14) | collective-permute-done | bytes 114720 | tf_op jit(solution)/shard_map/ppermute | solution.py:64
  (58 shorter events, 67.6 us)
Async XLA Ops:
  4.6 9.5 %collective-permute-start = (f32[256,128]{1,0:T(8,128)S(1)}, f32[256,128]{1,0:T(8,128)S(1)}, u32[]{:S(2)}, u32[]{:S(2)}) collective-permute-start(f32[256,128]{1,0:T(8,128)S(1)} %get-tuple-element.68), channel_id=1, source_target_pairs={{0,128},{256,384},{128,0},{384,256},{1,129},{257,385},{129,1},{385... | collective-permute-start | bytes 393224 | tf_op jit(solution)/shard_map/ppermute | solution.py:70
  7.3 11.8 %collective-permute-start.1 = (f32[256,128]{1,0:T(8,128)S(1)}, f32[256,128]{1,0:T(8,128)S(1)}, u32[]{:S(2)}, u32[]{:S(2)}) collective-permute-start(f32[256,128]{1,0:T(8,128)S(1)} %get-tuple-element.69), channel_id=1, source_target_pairs={{128,256},{256,128},{129,257},{257,129},{130,258},{258,130},{131,2... | collective-permute-start | bytes 393224 | tf_op jit(solution)/shard_map/ppermute | solution.py:70
  10.0 14.6 %copy-start = (bf16[1,1,1,1024,1024]{4,3,2,1,0:T(8,128)(2,1)S(1)}, bf16[1,1,1,1024,1024]{4,3,2,1,0:T(8,128)(2,1)}, u32[]{:S(2)}) copy-start(bf16[1,1,1,1024,1024]{4,3,2,1,0:T(8,128)(2,1)} %param.7) | copy-start | bytes 6291460
  19.7 7.4 %collective-permute-start.2 = (f32[256,128]{1,0:T(8,128)S(1)}, f32[256,128]{1,0:T(8,128)S(1)}, u32[]{:S(2)}, u32[]{:S(2)}) collective-permute-start(f32[256,128]{1,0:T(8,128)S(1)} %get-tuple-element.80), channel_id=1, source_target_pairs={{0,16},{32,48},{64,80},{96,112},{16,0},{48,32},{80,64},{112,96},{1... | collective-permute-start | bytes 393224 | tf_op jit(solution)/shard_map/ppermute | solution.py:70
  24.0 3.1 %collective-permute-start.3 = (f32[256,128]{1,0:T(8,128)S(1)}, f32[256,128]{1,0:T(8,128)S(1)}, u32[]{:S(2)}, u32[]{:S(2)}) collective-permute-start(f32[256,128]{1,0:T(8,128)S(1)} %get-tuple-element.81), channel_id=1, source_target_pairs={{16,32},{48,64},{80,96},{32,16},{64,48},{96,80},{17,33},{49,65},{8... | collective-permute-start | bytes 393224 | tf_op jit(solution)/shard_map/ppermute | solution.py:70
  27.0 37.8 %copy-start.1 = (s32[1024,4]{1,0:T(8,128)S(1)}, s32[1024,4]{1,0:T(8,128)}, u32[]{:S(2)}) copy-start(s32[1024,4]{1,0:T(8,128)} %constant.37.clone.block) | copy-start | bytes 49156
  27.6 8.4 %collective-permute-start.4 = (f32[256,128]{1,0:T(8,128)S(1)}, f32[256,128]{1,0:T(8,128)S(1)}, u32[]{:S(2)}, u32[]{:S(2)}) collective-permute-start(f32[256,128]{1,0:T(8,128)S(1)} %get-tuple-element.88), channel_id=1, source_target_pairs={{1,2},{3,4},{5,6},{7,8},{9,10},{11,12},{13,14},{2,1},{4,3},{6,5},{... | collective-permute-start | bytes 393224 | tf_op jit(solution)/shard_map/ppermute | solution.py:64
  67.6 10.7 %collective-permute-start.5 = (f32[224,128]{1,0:T(8,128)S(1)}, f32[224,128]{1,0:T(8,128)S(1)}, u32[]{:S(2)}, u32[]{:S(2)}) collective-permute-start(f32[224,128]{1,0:T(8,128)S(1)} %get-tuple-element.101), channel_id=1, source_target_pairs={{128,256},{256,128},{129,257},{257,129},{130,258},{258,130},{131,2... | collective-permute-start | bytes 344072 | tf_op jit(solution)/shard_map/ppermute | solution.py:64
  78.9 10.4 %collective-permute-start.6 = (f32[224,128]{1,0:T(8,128)S(1)}, f32[224,128]{1,0:T(8,128)S(1)}, u32[]{:S(2)}, u32[]{:S(2)}) collective-permute-start(f32[224,128]{1,0:T(8,128)S(1)} %get-tuple-element.103), channel_id=1, source_target_pairs={{16,32},{48,64},{80,96},{32,16},{64,48},{96,80},{17,33},{49,65},{8... | collective-permute-start | bytes 344072 | tf_op jit(solution)/shard_map/ppermute | solution.py:64
  89.9 8.2 %collective-permute-start.7 = (f32[224,128]{1,0:T(8,128)S(1)}, f32[224,128]{1,0:T(8,128)S(1)}, u32[]{:S(2)}, u32[]{:S(2)}) collective-permute-start(f32[224,128]{1,0:T(8,128)S(1)} %get-tuple-element.105), channel_id=1, source_target_pairs={{1,2},{3,4},{5,6},{7,8},{9,10},{11,12},{13,14},{2,1},{4,3},{6,5},{... | collective-permute-start | bytes 344072 | tf_op jit(solution)/shard_map/ppermute | solution.py:64
  123.4 12.8 %collective-permute-start.8 = (f32[224,128]{1,0:T(8,128)S(1)}, f32[224,128]{1,0:T(8,128)S(1)}, u32[]{:S(2)}, u32[]{:S(2)}) collective-permute-start(f32[224,128]{1,0:T(8,128)S(1)} %get-tuple-element.112), channel_id=1, source_target_pairs={{128,256},{256,128},{129,257},{257,129},{130,258},{258,130},{131,2... | collective-permute-start | bytes 344072 | tf_op jit(solution)/shard_map/ppermute | solution.py:64
  136.8 10.6 %collective-permute-start.9 = (f32[224,128]{1,0:T(8,128)S(1)}, f32[224,128]{1,0:T(8,128)S(1)}, u32[]{:S(2)}, u32[]{:S(2)}) collective-permute-start(f32[224,128]{1,0:T(8,128)S(1)} %get-tuple-element.114), channel_id=1, source_target_pairs={{16,32},{48,64},{80,96},{32,16},{64,48},{96,80},{17,33},{49,65},{8... | collective-permute-start | bytes 344072 | tf_op jit(solution)/shard_map/ppermute | solution.py:64
  148.0 8.2 %collective-permute-start.10 = (f32[224,128]{1,0:T(8,128)S(1)}, f32[224,128]{1,0:T(8,128)S(1)}, u32[]{:S(2)}, u32[]{:S(2)}) collective-permute-start(f32[224,128]{1,0:T(8,128)S(1)} %get-tuple-element.116), channel_id=1, source_target_pairs={{1,2},{3,4},{5,6},{7,8},{9,10},{11,12},{13,14},{2,1},{4,3},{6,5},{... | collective-permute-start | bytes 344072 | tf_op jit(solution)/shard_map/ppermute | solution.py:64
  183.6 8.1 %collective-permute-start.11 = (f32[224,128]{1,0:T(8,128)S(1)}, f32[224,128]{1,0:T(8,128)S(1)}, u32[]{:S(2)}, u32[]{:S(2)}) collective-permute-start(f32[224,128]{1,0:T(8,128)S(1)} %get-tuple-element.121), channel_id=1, source_target_pairs={{0,128},{256,384},{128,0},{384,256},{1,129},{257,385},{129,1},{385... | collective-permute-start | bytes 344072 | tf_op jit(solution)/shard_map/ppermute | solution.py:70
  185.9 11.4 %collective-permute-start.12 = (f32[224,128]{1,0:T(8,128)S(1)}, f32[224,128]{1,0:T(8,128)S(1)}, u32[]{:S(2)}, u32[]{:S(2)}) collective-permute-start(f32[224,128]{1,0:T(8,128)S(1)} %get-tuple-element.122), channel_id=1, source_target_pairs={{128,256},{256,128},{129,257},{257,129},{130,258},{258,130},{131,2... | collective-permute-start | bytes 344072 | tf_op jit(solution)/shard_map/ppermute | solution.py:70
  197.9 7.9 %collective-permute-start.13 = (f32[224,128]{1,0:T(8,128)S(1)}, f32[224,128]{1,0:T(8,128)S(1)}, u32[]{:S(2)}, u32[]{:S(2)}) collective-permute-start(f32[224,128]{1,0:T(8,128)S(1)} %get-tuple-element.129), channel_id=1, source_target_pairs={{16,32},{48,64},{80,96},{32,16},{64,48},{96,80},{17,33},{49,65},{8... | collective-permute-start | bytes 344072 | tf_op jit(solution)/shard_map/ppermute | solution.py:64
  206.3 8.2 %collective-permute-start.14 = (f32[224,128]{1,0:T(8,128)S(1)}, f32[224,128]{1,0:T(8,128)S(1)}, u32[]{:S(2)}, u32[]{:S(2)}) collective-permute-start(f32[224,128]{1,0:T(8,128)S(1)} %get-tuple-element.131), channel_id=1, source_target_pairs={{1,2},{3,4},{5,6},{7,8},{9,10},{11,12},{13,14},{2,1},{4,3},{6,5},{... | collective-permute-start | bytes 344072 | tf_op jit(solution)/shard_map/ppermute | solution.py:64
